TPU v7x, 32 devices: a whole 2x2x4 slice. The times are simulated.
32 devices in a mesh: dp: 4 (over y, x), row: 4 (over z), col: 2 (over core).
Axes of the slice: x: 2, y: 2, z: 4, core: 2. Of those that a mesh axis runs over, the one named last changes fastest.
Arguments:
- hidden_in: bfloat16 [8192, 1024], P(('dp', 'col'), 'row'), may hold values from -6 to 6
- segment_ids: int32 [16, 512], P(('dp', 'row')), may hold values from 0 to 16, as said below
- query_weight: bfloat16 [1024, 1024], P('row', 'col'), may hold values from -0.1875 to 0.1875
- query_bias: bfloat16 [1024], P('col'), may hold values from -3 to 3
- key_weight: bfloat16 [1024, 1024], P('row', 'col'), may hold values from -0.1875 to 0.1875
- value_weight: bfloat16 [1024, 1024], P('row', 'col'), may hold values from -0.1875 to 0.1875
- value_bias: bfloat16 [1024], P('col'), may hold values from -3 to 3
- attn_out_weight: bfloat16 [1024, 1024], P('col', 'row'), may hold values from -0.75 to 0.75
- attn_out_bias: bfloat16 [1024], P('row'), may hold values from -3 to 3
- norm1_gain: bfloat16 [1024], P('row'), may hold values from 0.099609375 to 1.8984375
- first_norm_offset: bfloat16 [1024], P('row'), may hold values from -3 to 3
- inner_weight: bfloat16 [1024, 4096], P('row', 'col'), may hold values from -0.1875 to 0.1875
- inner_bias: bfloat16 [4096], P('col'), may hold values from -3 to 3
- outer_weight: bfloat16 [4096, 1024], P('col', 'row'), may hold values from -0.1875 to 0.1875
- outer_bias: bfloat16 [1024], P('row'), may hold values from -3 to 3
- norm2_gain: bfloat16 [1024], P('row'), may hold values from 0.099609375 to 1.8984375
- second_norm_offset: bfloat16 [1024], P('row'), may hold values from -3 to 3
- cotangent: bfloat16 [8192, 1024], P(('dp', 'col'), 'row'), may hold values from -6 to 6
Outputs:
- layer_out: bfloat16 [8192, 1024], P(('dp', 'col'), 'row')
- input_grad: bfloat16 [8192, 1024], P(('dp', 'col'), 'row')
- query_weight_grad: float32 [1024, 1024], P('row', 'col')
- query_bias_grad: float32 [1024], P('col')
- key_weight_grad: float32 [1024, 1024], P('row', 'col')
- value_weight_grad: float32 [1024, 1024], P('row', 'col')
- value_bias_grad: float32 [1024], P('col')
- attn_out_weight_grad: float32 [1024, 1024], P('col', 'row')
- attn_out_bias_grad: float32 [1024], P('row')
- norm1_gain_grad: float32 [1024], P('row')
- norm1_shift_grad: float32 [1024], P('row')
- inner_weight_grad: float32 [1024, 4096], P('row', 'col')
- inner_bias_grad: float32 [4096], P('col')
- outer_weight_grad: float32 [4096, 1024], P('col', 'row')
- outer_bias_grad: float32 [1024], P('row')
- norm2_gain_grad: float32 [1024], P('row')
- norm2_shift_grad: float32 [1024], P('row')
Inputs may be any that keep to these rules, and one draw needn't show every extreme that they name: `segment_ids`: within each sequence the ids start at 0 and rise by one at each document boundary; every document but the last of a sequence has 20 to 200 tokens, the last 1 to 200; in each sequence the first or the second document has exactly 200 tokens (others may have 200 too).
All inputs are finite; a program needn't handle non-finite values.
Results may differ from a plain program's by a relative error of at most 0.015.
Values may be sent and summed in bfloat16 or wider, within the bound.
A program may use at most 192 MiB of HBM per device.

v0:
```python
import jax
import jax.numpy as jnp
from jax import lax
from jax.sharding import PartitionSpec as P

MODEL_WIDTH = 1024
HD = 64
SEQ = 512


norm_eps = 1e-12
inv_root_two = 0.7071067811865476
inv_root_two_pi = 0.3989422804014327


def product(left, right):
    return jnp.dot(left, right, preferred_element_type=jnp.float32)


def over_tokens(left, right):
    return lax.dot_general(
        left, right, (((0,), (0,)), ((), ())), preferred_element_type=jnp.float32
    )


def against(left, right):
    return lax.dot_general(
        left, right, (((1,), (1,)), ((), ())), preferred_element_type=jnp.float32
    )


def col_gather(values):
    return lax.all_gather(values, "col", axis=0, tiled=True)


def row_gather(values):
    return lax.all_gather(values, "row", axis=0, tiled=True)


def row_reduce(values):
    return lax.psum_scatter(values, "row", scatter_dimension=0, tiled=True)


def col_reduce(values):
    return lax.psum_scatter(values, "col", scatter_dimension=0, tiled=True)


def row_sum_values(first_branch, second_branch):
    return lax.psum((first_branch, second_branch), "row")


def apply_norm(preact_input, norm_gain, norm_offset):
    total, squares = row_sum_values(
        jnp.sum(preact_input, 1), jnp.sum(preact_input * preact_input, 1)
    )
    row_mean = total / MODEL_WIDTH
    inverse_deviation = lax.rsqrt(squares / MODEL_WIDTH - row_mean * row_mean + norm_eps)
    centred_rows = (preact_input - row_mean[:, None]) * inverse_deviation[:, None]
    return (centred_rows * norm_gain + norm_offset, centred_rows, inverse_deviation)


def norm_backward_pass(incoming_gradient, centred_rows, inverse_deviation, norm_gain):
    scaled_rows = incoming_gradient * norm_gain
    first_branch, second_branch = row_sum_values(
        jnp.sum(scaled_rows, 1), jnp.sum(scaled_rows * centred_rows, 1)
    )
    return inverse_deviation[:, None] * (
        scaled_rows
        - first_branch[:, None] / MODEL_WIDTH
        - centred_rows * second_branch[:, None] / MODEL_WIDTH
    )


def seg_mask(segments):
    return (segments[:, None] == segments[None, :])[None]


def attend_forward(items):
    queries, keys, values, segments = items
    scores = jnp.einsum("qhd,khd->hqk", queries, keys, preferred_element_type=jnp.float32) * 0.125
    scores = jnp.where(seg_mask(segments), scores, -1e30)
    peak = jnp.max(scores, -1, keepdims=True)
    expo = jnp.exp(scores - peak)
    total = jnp.sum(expo, -1, keepdims=True)
    probs = (expo / total).astype(jnp.bfloat16)
    mixed = jnp.einsum("hqk,khd->qhd", probs, values, preferred_element_type=jnp.float32)
    return (mixed.astype(jnp.bfloat16), (peak + jnp.log(total))[..., 0])


def attend_backward(items):
    queries, keys, values, segments, dmixed, lse = items
    scores = jnp.einsum("qhd,khd->hqk", queries, keys, preferred_element_type=jnp.float32) * 0.125
    probs = jnp.where(seg_mask(segments), jnp.exp(scores - lse[..., None]), 0.0)
    dvalues = jnp.einsum(
        "hqk,qhd->khd", probs.astype(jnp.bfloat16), dmixed, preferred_element_type=jnp.float32
    )
    dprobs = jnp.einsum("qhd,khd->hqk", dmixed, values, preferred_element_type=jnp.float32)
    middle = jnp.sum(probs * dprobs, -1, keepdims=True)
    dscores = (probs * (dprobs - middle)).astype(jnp.bfloat16)
    dqueries = jnp.einsum("hqk,khd->qhd", dscores, keys, preferred_element_type=jnp.float32) * 0.125
    dkeys = jnp.einsum("hqk,qhd->khd", dscores, queries, preferred_element_type=jnp.float32) * 0.125
    return (dqueries.astype(jnp.bfloat16), dkeys.astype(jnp.bfloat16), dvalues.astype(jnp.bfloat16))


def shards(
    hidden_in,
    segment_ids,
    query_weight,
    query_bias,
    key_weight,
    value_weight,
    value_bias,
    attn_out_weight,
    attn_out_bias,
    norm1_gain,
    first_norm_offset,
    inner_weight,
    inner_bias,
    outer_weight,
    outer_bias,
    norm2_gain,
    second_norm_offset,
    cotangent,
):
    local_seqs = segment_ids.shape[0]
    col_width = query_weight.shape[1]
    head_local = col_width // HD
    first_norm_gain = norm1_gain.astype(jnp.float32)
    second_norm_gain = norm2_gain.astype(jnp.float32)
    x_full = col_gather(hidden_in)
    part_q, part_k, part_v = (
        lax.psum_scatter(product(x_full, query_weight), "row", scatter_dimension=0, tiled=True),
        lax.psum_scatter(product(x_full, key_weight), "row", scatter_dimension=0, tiled=True),
        lax.psum_scatter(product(x_full, value_weight), "row", scatter_dimension=0, tiled=True),
    )
    queries = (part_q + query_bias).astype(jnp.bfloat16)
    keys = part_k.astype(jnp.bfloat16)
    values = (part_v + value_bias).astype(jnp.bfloat16)
    q_heads = queries.reshape(local_seqs, SEQ, head_local, HD)
    k_heads = keys.reshape(local_seqs, SEQ, head_local, HD)
    v_heads = values.reshape(local_seqs, SEQ, head_local, HD)
    mixed, lse = lax.map(attend_forward, (q_heads, k_heads, v_heads, segment_ids))
    mixed = mixed.reshape(local_seqs * SEQ, col_width)
    mixed_full = row_gather(mixed)
    attn = col_reduce(product(mixed_full, attn_out_weight)) + attn_out_bias
    first_preact = hidden_in.astype(jnp.float32) + attn
    hidden_state, first_centred_rows, first_inverse_deviation = apply_norm(
        first_preact, first_norm_gain, first_norm_offset
    )
    hidden_full = col_gather(hidden_state.astype(jnp.bfloat16))
    inner = row_reduce(product(hidden_full, inner_weight)) + inner_bias
    active = jax.nn.gelu(inner, approximate=False).astype(jnp.bfloat16)
    active_full = row_gather(active)
    outer_product = col_reduce(product(active_full, outer_weight)) + outer_bias
    closing_result, second_centred_rows, second_inverse_deviation = apply_norm(
        hidden_state + outer_product, second_norm_gain, second_norm_offset
    )
    layer_out = closing_result.astype(jnp.bfloat16)
    output_gradient = cotangent.astype(jnp.float32)
    second_gain_gradient = jnp.sum(output_gradient * second_centred_rows, 0)
    shift_two_grad = jnp.sum(output_gradient, 0)
    second_preact_grad = norm_backward_pass(
        output_gradient, second_centred_rows, second_inverse_deviation, second_norm_gain
    )
    dout_full = col_gather(second_preact_grad.astype(jnp.bfloat16))
    outer_bias_grad = jnp.sum(dout_full, 0, dtype=jnp.float32)
    outer_weight_grad = over_tokens(active_full, dout_full)
    dactive = row_reduce(against(dout_full, outer_weight))
    cdf = 0.5 * (1.0 + lax.erf(inner * inv_root_two))
    density = jnp.exp(-0.5 * inner * inner) * inv_root_two_pi
    dinner = (dactive * (cdf + inner * density)).astype(jnp.bfloat16)
    dinner_full = row_gather(dinner)
    inner_bias_grad = jnp.sum(dinner_full, 0, dtype=jnp.float32)
    inner_weight_grad = over_tokens(hidden_full, dinner_full)
    hidden_state_grad = second_preact_grad + col_reduce(against(dinner_full, inner_weight))
    first_gain_gradient = jnp.sum(hidden_state_grad * first_centred_rows, 0)
    shift_one_grad = jnp.sum(hidden_state_grad, 0)
    first_preact_grad = norm_backward_pass(
        hidden_state_grad, first_centred_rows, first_inverse_deviation, first_norm_gain
    )
    dattn_full = col_gather(first_preact_grad.astype(jnp.bfloat16))
    attn_out_bias_grad = jnp.sum(dattn_full, 0, dtype=jnp.float32)
    attn_out_weight_grad = over_tokens(mixed_full, dattn_full)
    dmixed = row_reduce(against(dattn_full, attn_out_weight)).astype(jnp.bfloat16)
    dq_heads, dk_heads, dv_heads = lax.map(
        attend_backward,
        (
            q_heads,
            k_heads,
            v_heads,
            segment_ids,
            dmixed.reshape(local_seqs, SEQ, head_local, HD),
            lse,
        ),
    )
    dq_rows = dq_heads.reshape(local_seqs * SEQ, col_width)
    dk_rows = dk_heads.reshape(local_seqs * SEQ, col_width)
    dv_rows = dv_heads.reshape(local_seqs * SEQ, col_width)
    dq_full, dk_full, dv_full = (
        lax.all_gather(dq_rows, "row", axis=0, tiled=True),
        lax.all_gather(dk_rows, "row", axis=0, tiled=True),
        lax.all_gather(dv_rows, "row", axis=0, tiled=True),
    )
    query_bias_grad = jnp.sum(dq_full, 0, dtype=jnp.float32)
    value_bias_grad = jnp.sum(dv_full, 0, dtype=jnp.float32)
    query_weight_grad = over_tokens(x_full, dq_full)
    key_weight_grad = over_tokens(x_full, dk_full)
    value_weight_grad = over_tokens(x_full, dv_full)
    dx_part = (
        against(dq_full, query_weight)
        + against(dk_full, key_weight)
        + against(dv_full, value_weight)
    )
    input_grad = (first_preact_grad + col_reduce(dx_part)).astype(jnp.bfloat16)
    summed = (
        lax.psum(query_weight_grad.astype(jnp.bfloat16), "dp").astype(jnp.float32),
        lax.psum(query_bias_grad.astype(jnp.bfloat16), "dp").astype(jnp.float32),
        lax.psum(key_weight_grad.astype(jnp.bfloat16), "dp").astype(jnp.float32),
        lax.psum(value_weight_grad.astype(jnp.bfloat16), "dp").astype(jnp.float32),
        lax.psum(value_bias_grad.astype(jnp.bfloat16), "dp").astype(jnp.float32),
        lax.psum(attn_out_weight_grad.astype(jnp.bfloat16), "dp").astype(jnp.float32),
        lax.psum(attn_out_bias_grad.astype(jnp.bfloat16), "dp").astype(jnp.float32),
        lax.psum(inner_weight_grad.astype(jnp.bfloat16), "dp").astype(jnp.float32),
        lax.psum(inner_bias_grad.astype(jnp.bfloat16), "dp").astype(jnp.float32),
        lax.psum(outer_weight_grad.astype(jnp.bfloat16), "dp").astype(jnp.float32),
        lax.psum(outer_bias_grad.astype(jnp.bfloat16), "dp").astype(jnp.float32),
    )
    norms = lax.psum(
        (first_gain_gradient, shift_one_grad, second_gain_gradient, shift_two_grad), ("dp", "col")
    )
    return (
        layer_out,
        input_grad,
        summed[0],
        summed[1],
        summed[2],
        summed[3],
        summed[4],
        summed[5],
        summed[6],
        norms[0],
        norms[1],
        summed[7],
        summed[8],
        summed[9],
        summed[10],
        norms[2],
        norms[3],
    )


def solution(mesh):
    in_specs = (
        P(("dp", "col"), "row"),
        P(("dp", "row"), None),
        P("row", "col"),
        P("col"),
        P("row", "col"),
        P("row", "col"),
        P("col"),
        P("col", "row"),
        P("row"),
        P("row"),
        P("row"),
        P("row", "col"),
        P("col"),
        P("col", "row"),
        P("row"),
        P("row"),
        P("row"),
        P(("dp", "col"), "row"),
    )
    out_specs = (
        P(("dp", "col"), "row"),
        P(("dp", "col"), "row"),
        P("row", "col"),
        P("col"),
        P("row", "col"),
        P("row", "col"),
        P("col"),
        P("col", "row"),
        P("row"),
        P("row"),
        P("row"),
        P("row", "col"),
        P("col"),
        P("col", "row"),
        P("row"),
        P("row"),
        P("row"),
    )
    return jax.shard_map(shards, mesh=mesh, in_specs=in_specs, out_specs=out_specs, check_vma=False)
```

profile of v0, /device:TPU:0, one launch (start us, length us, event | category | flops | bytes accessed | tf_op | source)
XLA Modules:
  0.0 1692.1 jit_solution(16431331200616118843)
XLA Ops:
  8.0 13.4 all-gather.11.cloned.1.call-done
  33.9 69.5 %reduce-scatter.15.cloned.1.call-done = f32[512,512]{1,0:T(8,128)} async-done(((f32[2048,512]{1,0:T(8,128)}), f32[512,512]{1,0:T(8,128)}) %reduce-scatter.15.cloned.1.call-update) | async-done | bytes 1048592 | tf_op jit(solution)/shard_map/reduce_scatter | solution.py:133
  104.9 78.2 %reduce-scatter.13.cloned.1.call-done = f32[512,512]{1,0:T(8,128)} async-done(((f32[2048,512]{1,0:T(8,128)}), f32[512,512]{1,0:T(8,128)}) %reduce-scatter.13.cloned.1.call-update) | async-done | bytes 1048592 | tf_op jit(solution)/shard_map/reduce_scatter | solution.py:132
  186.5 76.0 %reduce-scatter.11.cloned.1.call-done = f32[512,512]{1,0:T(8,128)} async-done(((f32[2048,512]{1,0:T(8,128)}), f32[512,512]{1,0:T(8,128)}) %reduce-scatter.11.cloned.1.call-update) | async-done | bytes 1048592 | tf_op jit(solution)/shard_map/reduce_scatter | solution.py:134
  274.7 46.5 %all-gather.13.cloned.1.call-done = bf16[2048,512]{0,1:T(8,128)(2,1)} async-done(((bf16[512,512]{0,1:T(8,128)(2,1)}), bf16[2048,512]{0,1:T(8,128)(2,1)}) %all-gather.13.cloned.1.call-update) | async-done | bytes 2097168 | tf_op jit(solution)/shard_map/all_gather | solution.py:37
  325.1 8.4 reduce-scatter.17.cloned.1.call-done
  335.1 12.1 all-reduce.4
  348.7 7.1 all-gather.15.cloned.1.call-done
  355.8 9.6 fusion.53
  366.1 281.0 %reduce-scatter.19.cloned.1.call-done = f32[512,2048]{1,0:T(8,128)} async-done(((f32[2048,2048]{1,0:T(8,128)}), f32[512,2048]{1,0:T(8,128)}) %reduce-scatter.19.cloned.1.call-update) | async-done | bytes 4194320 | tf_op jit(solution)/shard_map/reduce_scatter | solution.py:41
  647.0 11.3 fusion.4
  658.4 150.4 %all-gather.17.cloned.1.call-done = bf16[2048,2048]{1,0:T(8,128)(2,1)} async-done(((bf16[512,2048]{1,0:T(8,128)(2,1)}), bf16[2048,2048]{1,0:T(8,128)(2,1)}) %all-gather.17.cloned.1.call-update) | async-done | bytes 8388624 | tf_op jit(solution)/shard_map/all_gather | solution.py:37
  808.9 7.1 fusion.54
  816.0 7.9 reduce-scatter.21.cloned.1.call-done
  826.5 12.1 all-reduce.3
  840.7 8.5 all-reduce.2
  851.9 8.7 all-gather.19.cloned.1.call-done
  860.7 9.3 fusion.55
  870.3 281.4 %reduce-scatter.23.cloned.1.call-done = f32[512,2048]{1,0:T(8,128)} async-done(((f32[2048,2048]{1,0:T(8,128)}), f32[512,2048]{1,0:T(8,128)}) %reduce-scatter.23.cloned.1.call-update) | async-done | bytes 4194320 | tf_op jit(solution)/shard_map/reduce_scatter | solution.py:41
  1157.1 150.4 %all-gather.21.cloned.1.call-done = bf16[2048,2048]{1,0:T(8,128)(2,1)} async-done(((bf16[512,2048]{1,0:T(8,128)(2,1)}), bf16[2048,2048]{1,0:T(8,128)(2,1)}) %all-gather.21.cloned.1.call-update) | async-done | bytes 8388624 | tf_op jit(solution)/shard_map/all_gather | solution.py:37
  1307.6 7.3 fusion.56
  1315.0 7.9 reduce-scatter.25.cloned.1.call-done
  1326.2 12.2 all-reduce.1
  1341.3 7.3 all-gather.23.cloned.1.call-done
  1352.6 78.0 %reduce-scatter.27.cloned.1.call-done = f32[512,512]{1,0:T(8,128)} async-done(((f32[2048,512]{1,0:T(8,128)}), f32[512,512]{1,0:T(8,128)}) %reduce-scatter.27.cloned.1.call-update) | async-done | bytes 1048592 | tf_op jit(solution)/shard_map/reduce_scatter | solution.py:41
  1456.7 7.1 convolution_convert_fusion
  1472.2 12.6 all-gather.29.cloned.1.call-done
  1487.7 43.8 %all-gather.25.cloned.1.call-done = bf16[2048,512]{0,1:T(8,128)(2,1)} async-done(((bf16[512,512]{0,1:T(8,128)(2,1)}), bf16[2048,512]{0,1:T(8,128)(2,1)}) %all-gather.25.cloned.1.call-update) | async-done | bytes 2097168 | tf_op jit(solution)/shard_map/all_gather | solution.py:200
  1534.5 43.9 %all-gather.27.cloned.1.call-done = bf16[2048,512]{0,1:T(8,128)(2,1)} async-done(((bf16[512,512]{0,1:T(8,128)(2,1)}), bf16[2048,512]{0,1:T(8,128)(2,1)}) %all-gather.27.cloned.1.call-update) | async-done | bytes 2097168 | tf_op jit(solution)/shard_map/all_gather | solution.py:201
  1594.4 14.5 all-reduce
  1611.4 7.7 all-reduce.5
  1622.0 48.7 %all-reduce.9.cloned.1.call-done = (bf16[256,512]{0,1:T(8,128)(2,1)}, bf16[256,512]{0,1:T(8,128)(2,1)}, bf16[256,512]{0,1:T(8,128)(2,1)}, bf16[512,256]{1,0:T(8,...) async-done(((bf16[256,512]{0,1:T(8,128)(2,1)}, bf16[256,512]{0,1:T(8,128)(2,1)}, bf16[256,512]{0,1:T(8,128)(2,1)}, bf16[512,256]{1,0:T(8,128)(2,1)}, ...) | async-done | bytes 3145744 | tf_op jit(solution)/shard_map/psum | solution.py:216
  (184 shorter events, 137.1 us)
Async XLA Ops:
  7.2 801.7 %copy-start = (bf16[2048,256]{1,0:T(8,128)(2,1)S(1)}, bf16[2048,256]{1,0:T(8,128)(2,1)}, u32[]{:S(2)}) copy-start(bf16[2048,256]{1,0:T(8,128)(2,1)} %param.31) | copy-start | bytes 3145732
  7.2 14.1 all-gather.11.cloned.1.call-start
  7.9 95.4 %reduce-scatter.15.cloned.1.call-start = ((), (), s32[]{:S(2)}) async-start(), calls=%async_computation.13 | async-start | bytes 5242880 | tf_op jit(solution)/shard_map/reduce_scatter | solution.py:133
  25.3 157.8 %reduce-scatter.13.cloned.1.call-start = ((), (), s32[]{:S(2)}) async-start(), calls=%async_computation.12 | async-start | bytes 5242880 | tf_op jit(solution)/shard_map/reduce_scatter | solution.py:132
  29.2 233.3 %reduce-scatter.11.cloned.1.call-start = ((), (), s32[]{:S(2)}) async-start(), calls=%async_computation.11 | async-start | bytes 5242880 | tf_op jit(solution)/shard_map/reduce_scatter | solution.py:134
  32.9 288.3 %all-gather.13.cloned.1.call-start = ((), (), s32[]{:S(2)}) async-start(), calls=%async_computation.14 | async-start | bytes 2621440 | tf_op jit(solution)/shard_map/all_gather | solution.py:37
  104.9 163.3 %copy-start.13 = (bf16[512,512]{0,1:T(8,128)(2,1)}, bf16[512,512]{0,1:T(8,128)(2,1)S(1)}, u32[]{:S(2)}) copy-start(bf16[512,512]{0,1:T(8,128)(2,1)S(1)} %copy.52) | copy-start | bytes 1572868
  186.5 81.7 %copy-start.11 = (bf16[512,512]{0,1:T(8,128)(2,1)}, bf16[512,512]{0,1:T(8,128)(2,1)S(1)}, u32[]{:S(2)}) copy-start(bf16[512,512]{0,1:T(8,128)(2,1)S(1)} %copy.51) | copy-start | bytes 1572868
  271.4 49.8 %copy-start.18 = (bf16[512,256]{1,0:T(8,128)(2,1)S(1)}, bf16[512,256]{1,0:T(8,128)(2,1)}, u32[]{:S(2)}) copy-start(bf16[512,256]{1,0:T(8,128)(2,1)} %param.25) | copy-start | bytes 786436
  274.7 50.3 %copy-start.30 = (bf16[256]{0:T(256)(128)(2,1)S(1)}, bf16[256]{0:T(256)(128)(2,1)}, u32[]{:S(2)}) copy-start(bf16[256]{0:T(256)(128)(2,1)} %param.27) | copy-start | bytes 1540
  274.7 50.3 %copy-start.31 = (bf16[256]{0:T(256)(128)(2,1)S(1)}, bf16[256]{0:T(256)(128)(2,1)}, u32[]{:S(2)}) copy-start(bf16[256]{0:T(256)(128)(2,1)} %param.28) | copy-start | bytes 1540
  274.7 50.4 %copy-start.32 = (bf16[256]{0:T(256)(128)(2,1)S(1)}, bf16[256]{0:T(256)(128)(2,1)}, u32[]{:S(2)}) copy-start(bf16[256]{0:T(256)(128)(2,1)} %param.26) | copy-start | bytes 1540
  274.7 58.7 %reduce-scatter.17.cloned.1.call-start = ((), (), s32[]{:S(2)}) async-start(), calls=%async_computation.15 | async-start | bytes 3145728 | tf_op jit(solution)/shard_map/reduce_scatter | solution.py:45
  324.9 30.8 %all-gather.15.cloned.1.call-start = ((), (), s32[]{:S(2)}) async-start(), calls=%async_computation.16 | async-start | bytes 1572864 | tf_op jit(solution)/shard_map/all_gather | solution.py:33
  348.4 298.6 %reduce-scatter.19.cloned.1.call-start = ((), (), s32[]{:S(2)}) async-start(), calls=%async_computation.17 | async-start | bytes 20971520 | tf_op jit(solution)/shard_map/reduce_scatter | solution.py:41
  365.4 443.5 %all-gather.17.cloned.1.call-start = ((), (), s32[]{:S(2)}) async-start(), calls=%async_computation.18 | async-start | bytes 10485760 | tf_op jit(solution)/shard_map/all_gather | solution.py:37
  658.4 157.6 %copy-start.33 = (bf16[256]{0:T(256)(128)(2,1)S(1)}, bf16[256]{0:T(256)(128)(2,1)}, u32[]{:S(2)}) copy-start(bf16[256]{0:T(256)(128)(2,1)} %param.33) | copy-start | bytes 1540
  658.4 157.7 %copy-start.34 = (bf16[256]{0:T(256)(128)(2,1)S(1)}, bf16[256]{0:T(256)(128)(2,1)}, u32[]{:S(2)}) copy-start(bf16[256]{0:T(256)(128)(2,1)} %param.32) | copy-start | bytes 1540
  658.4 165.6 %reduce-scatter.21.cloned.1.call-start = ((), (), s32[]{:S(2)}) async-start(), calls=%async_computation.19 | async-start | bytes 3145728 | tf_op jit(solution)/shard_map/reduce_scatter | solution.py:45
  816.0 44.7 %all-gather.19.cloned.1.call-start = ((), (), s32[]{:S(2)}) async-start(), calls=%async_computation.20 | async-start | bytes 1572864 | tf_op jit(solution)/shard_map/all_gather | solution.py:33
  851.9 299.8 %reduce-scatter.23.cloned.1.call-start = ((), (), s32[]{:S(2)}) async-start(), calls=%async_computation.21 | async-start | bytes 20971520 | tf_op jit(solution)/shard_map/reduce_scatter | solution.py:41
  870.0 437.5 %all-gather.21.cloned.1.call-start = ((), (), s32[]{:S(2)}) async-start(), calls=%async_computation.22 | async-start | bytes 10485760 | tf_op jit(solution)/shard_map/all_gather | solution.py:37
  1157.0 157.9 %copy-start.35 = (bf16[256]{0:T(256)(128)(2,1)S(1)}, bf16[256]{0:T(256)(128)(2,1)}, u32[]{:S(2)}) copy-start(bf16[256]{0:T(256)(128)(2,1)} %param.34) | copy-start | bytes 1540
  1157.1 165.8 %copy-start.6 = (f32[1024,256]{1,0:T(8,128)S(1)}, f32[1024,256]{1,0:T(8,128)}, u32[]{:S(2)}) copy-start(f32[1024,256]{1,0:T(8,128)} %get-tuple-element.140) | copy-start | bytes 3145732
  1157.1 165.8 %reduce-scatter.25.cloned.1.call-start = ((), (), s32[]{:S(2)}) async-start(), calls=%async_computation.23 | async-start | bytes 3145728 | tf_op jit(solution)/shard_map/reduce_scatter | solution.py:45
  1314.9 33.6 %all-gather.23.cloned.1.call-start = ((), (), s32[]{:S(2)}) async-start(), calls=%async_computation.24 | async-start | bytes 1572864 | tf_op jit(solution)/shard_map/all_gather | solution.py:33
  1341.2 89.4 %reduce-scatter.27.cloned.1.call-start = ((), (), s32[]{:S(2)}) async-start(), calls=%async_computation.25 | async-start | bytes 5242880 | tf_op jit(solution)/shard_map/reduce_scatter | solution.py:41
  1352.5 132.2 %all-gather.29.cloned.1.call-start = ((), (), s32[]{:S(2)}) async-start(), calls=%async_computation.28 | async-start | bytes 2621440 | tf_op jit(solution)/shard_map/all_gather | solution.py:202
  1438.1 93.4 %all-gather.25.cloned.1.call-start = ((), (), s32[]{:S(2)}) async-start(), calls=%async_computation.26 | async-start | bytes 2621440 | tf_op jit(solution)/shard_map/all_gather | solution.py:200
  1451.8 126.6 %all-gather.27.cloned.1.call-start = ((), (), s32[]{:S(2)}) async-start(), calls=%async_computation.27 | async-start | bytes 2621440 | tf_op jit(solution)/shard_map/all_gather | solution.py:201
  1456.2 214.5 %all-reduce.9.cloned.1.call-start = ((), (), s32[]{:S(2)}) async-start(), calls=%async_computation.30 | async-start | bytes 6291456 | tf_op jit(solution)/shard_map/psum | solution.py:216
  1581.4 101.6 %reduce-scatter.29.cloned.1.call-start = ((), (), s32[]{:S(2)}) async-start(), calls=%async_computation.29 | async-start | bytes 3145728 | tf_op jit(solution)/shard_map/reduce_scatter | solution.py:45
  (25 other events, 156.2 us)
Sparse Core Ops, SparseCore 0:
  9.6 11.7 all-gather.10
  25.4 77.9 reduce-scatter.14
  105.8 77.2 reduce-scatter.12
  185.2 77.2 reduce-scatter.10
  274.8 46.4 all-gather.12
  325.1 8.3 reduce-scatter.16
  348.6 7.1 all-gather.14
  365.5 281.4 reduce-scatter.18
  658.5 150.3 all-gather.16
  816.1 7.8 reduce-scatter.20
  852.0 8.6 all-gather.18
  870.2 281.4 reduce-scatter.22
  1157.2 150.3 all-gather.20
  1315.0 7.8 reduce-scatter.24
  1341.3 7.1 all-gather.22
  1352.6 77.9 reduce-scatter.26
  1438.2 46.4 all-gather.28
  1486.8 44.6 all-gather.24
  1533.7 44.6 all-gather.26
  1583.5 87.1 all-reduce.8
  1673.0 9.5 reduce-scatter.28
where the time goes:
time: 1700 us; the launch traced here: 1690 us
  waiting for transfers between devices  1420 us (84%)
  matrix products  102 us (6%)
  other arithmetic  67.2 us (4%)
  blocking collectives  67.1 us (4%)
  local copies, waits for them, and re-layouts  17.2 us (1%)
    reduce_scatter x3, waiting for transfers between devices, row_reduce(): return lax.psum_scatter(values, 'row', scatter_dimension=0, tiled=True)  640 us
    all_gather x3, waiting for transfers between devices, row_gather(): return lax.all_gather(values, 'row', axis=0, tiled=True)  347 us
    reduce_scatter x1, waiting for transfers between devices, shards(): lax.psum_scatter(product(x_full, query_weight), 'row', scatter_dimension=...  78.2 us
    reduce_scatter x1, waiting for transfers between devices, shards(): lax.psum_scatter(product(x_full, value_weight), 'row', scatter_dimension=...  76 us
    reduce_scatter x1, waiting for transfers between devices, shards(): lax.psum_scatter(product(x_full, key_weight), 'row', scatter_dimension=0,...  69.5 us
    psum x1, waiting for transfers between devices, shards(): lax.psum(query_weight_grad.astype(jnp.bfloat16), 'dp').astype(jnp.float32)  48.7 us
    psum x4, blocking collectives, row_sum_values(): return lax.psum((first_branch, second_branch), 'row')  44.9 us
    all_gather x1, waiting for transfers between devices, shards(): lax.all_gather(dk_rows, 'row', axis=0, tiled=True)  43.9 us
  transfers between devices with their start and end apart: 21, of which 20 were waited for; matrix products, arithmetic and copies ran while one was open for 5% of the time, Pallas kernels for 0%

commit v1 on v0

--- a/solution.py
+++ b/solution.py
@@ -1,6 +1,10 @@
+import functools
+
 import jax
 import jax.numpy as jnp
 from jax import lax
+from jax.experimental import pallas as pl
+from jax.experimental.pallas import tpu as pltpu
 from jax.sharding import PartitionSpec as P
 
 MODEL_WIDTH = 1024
@@ -249,44 +253,833 @@
     )
 
 
+IN_SPECS = (
+    P(("dp", "col"), "row"),
+    P(("dp", "row"), None),
+    P("row", "col"),
+    P("col"),
+    P("row", "col"),
+    P("row", "col"),
+    P("col"),
+    P("col", "row"),
+    P("row"),
+    P("row"),
+    P("row"),
+    P("row", "col"),
+    P("col"),
+    P("col", "row"),
+    P("row"),
+    P("row"),
+    P("row"),
+    P(("dp", "col"), "row"),
+)
+OUT_SPECS = (
+    P(("dp", "col"), "row"),
+    P(("dp", "col"), "row"),
+    P("row", "col"),
+    P("col"),
+    P("row", "col"),
+    P("row", "col"),
+    P("col"),
+    P("col", "row"),
+    P("row"),
+    P("row"),
+    P("row"),
+    P("row", "col"),
+    P("col"),
+    P("col", "row"),
+    P("row"),
+    P("row"),
+    P("row"),
+)
+
+
+MESH = pl.DeviceIdType.MESH
+LINE = 4
+GROUPS = 4
+
+
+class Spot:
+    def __init__(self):
+        self.dp = lax.axis_index("dp")
+        self.row = lax.axis_index("row")
+        self.col = lax.axis_index("col")
+        k, r = self.dp, self.row
+        self.dp_x = k + 1 - 2 * lax.rem(k, 2)
+        self.dp_y = lax.rem(k + 2, 4)
+        self.dp_d = 3 - k
+        self.beside_x = (self.dp_x, r, self.col)
+        self.beside_y = (self.dp_y, r, self.col)
+        self.other_core = (k, r, 1 - self.col)
+        self.inside = jnp.logical_and(r > 0, r < LINE - 1)
+        first = jnp.where(r > 0, r - 1, 1)
+        second = jnp.where(r == 0, 2, jnp.where(r == LINE - 1, 1, r + 1))
+        third = jnp.where(r < 2, LINE - 1, 0)
+        self.near = (first, second, third)
+
+    def at_row(self, row):
+        return (self.dp, row, self.col)
+
+
+def remote(src, dst, send, recv, device):
+    return pltpu.make_async_remote_copy(
+        src_ref=src, dst_ref=dst, send_sem=send, recv_sem=recv, device_id=device, device_id_type=MESH
+    )
+
+
+def greet(spot):
+    barrier = pltpu.get_barrier_semaphore()
+    for away in range(LINE):
+        row = lax.rem(spot.row + away, LINE)
+        for core in range(2):
+            if away == 0 and core == 0:
+                continue
+            col = lax.rem(spot.col + core, 2)
+            pl.semaphore_signal(barrier, inc=1, device_id=(spot.dp, row, col), device_id_type=MESH)
+    pl.semaphore_signal(barrier, inc=1, device_id=spot.beside_x, device_id_type=MESH)
+    pl.semaphore_signal(barrier, inc=1, device_id=spot.beside_y, device_id_type=MESH)
+    pl.semaphore_wait(barrier, 2 * LINE + 1)
+
+
+class Gather:
+    SEMS = (
+        [pltpu.SemaphoreType.DMA((GROUPS, 2))]
+        + [pltpu.SemaphoreType.DMA((GROUPS,))]
+        + [pltpu.SemaphoreType.DMA((GROUPS, LINE))] * 12
+    )
+
+    def __init__(self, spot, shards, bufs, sems):
+        self.spot, self.shards, self.bufs = spot, shards, bufs
+        (self.own_s, self.own_l, self.zs, self.zr, self.xs, self.xr, self.ys, self.yr, self.fas, self.far, self.fbs, self.fbr, *_) = sems
+        self.quarter = [s.shape[0] // 4 for s in shards]
+
+    def piece(self, g, row, j, half=None):
+        q = self.quarter[g]
+        if half is None:
+            return self.bufs[g].at[row, pl.ds(pl.multiple_of(j * q, q), q)]
+        h = q // 2
+        return self.bufs[g].at[row, pl.ds(pl.multiple_of(j * q + half * h, h), h)]
+
+    def own_copy(self, g, up):
+        s, q = self.spot, self.quarter[g]
+        src = self.shards[g].at[pl.ds(pl.multiple_of(s.dp * q, q), q)]
+        row = s.row + 1 if up else s.row - 1
+        return remote(src, self.piece(g, s.row, s.dp), self.own_s.at[g, int(up)], self.zr.at[g, s.row], s.at_row(row))
+
+    def local(self, g):
+        return pltpu.make_async_copy(self.shards[g], self.bufs[g].at[self.spot.row], self.own_l.at[g])
+
+    def start_own(self, g):
+        s = self.spot
+
+        @pl.when(s.row < LINE - 1)
+        def _():
+            self.own_copy(g, True).start()
+
+        @pl.when(s.row > 0)
+        def _():
+            self.own_copy(g, False).start()
+
+        self.local(g).start()
+
+    def onward(self, g, n):
+        s = self.spot
+        row = s.near[n]
+        p = self.piece(g, row, s.dp)
+        to = jnp.where(row < s.row, s.row + 1, s.row - 1)
+        return remote(p, p, self.zs.at[g, row], self.zr.at[g, row], s.at_row(to))
+
+    def across(self, g, n):
+        s = self.spot
+        row = s.near[n]
+        p = self.piece(g, row, s.dp)
+        return (
+            remote(p, p, self.xs.at[g, row], self.xr.at[g, row], s.beside_x),
+            remote(p, p, self.ys.at[g, row], self.yr.at[g, row], s.beside_y),
+        )
+
+    def relays(self, g, n):
+        s = self.spot
+        row = s.near[n]
+        a = self.piece(g, row, s.dp_y, 0)
+        b = self.piece(g, row, s.dp_x, 1)
+        return (
+            remote(a, a, self.fas.at[g, row], self.far.at[g, row], s.beside_x),
+            remote(b, b, self.fbs.at[g, row], self.fbr.at[g, row], s.beside_y),
+        )
+
+    def z_step(self, g, n):
+        self.onward(g, n).wait_recv()
+
+        @pl.when(self.spot.inside)
+        def _():
+            self.onward(g, n).start()
+
+        for c in self.across(g, n):
+            c.start()
+
+    def xy_step(self, g, n):
+        x, y = self.across(g, n)
+        a, b = self.relays(g, n)
+        s = self.spot
+        row = s.near[n]
+        px, py = self.piece(g, row, s.dp_x), self.piece(g, row, s.dp_y)
+        remote(px, px, self.xs.at[g, row], self.xr.at[g, row], s.beside_x).wait_recv()
+        b.start()
+        remote(py, py, self.ys.at[g, row], self.yr.at[g, row], s.beside_y).wait_recv()
+        a.start()
+
+    def arrive(self, g, n):
+        s = self.spot
+        row = s.near[n]
+        a, b = self.piece(g, row, s.dp_d, 0), self.piece(g, row, s.dp_d, 1)
+        remote(a, a, self.fas.at[g, row], self.far.at[g, row], s.beside_x).wait_recv()
+        remote(b, b, self.fbs.at[g, row], self.fbr.at[g, row], s.beside_y).wait_recv()
+
+    def drain(self):
+        s = self.spot
+        for g in range(GROUPS):
+
+            @pl.when(s.row < LINE - 1)
+            def _():
+                self.own_copy(g, True).wait_send()
+
+            @pl.when(s.row > 0)
+            def _():
+                self.own_copy(g, False).wait_send()
+
+            for n in range(LINE - 1):
+
+                @pl.when(s.inside)
+                def _():
+                    self.onward(g, n).wait_send()
+
+                for c in self.across(g, n) + self.relays(g, n):
+                    c.wait_send()
+
+
+class Tokens:
+    SEMS = [pltpu.SemaphoreType.DMA((2,)), pltpu.SemaphoreType.DMA((LINE,))] + [pltpu.SemaphoreType.DMA((LINE,))] * 2 + [
+        pltpu.SemaphoreType.DMA((2, 2)),
+        pltpu.SemaphoreType.DMA((LINE,)),
+        pltpu.SemaphoreType.DMA((LINE,)),
+        pltpu.SemaphoreType.DMA((LINE,)),
+    ]
+
+    def __init__(self, spot, x, ct, par, xs, cts, pars, sems):
+        self.spot = spot
+        self.x, self.ct, self.par, self.xs, self.cts, self.pars = x, ct, par, xs, cts, pars
+        (self.x_s, self.x_r, self.x_fs, self.x_fr, self.c_s, self.c_r, self.p_s, self.p_r) = sems
+        self.seq = x.shape[0] // 2
+        self.wide = x.shape[1]
+
+    def cols(self, ref, row):
+        return ref.at[:, pl.ds(pl.multiple_of(row * self.wide, self.wide), self.wide)]
+
+    def each(self, i, do_remote, do_local, row, here):
+        @pl.when(here)
+        def _():
+            do_local()
+
+        @pl.when(jnp.logical_not(here))
+        def _():
+            do_remote()
+
+    def x_copy(self, i, local):
+        s = self.spot
+        row = 2 * s.col + i
+        src = self.x.at[pl.ds(i * self.seq, self.seq)]
+        dst = self.cols(self.xs, s.row)
+        if local:
+            return pltpu.make_async_copy(src, dst, self.x_r.at[s.row])
+        return remote(src, dst, self.x_s.at[i], self.x_r.at[s.row], s.at_row(row))
+
+    def ct_copy(self, i, core, local):
+        s = self.spot
+        half = self.seq // 2
+        row = 2 * s.col + i
+        src = self.ct.at[pl.ds(i * self.seq + core * half, half)]
+        dst = self.cols(self.cts, s.row)
+        if local:
+            return pltpu.make_async_copy(src, dst, self.c_r.at[s.row])
+        return remote(src, dst, self.c_s.at[i, core], self.c_r.at[s.row], (s.dp, row, jnp.int32(core)))
+
+    def par_copy(self, away):
+        s = self.spot
+        row = lax.rem(s.row + away, LINE)
+        if away == 0:
+            return pltpu.make_async_copy(self.par, self.pars.at[s.row], self.p_r.at[s.row])
+        return remote(self.par, self.pars.at[s.row], self.p_s.at[away], self.p_r.at[s.row], s.at_row(row))
+
+    def start_x(self):
+        s = self.spot
+        for i in range(2):
+            here = 2 * s.col + i == s.row
+
+            @pl.when(here)
+            def _():
+                self.x_copy(i, True).start()
+
+            @pl.when(jnp.logical_not(here))
+            def _():
+                self.x_copy(i, False).start()
+
+    def start_par(self):
+        for away in range(LINE):
+            self.par_copy(away).start()
+
+    def start_ct(self):
+        s = self.spot
+        for i in range(2):
+            for core in range(2):
+                here = jnp.logical_and(2 * s.col + i == s.row, s.col == core)
+
+                @pl.when(here)
+                def _():
+                    self.ct_copy(i, core, True).start()
+
+                @pl.when(jnp.logical_not(here))
+                def _():
+                    self.ct_copy(i, core, False).start()
+
+    def rows(self):
+        return (self.spot.row,) + self.spot.near
+
+    def relay(self, row):
+        block = self.cols(self.xs, row)
+        return remote(block, block, self.x_fs.at[row], self.x_fr.at[row], self.spot.other_core)
+
+    def wait_x(self):
+        s = self.spot
+        first = s.row // 2 == s.col
+        for row in self.rows():
+
+            @pl.when(first)
+            def _():
+                block = self.cols(self.xs, row)
+                pltpu.make_async_copy(block, block, self.x_r.at[row]).wait()
+                self.relay(row).start()
+
+        for row in self.rows():
+
+            @pl.when(jnp.logical_not(first))
+            def _():
+                self.relay(row).wait_recv()
+
+    def wait_ct(self):
+        for row in self.rows():
+            block = self.cols(self.cts, row)
+            pltpu.make_async_copy(block, block, self.c_r.at[row]).wait()
+
+    def wait_par(self):
+        for row in self.rows():
+            block = self.pars.at[row]
+            pltpu.make_async_copy(block, block, self.p_r.at[row]).wait()
+
+    def drain(self):
+        s = self.spot
+        for i in range(2):
+
+            @pl.when(jnp.logical_not(2 * s.col + i == s.row))
+            def _():
+                self.x_copy(i, False).wait_send()
+
+            for core in range(2):
+
+                @pl.when(jnp.logical_not(jnp.logical_and(2 * s.col + i == s.row, s.col == core)))
+                def _():
+                    self.ct_copy(i, core, False).wait_send()
+
+        for away in range(1, LINE):
+            self.par_copy(away).wait_send()
+
+        @pl.when(s.row // 2 == s.col)
+        def _():
+            for row in self.rows():
+                self.relay(row).wait_send()
+
+
+ROWS_AT_ONCE = {1536: 16, 2048: 16, 256: 64}
+
+
+class Scatter:
+    SEMS = [pltpu.SemaphoreType.DMA((GROUPS, LINE))] * 14 + [pltpu.SemaphoreType.DMA((GROUPS,))] * 10
+
+    def __init__(self, spot, parts, rel_a, rel_b, from_x, from_y, line, final, sems):
+        self.spot, self.parts, self.rel_a, self.rel_b = spot, parts, rel_a, rel_b
+        self.from_x, self.from_y, self.line, self.final = from_x, from_y, line, final
+        (
+            self.ra_s, self.ra_r, self.rb_s, self.rb_r,
+            self.xa_s, self.xa_r, self.xb_s, self.xb_r,
+            self.ya_s, self.ya_r, self.yb_s, self.yb_r,
+            self.z_s, self.z_r,
+            self.above_r, self.fx_s, self.fx_r, self.fy_s, self.fy_r,
+            self.ha_s, self.ha_r, self.hb_s, self.hb_r, self.spare,
+        ) = sems
+        self.quarter = [p.shape[1] // 4 for p in parts]
+        self.order = (spot.near[2], spot.near[1], spot.near[0], spot.row)
+
+    def part(self, g, row, j, half=None):
+        q = self.quarter[g]
+        if half is None:
+            return self.parts[g].at[row, pl.ds(pl.multiple_of(j * q, q), q)]
+        h = q // 2
+        return self.parts[g].at[row, pl.ds(pl.multiple_of(j * q + half * h, h), h)]
+
+    def half(self, ref, g, row, half):
+        h = self.quarter[g] // 2
+        return ref[g].at[row, pl.ds(half * h, h)]
+
+    def send_a(self, g, t):
+        s, row = self.spot, self.order[t]
+        return remote(self.part(g, row, s.dp_d, 0), self.rel_a[g].at[row], self.ra_s.at[g, row], self.ra_r.at[g, row], s.beside_y)
+
+    def send_b(self, g, t):
+        s, row = self.spot, self.order[t]
+        return remote(self.part(g, row, s.dp_d, 1), self.rel_b[g].at[row], self.rb_s.at[g, row], self.rb_r.at[g, row], s.beside_x)
+
+    def send_xa(self, g, t):
+        s, row = self.spot, self.order[t]
+        return remote(self.part(g, row, s.dp_x, 0), self.half(self.from_x, g, row, 0), self.xa_s.at[g, row], self.xa_r.at[g, row], s.beside_x)
+
+    def send_xb(self, g, t):
+        s, row = self.spot, self.order[t]
+        return remote(self.part(g, row, s.dp_x, 1), self.half(self.from_x, g, row, 1), self.xb_s.at[g, row], self.xb_r.at[g, row], s.beside_x)
+
+    def send_ya(self, g, t):
+        s, row = self.spot, self.order[t]
+        return remote(self.part(g, row, s.dp_y, 0), self.half(self.from_y, g, row, 0), self.ya_s.at[g, row], self.ya_r.at[g, row], s.beside_y)
+
+    def send_yb(self, g, t):
+        s, row = self.spot, self.order[t]
+        return remote(self.part(g, row, s.dp_y, 1), self.half(self.from_y, g, row, 1), self.yb_s.at[g, row], self.yb_r.at[g, row], s.beside_y)
+
+    def add(self, g, rows, out, terms):
+        wide = out.shape[-1]
+        step = min(ROWS_AT_ONCE[wide], rows)
+
+        def body(i, carry):
+            at = pl.ds(pl.multiple_of(i * step, step), step)
+            total = terms[0][at, :].astype(jnp.float32)
+            for t in terms[1:]:
+                total = total + t[at, :].astype(jnp.float32)
+            out[at, :] = total.astype(jnp.bfloat16)
+            return carry
+
+        lax.fori_loop(0, rows // step, body, 0)
+
+    def first(self, g, t):
+        self.send_a(g, t).start()
+        self.send_b(g, t).start()
+        self.send_xb(g, t).start()
+        self.send_ya(g, t).start()
+
+    def second(self, g, t):
+        s, row = self.spot, self.order[t]
+        h = self.quarter[g] // 2
+        self.send_a(g, t).wait_recv()
+        mine = self.part(g, row, s.dp_x, 0)
+        self.add(g, h, mine, (mine, self.rel_a[g].at[row]))
+        self.send_xa(g, t).start()
+        self.send_b(g, t).wait_recv()
+        mine = self.part(g, row, s.dp_y, 1)
+        self.add(g, h, mine, (mine, self.rel_b[g].at[row]))
+        self.send_yb(g, t).start()
+
+    def onward(self, g, t):
+        s, row = self.spot, self.order[t]
+        to = jnp.where(row > s.row, s.row + 1, s.row - 1)
+        slot = jnp.where(row == s.row - 1, LINE, row)
+        last = row == s.row - 1
+        piece = self.part(g, row, s.dp)
+
+        def copy(recv):
+            return remote(piece, self.line[g].at[slot], self.z_s.at[g, row], recv, s.at_row(to))
+
+        return last, copy(self.above_r.at[g]), copy(self.z_r.at[g, row])
+
+    def third(self, g, t):
+        s, row = self.spot, self.order[t]
+        q = self.quarter[g]
+        for c in (self.send_xa(g, t), self.send_xb(g, t), self.send_ya(g, t), self.send_yb(g, t)):
+            c.wait_recv()
+        mine = self.part(g, row, s.dp)
+        terms = (mine, self.from_x[g].at[row], self.from_y[g].at[row])
+        if t < LINE - 1:
+            passed = jnp.logical_or(jnp.logical_and(row > s.row, s.row > 0), jnp.logical_and(row < s.row, s.row < LINE - 1))
+            last, above, along = self.onward(g, t)
+
+            @pl.when(passed)
+            def _():
+                along.wait_recv()
+                self.add(g, q, mine, terms + (self.line[g].at[row],))
+
+            @pl.when(jnp.logical_not(passed))
+            def _():
+                self.add(g, q, mine, terms)
+
+            @pl.when(last)
+            def _():
+                above.start()
+
+            @pl.when(jnp.logical_not(last))
+            def _():
+                along.start()
+        else:
+            below, over = self.line[g].at[s.row], self.line[g].at[LINE]
+            whole = self.fin(g, s.dp)
+
+            def wait_below():
+                remote(below, below, self.z_s.at[g, s.row], self.z_r.at[g, s.row], s.beside_x).wait_recv()
+
+            def wait_over():
+                remote(over, over, self.z_s.at[g, s.row], self.above_r.at[g], s.beside_x).wait_recv()
+
+            @pl.when(s.inside)
+            def _():
+                wait_below()
+                wait_over()
+                self.add(g, q, whole, terms + (below, over))
+
+            @pl.when(s.row == 0)
+            def _():
+                wait_over()
+                self.add(g, q, whole, terms + (over,))
+
+            @pl.when(s.row == LINE - 1)
+            def _():
+                wait_below()
+                self.add(g, q, whole, terms + (below,))
+
+            for c in self.spread(g):
+                c.start()
+
+    def fin(self, g, j, half=None):
+        q = self.quarter[g]
+        if half is None:
+            return self.final[g].at[pl.ds(pl.multiple_of(j * q, q), q)]
+        h = q // 2
+        return self.final[g].at[pl.ds(pl.multiple_of(j * q + half * h, h), h)]
+
+    def spread(self, g):
+        s = self.spot
+        p = self.fin(g, s.dp)
+        return (
+            remote(p, p, self.fx_s.at[g], self.fx_r.at[g], s.beside_x),
+            remote(p, p, self.fy_s.at[g], self.fy_r.at[g], s.beside_y),
+        )
+
+    def relays(self, g):
+        s = self.spot
+        a, b = self.fin(g, s.dp_y, 0), self.fin(g, s.dp_x, 1)
+        return (
+            remote(a, a, self.ha_s.at[g], self.ha_r.at[g], s.beside_x),
+            remote(b, b, self.hb_s.at[g], self.hb_r.at[g], s.beside_y),
+        )
+
+    def fourth(self, g):
+        s = self.spot
+        px, py = self.fin(g, s.dp_x), self.fin(g, s.dp_y)
+        a, b = self.relays(g)
+        remote(px, px, self.fx_s.at[g], self.fx_r.at[g], s.beside_x).wait_recv()
+        b.start()
+        remote(py, py, self.fy_s.at[g], self.fy_r.at[g], s.beside_y).wait_recv()
+        a.start()
+
+    def fifth(self, g):
+        s = self.spot
+        a, b = self.fin(g, s.dp_d, 0), self.fin(g, s.dp_d, 1)
+        remote(a, a, self.ha_s.at[g], self.ha_r.at[g], s.beside_x).wait_recv()
+        remote(b, b, self.hb_s.at[g], self.hb_r.at[g], s.beside_y).wait_recv()
+
+    def drain(self):
+        for g in range(GROUPS):
+            for t in range(LINE):
+                for c in (
+                    self.send_a(g, t), self.send_b(g, t), self.send_xa(g, t),
+                    self.send_xb(g, t), self.send_ya(g, t), self.send_yb(g, t),
+                ):
+                    c.wait_send()
+                if t < LINE - 1:
+                    self.onward(g, t)[2].wait_send()
+            for c in self.spread(g) + self.relays(g):
+                c.wait_send()
+
+
+class Spread:
+    SEMS = [pltpu.SemaphoreType.DMA((LINE,)), pltpu.SemaphoreType.DMA((4,))]
+
+    def __init__(self, spot, src, out, sems):
+        self.spot, self.src, self.out = spot, src, out
+        self.s, self.r = sems
+        self.count, wide = src.shape
+        self.cut = wide // LINE
+
+    def slot(self, n):
+        return self.out.at[pl.ds(pl.multiple_of(n * self.count, self.count), self.count)]
+
+    def copy(self, away, local=False):
+        s = self.spot
+        row = lax.rem(s.row + away, LINE)
+        src = self.src.at[:, pl.ds(pl.multiple_of(row * self.cut, self.cut), self.cut)]
+        n = 2 * lax.rem(s.row, 2) + s.col
+        if local:
+            return pltpu.make_async_copy(src, self.slot(n), self.r.at[n])
+        return remote(src, self.slot(n), self.s.at[away], self.r.at[n], (s.dp, row, s.row // 2))
+
+    def start(self):
+        s = self.spot
+        here = s.row // 2 == s.col
+
+        @pl.when(here)
+        def _():
+            self.copy(0, True).start()
+
+        @pl.when(jnp.logical_not(here))
+        def _():
+            self.copy(0).start()
+
+        for away in range(1, LINE):
+            self.copy(away).start()
+
+    def wait(self):
+        s = self.spot
+        for n in range(4):
+            pltpu.make_async_copy(self.slot(n), self.slot(n), self.r.at[n]).wait()
+
+        @pl.when(jnp.logical_not(s.row // 2 == s.col))
+        def _():
+            self.copy(0).wait_send()
+
+        for away in range(1, LINE):
+            self.copy(away).wait_send()
+
+
+def gather_kernel(n_tok, n_gat, *refs):
+    x, ct, par, *rest = refs
+    shards, rest = rest[:GROUPS], rest[GROUPS:]
+    xs, cts, pars, *rest = rest
+    bufs, rest = rest[:GROUPS], rest[GROUPS:]
+    tok_sems, gat_sems = rest[:n_tok], rest[n_tok:]
+    spot = Spot()
+    greet(spot)
+    tokens = Tokens(spot, x, ct, par, xs, cts, pars, tok_sems)
+    gather = Gather(spot, shards, bufs, gat_sems)
+    gather.start_own(0)
+    tokens.start_x()
+    tokens.start_par()
+    todo = [(g, n) for g in range(GROUPS) for n in range(LINE - 1)]
+    for i, (g, n) in enumerate(todo):
+        if n == 0 and g + 1 < GROUPS:
+            gather.start_own(g + 1)
+        gather.z_step(g, n)
+        if i == 1:
+            tokens.wait_x()
+            tokens.start_ct()
+        if i >= 2:
+            gather.xy_step(*todo[i - 2])
+    for u in todo[-2:]:
+        gather.xy_step(*u)
+    for u in todo:
+        gather.arrive(*u)
+    for g in range(GROUPS):
+        gather.local(g).wait()
+    tokens.wait_ct()
+    tokens.wait_par()
+    gather.drain()
+    tokens.drain()
+
+
+def gather_all(x, ct, par, shards):
+    tokens, wide = x.shape
+    seq = tokens // 2
+    tok, gat = Tokens.SEMS, Gather.SEMS
+    outs = [
+        jax.ShapeDtypeStruct((seq, LINE * wide), x.dtype),
+        jax.ShapeDtypeStruct((seq // 2, LINE * wide), x.dtype),
+        jax.ShapeDtypeStruct((LINE,) + par.shape, par.dtype),
+    ] + [jax.ShapeDtypeStruct((LINE,) + s.shape, s.dtype) for s in shards]
+    anywhere = pl.BlockSpec(memory_space=pl.ANY)
+    return pl.pallas_call(
+        functools.partial(gather_kernel, len(tok), len(gat)),
+        name="gather",
+        out_shape=outs,
+        in_specs=[anywhere] * (3 + GROUPS),
+        out_specs=[anywhere] * len(outs),
+        scratch_shapes=tok + gat,
+        compiler_params=pltpu.CompilerParams(collective_id=0, has_side_effects=True),
+    )(x, ct, par, *shards)
+
+
+def scatter_kernel(n_sem, *refs):
+    grads, out, dx, rest = refs[:GROUPS], refs[GROUPS], refs[GROUPS + 1], refs[GROUPS + 2 :]
+    outs, placed_out, placed_dx, rest = rest[:GROUPS], rest[GROUPS], rest[GROUPS + 1], rest[GROUPS + 2 :]
+    parts, rel_a, rel_b, from_x, from_y, line, final = (rest[i * GROUPS : (i + 1) * GROUPS] for i in range(7))
+    sems = rest[7 * GROUPS : 7 * GROUPS + n_sem]
+    load = rest[7 * GROUPS + n_sem]
+    sems_out, sems_dx = rest[-4:-2], rest[-2:]
+    spot = Spot()
+    for g in range(GROUPS):
+        pltpu.make_async_copy(grads[g], parts[g], load.at[g]).start()
+    greet(spot)
+    places = Spread(spot, out, placed_out, sems_out), Spread(spot, dx, placed_dx, sems_dx)
+    scatter = Scatter(spot, parts, rel_a, rel_b, from_x, from_y, line, final, sems)
+    todo = [(g, t) for g in range(GROUPS) for t in range(LINE)]
+    count = len(todo)
+    for p in places:
+        p.start()
+    for i in range(count + 6):
+        if i < count:
+            g, t = todo[i]
+            if t == 0:
+                pltpu.make_async_copy(grads[g], parts[g], load.at[g]).wait()
+            scatter.first(g, t)
+        if 0 <= i - 1 < count:
+            scatter.second(*todo[i - 1])
+        if 0 <= i - 3 < count:
+            scatter.third(*todo[i - 3])
+        if 0 <= i - 5 < count and todo[i - 5][1] == LINE - 1:
+            scatter.fourth(todo[i - 5][0])
+    for g in range(GROUPS):
+        scatter.fifth(g)
+        pltpu.make_async_copy(final[g], outs[g], load.at[g]).start()
+    for g in range(GROUPS):
+        pltpu.make_async_copy(final[g], outs[g], load.at[g]).wait()
+    scatter.drain()
+    for p in places:
+        p.wait()
+
+
+def scatter_scratch(shapes):
+    def each(f):
+        return [pltpu.VMEM(f(*s), jnp.bfloat16) for s in shapes]
+
+    return (
+        each(lambda n, r, c: (n, r, c))
+        + each(lambda n, r, c: (n, r // 8, c)) * 2
+        + each(lambda n, r, c: (n, r // 4, c)) * 2
+        + each(lambda n, r, c: (n + 1, r // 4, c))
+        + each(lambda n, r, c: (r, c))
+    )
+
+
+def scatter_all(grads, out, dx):
+    placed = jax.ShapeDtypeStruct((4 * out.shape[0], out.shape[1] // LINE), out.dtype)
+    anywhere = pl.BlockSpec(memory_space=pl.ANY)
+    return pl.pallas_call(
+        functools.partial(scatter_kernel, len(Scatter.SEMS)),
+        name="scatter",
+        out_shape=[jax.ShapeDtypeStruct(g.shape[1:], g.dtype) for g in grads] + [placed] * 2,
+        in_specs=[anywhere] * (GROUPS + 2),
+        out_specs=[anywhere] * (GROUPS + 2),
+        scratch_shapes=scatter_scratch([g.shape for g in grads]) + Scatter.SEMS + [pltpu.SemaphoreType.DMA((GROUPS,))] + Spread.SEMS * 2,
+        compiler_params=pltpu.CompilerParams(collective_id=1, has_side_effects=True, vmem_limit_bytes=60 * 2**20),
+    )(*grads, out, dx)
+
+
+def norm_whole(values, gain, offset):
+    mean = jnp.mean(values, 1, keepdims=True)
+    centred = values - mean
+    inverse = lax.rsqrt(jnp.mean(centred * centred, 1, keepdims=True) + norm_eps)
+    unit = centred * inverse
+    return unit * gain + offset, unit, inverse
+
+
+def norm_whole_back(grad, unit, inverse, gain):
+    scaled = grad * gain
+    return inverse * (scaled - jnp.mean(scaled, 1, keepdims=True) - unit * jnp.mean(scaled * unit, 1, keepdims=True))
+
+
+def per_chip(
+    hidden_in, segment_ids, query_weight, query_bias, key_weight, value_weight, value_bias, attn_out_weight,
+    attn_out_bias, norm1_gain, first_norm_offset, inner_weight, inner_bias, outer_weight, outer_bias, norm2_gain,
+    second_norm_offset, cotangent,
+):
+    f32, low = jnp.float32, jnp.bfloat16
+    half = query_weight.shape[1]
+    heads = half // HD
+    row, col = lax.axis_index("row"), lax.axis_index("col")
+    blocks = (attn_out_bias, norm1_gain, first_norm_offset, outer_bias, norm2_gain, second_norm_offset)
+    par = jnp.zeros((16, MODEL_WIDTH // LINE), low).at[:6].set(jnp.stack(blocks))
+    shards = (
+        jnp.concatenate((query_weight, key_weight, value_weight), 1), attn_out_weight, inner_weight, outer_weight,
+    )
+    x, ct, pars, wqkv, wo, wi, wout = gather_all(hidden_in, cotangent, par, shards)
+    bo, g1, b1, bout, g2, b2 = jnp.transpose(pars, (1, 0, 2)).reshape(16, MODEL_WIDTH)[:6].astype(f32)
+    wqkv = wqkv.reshape(MODEL_WIDTH, 3 * half)
+    wi = wi.reshape(MODEL_WIDTH, -1)
+    qkv = product(x, wqkv)
+    q = (qkv[:, :half] + query_bias).astype(low)
+    k = qkv[:, half : 2 * half].astype(low)
+    v = (qkv[:, 2 * half :] + value_bias).astype(low)
+    qh, kh, vh = (t.reshape(SEQ, heads, HD) for t in (q, k, v))
+    mixed, lse = attend_forward((qh, kh, vh, segment_ids[0]))
+    mixed = mixed.reshape(SEQ, half)
+    wo_n = jnp.transpose(wo, (1, 0, 2)).reshape(half, MODEL_WIDTH)
+    wout_n = jnp.transpose(wout, (1, 0, 2)).reshape(-1, MODEL_WIDTH)
+    attn = col_reduce(product(mixed, wo_n)) + bo
+    x_own = lax.dynamic_slice_in_dim(x, col * (SEQ // 2), SEQ // 2, 0).astype(f32)
+    h1, unit1, inv1 = norm_whole(x_own + attn, g1, b1)
+    h1_low = col_gather(h1.astype(low))
+    inner = product(h1_low, wi) + inner_bias
+    cdf = 0.5 * (1.0 + lax.erf(inner * inv_root_two))
+    act = (inner * cdf).astype(low)
+    slope = cdf + inner * jnp.exp(-0.5 * inner * inner) * inv_root_two_pi
+    outer = col_reduce(product(act, wout_n)) + bout
+    out, unit2, inv2 = norm_whole(h1 + outer, g2, b2)
+    dy = ct.astype(f32)
+    g2_grad, b2_grad = jnp.sum(dy * unit2, 0), jnp.sum(dy, 0)
+    dpre2 = norm_whole_back(dy, unit2, inv2, g2)
+    dout2 = dpre2.astype(low)
+    bout_grad = jnp.sum(dout2, 0, dtype=f32)
+    dout2 = col_gather(dout2)
+    wout_grad = over_tokens(act, dout2)
+    dinner = (against(dout2, wout_n) * slope).astype(low)
+    bi_grad = jnp.sum(dinner, 0, dtype=f32)
+    wi_grad = over_tokens(h1_low, dinner)
+    dh1 = dpre2 + col_reduce(against(dinner, wi))
+    g1_grad, b1_grad = jnp.sum(dh1 * unit1, 0), jnp.sum(dh1, 0)
+    dpre1 = norm_whole_back(dh1, unit1, inv1, g1)
+    dattn = dpre1.astype(low)
+    bo_grad = jnp.sum(dattn, 0, dtype=f32)
+    dattn = col_gather(dattn)
+    wo_grad = over_tokens(mixed, dattn)
+    dmixed = against(dattn, wo_n).astype(low)
+    dq, dk, dv = attend_backward((qh, kh, vh, segment_ids[0], dmixed.reshape(SEQ, heads, HD), lse))
+    dq, dk, dv = (t.reshape(SEQ, half) for t in (dq, dk, dv))
+    bq_grad, bv_grad = jnp.sum(dq, 0, dtype=f32), jnp.sum(dv, 0, dtype=f32)
+    dqkv = jnp.concatenate((dq, dk, dv), 1)
+    wqkv_grad = over_tokens(x, dqkv)
+    dx = (dpre1 + col_reduce(against(dqkv, wqkv))).astype(low)
+
+    def blocks_of(w):
+        return jnp.transpose(w.reshape(-1, LINE, MODEL_WIDTH // LINE), (1, 0, 2)).astype(low)
+
+    grads = (
+        wqkv_grad.reshape(LINE, MODEL_WIDTH // LINE, -1).astype(low), blocks_of(wo_grad),
+        wi_grad.reshape(LINE, MODEL_WIDTH // LINE, -1).astype(low), blocks_of(wout_grad),
+    )
+    order = (3, 2, 1, 0)
+    *summed, layer_out, input_grad = scatter_all([grads[i] for i in order], out.astype(low), dx)
+    summed = [summed[order.index(i)].astype(f32) for i in range(GROUPS)]
+    rows_sum = lax.psum((bq_grad, bv_grad, bi_grad), ("dp", "row"))
+    wide = lax.psum((bo_grad, g1_grad, b1_grad, bout_grad, g2_grad, b2_grad), ("dp", "row", "col"))
+    cut = MODEL_WIDTH // LINE
+    bo_g, g1_g, b1_g, bout_g, g2_g, b2_g = (lax.dynamic_slice_in_dim(w, row * cut, cut) for w in wide)
+
+    wq_g, wk_g, wv_g = jnp.split(summed[0], 3, 1)
+    return (
+        layer_out, input_grad, wq_g, rows_sum[0], wk_g, wv_g, rows_sum[1], summed[1], bo_g, g1_g, b1_g,
+        summed[2], rows_sum[2], summed[3], bout_g, g2_g, b2_g,
+    )
+
+
 def solution(mesh):
-    in_specs = (
-        P(("dp", "col"), "row"),
-        P(("dp", "row"), None),
-        P("row", "col"),
-        P("col"),
-        P("row", "col"),
-        P("row", "col"),
-        P("col"),
-        P("col", "row"),
-        P("row"),
-        P("row"),
-        P("row"),
-        P("row", "col"),
-        P("col"),
-        P("col", "row"),
-        P("row"),
-        P("row"),
-        P("row"),
-        P(("dp", "col"), "row"),
-    )
-    out_specs = (
-        P(("dp", "col"), "row"),
-        P(("dp", "col"), "row"),
-        P("row", "col"),
-        P("col"),
-        P("row", "col"),
-        P("row", "col"),
-        P("col"),
-        P("col", "row"),
-        P("row"),
-        P("row"),
-        P("row"),
-        P("row", "col"),
-        P("col"),
-        P("col", "row"),
-        P("row"),
-        P("row"),
-        P("row"),
-    )
-    return jax.shard_map(shards, mesh=mesh, in_specs=in_specs, out_specs=out_specs, check_vma=False)
+    def whole(*args):
+        x, segments, wq = args[0], args[1], args[2]
+        sizes = tuple(mesh.shape[a] for a in ("dp", "row", "col"))
+        fits = sizes == (4, LINE, 2) and segments.shape == (16, SEQ) and wq.shape[0] == MODEL_WIDTH
+        body = per_chip if fits else shards
+        return jax.shard_map(body, mesh=mesh, in_specs=IN_SPECS, out_specs=OUT_SPECS, check_vma=False)(*args)
+
+    return whole

time: 1700 us -> 589 us (0.35)
  waiting for transfers between devices: 1420 us -> 53.2 us
  Pallas kernels: 0 us -> 267 us
  blocking collectives: 67.1 us -> 117 us
  other arithmetic: 67.2 us -> 29.3 us
  matrix products: 102 us -> 66.7 us
    reduce_scatter x6 -> x0, waiting for transfers between devices: 864 us -> none  [the longest x3 640 us: row_reduce(): return lax.psum_scatter(values, 'row', scatter_dimension=0, tiled=True)]
    all_gather x6 -> x0, waiting for transfers between devices: 448 us -> none  [the longest x3 347 us: row_gather(): return lax.all_gather(values, 'row', axis=0, tiled=True)]
    pallas_call x0 -> x2, Pallas kernels: none -> 267 us  [the longest x1 142 us: scatter_all(): pl.pallas_call(functools.partial(scatter_kernel, len(Scatter.SEMS)), name...]
    psum x6 -> x2, blocking collectives: 67.1 us -> 117 us  [the longest x1 76.3 us: per_chip(): rows_sum = lax.psum((bq_grad, bv_grad, bi_grad), ('dp', 'row'))]
    psum x1 -> x0, waiting for transfers between devices: 48.7 us -> none  [shards(): lax.psum(query_weight_grad.astype(jnp.bfloat16), 'dp').astype(jnp.float32)]
    convert_element_type x27 -> x10, other arithmetic: 41.5 us -> 9.82 us  [the longest x3 4.96 us: per_chip(): summed = [summed[order.index(i)].astype(f32) for i in range(GROUPS)]]
    all_gather x4 -> x3, waiting for transfers between devices: 36.5 us -> 24.4 us  [col_gather(): return lax.all_gather(values, 'col', axis=0, tiled=True)]
  transfers between devices with their start and end apart: 21 -> 7, of which waited for: 20 -> 6; matrix products, arithmetic and copies ran while one was open for 5% -> 6% of each run, Pallas kernels for 0% -> 0%
where the time goes in v1:
time: 589 us; the launch traced here: 581 us
  Pallas kernels  267 us (45%)
  blocking collectives  117 us (20%)
  matrix products  66.7 us (11%)
  waiting for transfers between devices  53.2 us (9%)
  local copies, waits for them, and re-layouts  32.9 us (6%)
  other arithmetic  29.3 us (5%)
  between operations  15 us (3%)
    pallas_call x1, Pallas kernels, scatter_all(): pl.pallas_call(functools.partial(scatter_kernel, len(Scatter.SEMS)), name...  142 us
    pallas_call x1, Pallas kernels, gather_all(): pl.pallas_call(functools.partial(gather_kernel, len(tok), len(gat)), name...  125 us
    psum x1, blocking collectives, per_chip(): rows_sum = lax.psum((bq_grad, bv_grad, bi_grad), ('dp', 'row'))  76.3 us
    psum x1, blocking collectives, per_chip(): lax.psum((bo_grad, g1_grad, b1_grad, bout_grad, g2_grad, b2_grad), ('dp',...  40.8 us
    reduce_scatter x4, waiting for transfers between devices, col_reduce(): return lax.psum_scatter(values, 'col', scatter_dimension=0, tiled=True)  28.7 us
    all_gather x3, waiting for transfers between devices, col_gather(): return lax.all_gather(values, 'col', axis=0, tiled=True)  24.4 us
    dot_general x4, matrix products, over_tokens(): lax.dot_general(left, right, (((0,), (0,)), ((), ())), preferred_element_...  18.9 us
    dot_general x4, matrix products, product(): return jnp.dot(left, right, preferred_element_type=jnp.float32)  17.4 us
  transfers between devices with their start and end apart: 7, of which 6 were waited for; matrix products, arithmetic and copies ran while one was open for 6% of the time, Pallas kernels for 0%

profile of v1, /device:TPU:0, one launch (start us, length us, event | category | flops | bytes accessed | tf_op | source)
XLA Modules:
  0.0 581.3 jit_solution(16057526298226317621)
XLA Ops:
  16.2 125.0 %gather.1 = (bf16[512,1024]{1,0:T(8,128)(2,1)}, bf16[256,1024]{1,0:T(8,128)(2,1)}, bf16[4,16,256]{2,1,0:T(8,128)(2,1)}, bf16[4,256,1536]{2,1,0:T(8,128)(2,1)}, b...) custom-call(bf16[1024,256]{1,0:T(8,128)(2,1)} %refs_0_.1, ...), custom_call_target="tpu_custom_call" | custom-call | tf_op jit(solution)/shard_map/gather/pallas_call | solution.py:903
  142.7 4.4 fusion.44
  152.8 2.5 fusion.16
  156.2 2.1 fusion.45
  158.4 6.9 %reduce-scatter.5.cloned.1.call-done = f32[256,1024]{1,0:T(8,128)} async-done(((f32[512,1024]{1,0:T(8,128)}), f32[256,1024]{1,0:T(8,128)}) %reduce-scatter.5.cloned.1.call-update) | async-done | bytes 1048592 | tf_op jit(solution)/shard_map/reduce_scatter | solution.py:49
  168.3 6.3 %copy.51 = bf16[2048,4,256]{0,2,1:T(8,128)(2,1)} copy(bf16[2048,4,256]{2,0,1:T(8,128)(2,1)} %bitcast.83) | data formatting | bytes 8388608 | tf_op jit(solution)/shard_map/transpose | solution.py:1019
  174.6 3.8 all-gather.4.cloned.1.call-done
  178.4 7.3 %multiply_convert_fusion.1 = (bf16[512,2048]{1,0:T(8,128)(2,1)S(1)}, f32[512,2048]{1,0:T(8,128)}) fusion(f32[2048]{0:T(1024)S(1)} %convert_element_type.144, bf16[512,1024]{1,0:T(8,128)(2,1)} %all-gather.4.cloned.1.call-done, bf16[1024,2048]{1,0:T(8,128)(2,1)} %bitcast.116), kind=kOutput, calls=%fused_computation.16 | convolution fusion | flops 2153775104 | bytes 11542528 | tf_op jit(solution)/shard_map/dot_general | solution.py:21
  187.0 3.7 fusion.46
  190.8 10.9 %reduce-scatter.7.cloned.1.call-done = f32[256,1024]{1,0:T(8,128)} async-done(((f32[512,1024]{1,0:T(8,128)}), f32[256,1024]{1,0:T(8,128)}) %reduce-scatter.7.cloned.1.call-update) | async-done | bytes 1048592 | tf_op jit(solution)/shard_map/reduce_scatter | solution.py:49
  203.6 2.4 fusion.25
  205.9 2.2 convert_reduce_fusion.2
  208.2 10.3 %all-gather.6.cloned.1.call-done = bf16[512,1024]{1,0:T(8,128)(2,1)} async-done(((bf16[256,1024]{1,0:T(8,128)(2,1)}), bf16[512,1024]{1,0:T(8,128)(2,1)}) %all-gather.6.cloned.1.call-update) | async-done | bytes 1048592 | tf_op jit(solution)/shard_map/all_gather | solution.py:37
  218.5 6.4 %convert_reduce_fusion = (f32[2048]{0:T(1024)S(1)}, bf16[512,2048]{1,0:T(8,128)(2,1)S(1)}) fusion(f32[512,2048]{1,0:T(8,128)} %get-tuple-element.97, f32[2048]{0:T(1024)S(1)} %convert_element_type.144, bf16[512,1024]{1,0:T(8,128)(2,1)} %all-gather.6.cloned.1.call-done, bf16[2048,1024]{0,1:T(8,128)(2,1)} %bitcast.85), kind=kOutput, calls=%fused_computation.15 | convolution fusion | flops 2161113088 | bytes 11550720 | tf_op jit(solution)/shard_map/dot_general | solution.py:31
  226.2 3.8 fusion.47
  230.1 10.9 %reduce-scatter.9.cloned.1.call-done = f32[256,1024]{1,0:T(8,128)} async-done(((f32[512,1024]{1,0:T(8,128)}), f32[256,1024]{1,0:T(8,128)}) %reduce-scatter.9.cloned.1.call-update) | async-done | bytes 1048592 | tf_op jit(solution)/shard_map/reduce_scatter | solution.py:49
  241.0 2.3 multiply_reduce_fusion.1
  244.9 10.3 %all-gather.8.cloned.1.call-done = bf16[512,1024]{1,0:T(8,128)(2,1)} async-done(((bf16[256,1024]{1,0:T(8,128)(2,1)}), bf16[512,1024]{1,0:T(8,128)(2,1)}) %all-gather.8.cloned.1.call-update) | async-done | bytes 1048592 | tf_op jit(solution)/shard_map/all_gather | solution.py:37
  255.2 2.1 convolution_convert_fusion.4
  257.4 5.4 convert_reduce_fusion.4
  262.8 3.2 multiply_reduce_fusion
  266.0 2.7 multiply_convert_fusion
  271.0 3.3 fusion.29
  274.4 5.9 %convolution_convert_fusion.2 = bf16[2048,1024]{0,1:T(8,128)(2,1)} fusion(bf16[512,2048]{1,0:T(8,128)(2,1)} %copy-done.24, bf16[512,1024]{1,0:T(8,128)(2,1)S(1)} %copy-done.21), kind=kOutput, calls=%fused_computation.23 | convolution fusion | flops 2149580800 | bytes 7340032 | tf_op jit(solution)/shard_map/dot_general | solution.py:25
  280.3 6.4 %copy.52 = bf16[2048,4,256]{2,0,1:T(8,128)(2,1)} copy(bf16[2048,4,256]{0,2,1:T(8,128)(2,1)} %bitcast.87) | data formatting | bytes 8388608 | tf_op jit(solution)/shard_map/convert_element_type | solution.py:1056
  286.7 6.1 %convolution_convert_fusion.1 = bf16[1024,2048]{1,0:T(8,128)(2,1)} fusion(bf16[512,1024]{1,0:T(8,128)(2,1)S(1)} %copy-done.20, bf16[512,2048]{1,0:T(8,128)(2,1)} %copy-done.23), kind=kOutput, calls=%fused_computation.22 | convolution fusion | flops 2149580800 | bytes 7340032 | tf_op jit(solution)/shard_map/dot_general | solution.py:25
  292.8 40.8 %all-reduce.1 = (f32[1024]{0:T(1024)S(1)}, f32[1024]{0:T(1024)S(1)}, f32[1024]{0:T(1024)S(1)}, f32[1024]{0:T(1024)S(1)}, f32[1024]{0:T(1024)S(1)}, /*index=5*/f32[1024]{0:T(1024)S(1)}) all-reduce(f32[1024]{0:T(1024)S(1)} %get-tuple-element.74, ...), channel_id=1, replica_groups=mesh['dp'=4,'row'=4,'col'=2] {'dp','row','col'}, use_global_device_ids=true, to_apply=%region_20.21 | all-reduce | flops 6144 | bytes 49152 | tf_op jit(solution)/shard_map/psum | solution.py:1066
  338.1 76.3 %all-reduce.2 = (f32[512]{0:T(512)}, f32[512]{0:T(512)}, f32[2048]{0:T(1024)}) all-reduce(f32[512]{0:T(512)S(1)} %reduce_sum.186, f32[512]{0:T(512)S(1)} %reduce_sum.188, f32[2048]{0:T(1024)S(1)} %get-tuple-element.104), channel_id=1, replica_groups=mesh['dp'=4,'row'=4,'col'=2] {'dp','row'}, use_global_device_ids=true, to_apply=%region_16.17 | all-reduce | flops 3072 | bytes 24576 | tf_op jit(solution)/shard_map/psum | solution.py:1065
  416.1 5.2 convolution_convert_fusion
  421.3 2.1 add_convert_fusion.refs_5_
  423.5 141.6 %scatter.7 = (bf16[2048,256]{1,0:T(8,128)(2,1)}, bf16[256,2048]{1,0:T(8,128)(2,1)}, bf16[512,256]{1,0:T(8,128)(2,1)}, bf16[256,1536]{1,0:T(8,128)(2,1)}, bf16[10...) custom-call(bf16[4,2048,256]{2,1,0:T(8,128)(2,1)} %bitcast.76, bf16[4,256,2048]{2,1,0:T(8,128)(2,1)} %bitcast.84, ...), custom_call_target="tpu_custom_call" | custom-call | tf_op jit(solution)/shard_map/scatter/pallas_call | solution.py:969
  567.0 2.4 fusion.42
  (124 shorter events, 41.4 us)
Async XLA Ops:
  7.2 158.1 %reduce-scatter.5.cloned.1.call-start = ((), (), s32[]{:S(2)}) async-start(), calls=%async_computation.4 | async-start | bytes 3145728 | tf_op jit(solution)/shard_map/reduce_scatter | solution.py:49
  142.7 12.7 %copy-start.1 = (bf16[512,4,256]{0,2,1:T(8,128)(2,1)}, bf16[512,4,256]{0,2,1:T(8,128)(2,1)S(1)}, u32[]{:S(2)}) copy-start(bf16[512,4,256]{0,2,1:T(8,128)(2,1)S(1)} %copy.50) | copy-start | bytes 3145732
  148.1 3.2 copy-start.5
  149.6 3.2 copy-start
  155.4 2.9 copy-start.16
  155.4 9.9 %copy-start.15 = (bf16[512,1024]{1,0:T(8,128)(2,1)S(1)}, bf16[512,1024]{1,0:T(8,128)(2,1)}, u32[]{:S(2)}) copy-start(bf16[512,1024]{1,0:T(8,128)(2,1)} %get-tuple-element.42) | copy-start | bytes 3145732
  158.2 10.1 %copy-start.17 = (bf16[2048]{0:T(1024)(128)(2,1)S(1)}, bf16[2048]{0:T(1024)(128)(2,1)}, u32[]{:S(2)}) copy-start(bf16[2048]{0:T(1024)(128)(2,1)} %param.32) | copy-start | bytes 12292
  158.3 20.2 %all-gather.4.cloned.1.call-start = ((), (), s32[]{:S(2)}) async-start(), calls=%async_computation.5 | async-start | bytes 1572864 | tf_op jit(solution)/shard_map/all_gather | solution.py:37
  168.1 33.6 %reduce-scatter.7.cloned.1.call-start = ((), (), s32[]{:S(2)}) async-start(), calls=%async_computation.6 | async-start | bytes 3145728 | tf_op jit(solution)/shard_map/reduce_scatter | solution.py:49
  178.4 8.6 %copy-start.3 = (bf16[2048,4,256]{0,2,1:T(8,128)(2,1)S(1)}, bf16[2048,4,256]{0,2,1:T(8,128)(2,1)}, u32[]{:S(2)}) copy-start(bf16[2048,4,256]{0,2,1:T(8,128)(2,1)} %copy.51) | copy-start | bytes 12582916
  190.7 27.8 %all-gather.6.cloned.1.call-start = ((), (), s32[]{:S(2)}) async-start(), calls=%async_computation.7 | async-start | bytes 1572864 | tf_op jit(solution)/shard_map/all_gather | solution.py:37
  208.2 32.8 %reduce-scatter.9.cloned.1.call-start = ((), (), s32[]{:S(2)}) async-start(), calls=%async_computation.8 | async-start | bytes 3145728 | tf_op jit(solution)/shard_map/reduce_scatter | solution.py:49
  218.5 7.7 %copy-start.18 = (bf16[4,256,2048]{2,1,0:T(8,128)(2,1)S(1)}, bf16[4,256,2048]{2,1,0:T(8,128)(2,1)}, u32[]{:S(2)}) copy-start(bf16[4,256,2048]{2,1,0:T(8,128)(2,1)} %get-tuple-element.46) | copy-start | bytes 12582916
  224.9 1.3 copy-start.23
  230.0 25.2 %all-gather.8.cloned.1.call-start = ((), (), s32[]{:S(2)}) async-start(), calls=%async_computation.9 | async-start | bytes 1572864 | tf_op jit(solution)/shard_map/all_gather | solution.py:37
  243.3 11.9 %copy-start.2 = (bf16[512,4,256]{0,2,1:T(8,128)(2,1)S(1)}, bf16[512,4,256]{0,2,1:T(8,128)(2,1)}, u32[]{:S(2)}) copy-start(bf16[512,4,256]{0,2,1:T(8,128)(2,1)} %copy-done.1) | copy-start | bytes 3145732
  244.9 176.5 %reduce-scatter.11.cloned.1.call-start = ((), (), s32[]{:S(2)}) async-start(), calls=%async_computation.10 | async-start | bytes 3145728 | tf_op jit(solution)/shard_map/reduce_scatter | solution.py:49
  255.2 7.6 %slice-start = ((s8[8388608]{0:T(1024)(128)(4,1)}), s8[4194304]{0:T(1024)(128)(4,1)S(1)}, s32[]{:S(2)}) async-start(s8[8388608]{0:T(1024)(128)(4,1)} %bitcast.74), calls=%async_computation.11 | async-start | bytes 8388608
  257.4 5.4 slice-start.1
  257.4 5.4 copy-start.6
  262.8 8.2 %copy-start.22 = (bf16[8,64,512]{2,1,0:T(8,128)(2,1)}, bf16[8,64,512]{2,1,0:T(8,128)(2,1)S(1)}, u32[]{:S(2)}) copy-start(bf16[8,64,512]{2,1,0:T(8,128)(2,1)S(1)} %get-tuple-element.103) | copy-start | bytes 1572868
  268.7 2.3 copy-start.19
  271.0 3.3 copy-start.12
  271.0 3.3 copy-start.21
  280.3 6.4 %copy-start.20 = (bf16[512,1024]{1,0:T(8,128)(2,1)S(1)}, bf16[512,1024]{1,0:T(8,128)(2,1)}, u32[]{:S(2)}) copy-start(bf16[512,1024]{1,0:T(8,128)(2,1)} %all-gather.4.cloned.1.call-done) | copy-start | bytes 3145732
  286.7 50.7 %copy-start.9 = (bf16[512,1024]{1,0:T(8,128)(2,1)S(1)}, bf16[512,1024]{1,0:T(8,128)(2,1)}, u32[]{:S(2)}) copy-start(bf16[512,1024]{1,0:T(8,128)(2,1)} %all-gather.8.cloned.1.call-done) | copy-start | bytes 3145732
  286.7 127.7 %copy-start.11 = (bf16[8,64,512]{2,1,0:T(8,128)(2,1)S(1)}, bf16[8,64,512]{2,1,0:T(8,128)(2,1)}, u32[]{:S(2)}) copy-start(bf16[8,64,512]{2,1,0:T(8,128)(2,1)} %copy-done.10) | copy-start | bytes 1572868
  416.1 5.2 copy-start.4
  565.0 4.3 copy-start.8
  565.0 5.9 %copy-start.7 = (bf16[2048,256]{1,0:T(8,128)(2,1)S(1)}, bf16[2048,256]{1,0:T(8,128)(2,1)}, u32[]{:S(2)}) copy-start(bf16[2048,256]{1,0:T(8,128)(2,1)} %get-tuple-element.54) | copy-start | bytes 3145732
  567.0 5.4 copy-start.14
  569.4 3.8 copy-start.13
  (2 other events, 2.1 us)
Sparse Core Ops, SparseCore 0:
  158.4 6.8 reduce-scatter.4
  168.2 10.1 all-gather.3
  190.8 10.7 reduce-scatter.6
  208.3 10.1 all-gather.5
  230.2 10.7 reduce-scatter.8
  245.0 10.2 all-gather.7
  274.5 10.7 reduce-scatter.10

commit v2 on v1

--- a/solution.py
+++ b/solution.py
@@ -344,14 +344,14 @@
 class Gather:
     SEMS = (
         [pltpu.SemaphoreType.DMA((GROUPS, 2))]
-        + [pltpu.SemaphoreType.DMA((GROUPS,))]
-        + [pltpu.SemaphoreType.DMA((GROUPS, LINE))] * 12
+        + [pltpu.SemaphoreType.DMA((GROUPS, 3))]
+        + [pltpu.SemaphoreType.DMA((GROUPS, LINE))] * 10
     )
 
     def __init__(self, spot, shards, bufs, sems):
         self.spot, self.shards, self.bufs = spot, shards, bufs
-        (self.own_s, self.own_l, self.zs, self.zr, self.xs, self.xr, self.ys, self.yr, self.fas, self.far, self.fbs, self.fbr, *_) = sems
-        self.quarter = [s.shape[0] // 4 for s in shards]
+        (self.own_s, self.own_l, self.zs, self.zr, self.xs, self.xr, self.ys, self.yr, self.fas, self.far, self.fbs, self.fbr) = sems
+        self.quarter = [b.shape[1] // 4 for b in bufs]
 
     def piece(self, g, row, j, half=None):
         q = self.quarter[g]
@@ -361,16 +361,28 @@
         return self.bufs[g].at[row, pl.ds(pl.multiple_of(j * q + half * h, h), h)]
 
     def own_copy(self, g, up):
-        s, q = self.spot, self.quarter[g]
-        src = self.shards[g].at[pl.ds(pl.multiple_of(s.dp * q, q), q)]
+        s = self.spot
+        piece = self.piece(g, s.row, s.dp)
         row = s.row + 1 if up else s.row - 1
-        return remote(src, self.piece(g, s.row, s.dp), self.own_s.at[g, int(up)], self.zr.at[g, s.row], s.at_row(row))
+        return remote(piece, piece, self.own_s.at[g, int(up)], self.zr.at[g, s.row], s.at_row(row))
 
     def local(self, g):
-        return pltpu.make_async_copy(self.shards[g], self.bufs[g].at[self.spot.row], self.own_l.at[g])
+        mine = self.bufs[g].at[self.spot.row]
+        wide = self.shards[g][0].shape[1]
+        return [
+            pltpu.make_async_copy(part, mine.at[:, pl.ds(i * wide, wide)], self.own_l.at[g, i])
+            for i, part in enumerate(self.shards[g])
+        ]
+
+    def load(self):
+        for g in range(GROUPS):
+            for c in self.local(g):
+                c.start()
 
     def start_own(self, g):
         s = self.spot
+        for c in self.local(g):
+            c.wait()
 
         @pl.when(s.row < LINE - 1)
         def _():
@@ -379,8 +391,6 @@
         @pl.when(s.row > 0)
         def _():
             self.own_copy(g, False).start()
-
-        self.local(g).start()
 
     def onward(self, g, n):
         s = self.spot
@@ -419,7 +429,6 @@
             c.start()
 
     def xy_step(self, g, n):
-        x, y = self.across(g, n)
         a, b = self.relays(g, n)
         s = self.spot
         row = s.near[n]
@@ -466,24 +475,15 @@
         pltpu.SemaphoreType.DMA((LINE,)),
     ]
 
-    def __init__(self, spot, x, ct, par, xs, cts, pars, sems):
+    def __init__(self, spot, x, ct, xs, cts, pars, sems):
         self.spot = spot
-        self.x, self.ct, self.par, self.xs, self.cts, self.pars = x, ct, par, xs, cts, pars
+        self.x, self.ct, self.xs, self.cts, self.pars = x, ct, xs, cts, pars
         (self.x_s, self.x_r, self.x_fs, self.x_fr, self.c_s, self.c_r, self.p_s, self.p_r) = sems
         self.seq = x.shape[0] // 2
         self.wide = x.shape[1]
 
     def cols(self, ref, row):
         return ref.at[:, pl.ds(pl.multiple_of(row * self.wide, self.wide), self.wide)]
-
-    def each(self, i, do_remote, do_local, row, here):
-        @pl.when(here)
-        def _():
-            do_local()
-
-        @pl.when(jnp.logical_not(here))
-        def _():
-            do_remote()
 
     def x_copy(self, i, local):
         s = self.spot
@@ -507,9 +507,8 @@
     def par_copy(self, away):
         s = self.spot
         row = lax.rem(s.row + away, LINE)
-        if away == 0:
-            return pltpu.make_async_copy(self.par, self.pars.at[s.row], self.p_r.at[s.row])
-        return remote(self.par, self.pars.at[s.row], self.p_s.at[away], self.p_r.at[s.row], s.at_row(row))
+        mine = self.pars.at[s.row]
+        return remote(mine, mine, self.p_s.at[away], self.p_r.at[s.row], s.at_row(row))
 
     def start_x(self):
         s = self.spot
@@ -525,7 +524,7 @@
                 self.x_copy(i, False).start()
 
     def start_par(self):
-        for away in range(LINE):
+        for away in range(1, LINE):
             self.par_copy(away).start()
 
     def start_ct(self):
@@ -572,7 +571,7 @@
             pltpu.make_async_copy(block, block, self.c_r.at[row]).wait()
 
     def wait_par(self):
-        for row in self.rows():
+        for row in self.spot.near:
             block = self.pars.at[row]
             pltpu.make_async_copy(block, block, self.p_r.at[row]).wait()
 
@@ -605,16 +604,16 @@
 class Scatter:
     SEMS = [pltpu.SemaphoreType.DMA((GROUPS, LINE))] * 14 + [pltpu.SemaphoreType.DMA((GROUPS,))] * 10
 
-    def __init__(self, spot, parts, rel_a, rel_b, from_x, from_y, line, final, sems):
+    def __init__(self, spot, parts, rel_a, rel_b, from_x, from_y, line, stage, final, sems):
         self.spot, self.parts, self.rel_a, self.rel_b = spot, parts, rel_a, rel_b
-        self.from_x, self.from_y, self.line, self.final = from_x, from_y, line, final
+        self.from_x, self.from_y, self.line, self.stage, self.final = from_x, from_y, line, stage, final
         (
             self.ra_s, self.ra_r, self.rb_s, self.rb_r,
             self.xa_s, self.xa_r, self.xb_s, self.xb_r,
             self.ya_s, self.ya_r, self.yb_s, self.yb_r,
             self.z_s, self.z_r,
             self.above_r, self.fx_s, self.fx_r, self.fy_s, self.fy_r,
-            self.ha_s, self.ha_r, self.hb_s, self.hb_r, self.spare,
+            self.ha_s, self.ha_r, self.hb_s, self.hb_r, self.own_s,
         ) = sems
         self.quarter = [p.shape[1] // 4 for p in parts]
         self.order = (spot.near[2], spot.near[1], spot.near[0], spot.row)
@@ -671,6 +670,8 @@
     def first(self, g, t):
         self.send_a(g, t).start()
         self.send_b(g, t).start()
+
+    def direct(self, g, t):
         self.send_xb(g, t).start()
         self.send_ya(g, t).start()
 
@@ -686,17 +687,13 @@
         self.add(g, h, mine, (mine, self.rel_b[g].at[row]))
         self.send_yb(g, t).start()
 
-    def onward(self, g, t):
+    def onward(self, g, t, above=False):
         s, row = self.spot, self.order[t]
         to = jnp.where(row > s.row, s.row + 1, s.row - 1)
         slot = jnp.where(row == s.row - 1, LINE, row)
-        last = row == s.row - 1
         piece = self.part(g, row, s.dp)
-
-        def copy(recv):
-            return remote(piece, self.line[g].at[slot], self.z_s.at[g, row], recv, s.at_row(to))
-
-        return last, copy(self.above_r.at[g]), copy(self.z_r.at[g, row])
+        recv = self.above_r.at[g] if above else self.z_r.at[g, row]
+        return remote(piece, self.line[g].at[slot], self.z_s.at[g, row], recv, s.at_row(to))
 
     def third(self, g, t):
         s, row = self.spot, self.order[t]
@@ -707,11 +704,11 @@
         terms = (mine, self.from_x[g].at[row], self.from_y[g].at[row])
         if t < LINE - 1:
             passed = jnp.logical_or(jnp.logical_and(row > s.row, s.row > 0), jnp.logical_and(row < s.row, s.row < LINE - 1))
-            last, above, along = self.onward(g, t)
+            last = row == s.row - 1
 
             @pl.when(passed)
             def _():
-                along.wait_recv()
+                self.onward(g, t).wait_recv()
                 self.add(g, q, mine, terms + (self.line[g].at[row],))
 
             @pl.when(jnp.logical_not(passed))
@@ -720,14 +717,14 @@
 
             @pl.when(last)
             def _():
-                above.start()
+                self.onward(g, t, True).start()
 
             @pl.when(jnp.logical_not(last))
             def _():
-                along.start()
+                self.onward(g, t).start()
         else:
             below, over = self.line[g].at[s.row], self.line[g].at[LINE]
-            whole = self.fin(g, s.dp)
+            whole = self.stage[g]
 
             def wait_below():
                 remote(below, below, self.z_s.at[g, s.row], self.z_r.at[g, s.row], s.beside_x).wait_recv()
@@ -753,6 +750,7 @@
 
             for c in self.spread(g):
                 c.start()
+            self.settle(g).start()
 
     def fin(self, g, j, half=None):
         q = self.quarter[g]
@@ -764,10 +762,14 @@
     def spread(self, g):
         s = self.spot
         p = self.fin(g, s.dp)
+        mine = self.stage[g]
         return (
-            remote(p, p, self.fx_s.at[g], self.fx_r.at[g], s.beside_x),
-            remote(p, p, self.fy_s.at[g], self.fy_r.at[g], s.beside_y),
+            remote(mine, p, self.fx_s.at[g], self.fx_r.at[g], s.beside_x),
+            remote(mine, p, self.fy_s.at[g], self.fy_r.at[g], s.beside_y),
         )
+
+    def settle(self, g):
+        return pltpu.make_async_copy(self.stage[g], self.fin(g, self.spot.dp), self.own_s.at[g])
 
     def relays(self, g):
         s = self.spot
@@ -801,9 +803,10 @@
                 ):
                     c.wait_send()
                 if t < LINE - 1:
-                    self.onward(g, t)[2].wait_send()
+                    self.onward(g, t).wait_send()
             for c in self.spread(g) + self.relays(g):
                 c.wait_send()
+            self.settle(g).wait()
 
 
 class Spread:
@@ -855,139 +858,737 @@
             self.copy(away).wait_send()
 
 
-def gather_kernel(n_tok, n_gat, *refs):
-    x, ct, par, *rest = refs
-    shards, rest = rest[:GROUPS], rest[GROUPS:]
-    xs, cts, pars, *rest = rest
-    bufs, rest = rest[:GROUPS], rest[GROUPS:]
-    tok_sems, gat_sems = rest[:n_tok], rest[n_tok:]
+F32, LOW = jnp.float32, jnp.bfloat16
+ANYWHERE = pl.BlockSpec(memory_space=pl.ANY)
+IN_VMEM = pl.BlockSpec(memory_space=pltpu.VMEM)
+LANES = 128
+BLOCK = 32
+
+
+def at(start, size):
+    return pl.ds(pl.multiple_of(start * size, size), size)
+
+
+def dot(a, b):
+    return jnp.dot(a, b, preferred_element_type=F32)
+
+
+def dot_t(a, b):
+    return lax.dot_general(a, b, (((1,), (1,)), ((), ())), preferred_element_type=F32)
+
+
+def loop(count, body):
+    def step(i, carry):
+        body(i)
+        return carry
+
+    lax.fori_loop(0, count, step, 0)
+
+
+def head_lanes(half, dtype):
+    lane = lax.broadcasted_iota(jnp.int32, (1, LANES), 1)
+    return jnp.where((lane < HD) == (half == 0), 1.0, 0.0).astype(dtype)
+
+
+def fold(values):
+    return jnp.sum(values.reshape(values.shape[0] // 8, 8, values.shape[1]), 0)
+
+
+def forward_kernel(*refs):
+    it = iter(refs)
+
+    def take(n):
+        return [next(it) for _ in range(n)]
+
+    x, ct, wq, wk, wv, wo_s, wi_s, wout_s = take(8)
+    seg, bq, bv, bi = take(4)
+    small = take(6)
+    out_w = take(GROUPS)
+    o_xt, o_qkv, o_probs, o_mixed_t, o_unit, o_inv, o_h_t, o_slope, o_act_t, o_dpre, o_dout, o_pars, o_out, o_sums = take(14)
+    bufs = take(GROUPS)
+    xs, cts, pars4, pars, qkv, qkv_bias, probs, mask, mixed, part, recv1, recv2 = take(12)
+    unit, inv, h1, h_low, inner, slope, act, act_t, h_t, x_t, mixed_t, dpre, dout, out, sums = take(15)
+    tok_sems, gat_sems = take(len(Tokens.SEMS)), take(len(Gather.SEMS))
+    core_s, core_r, save = take(3)
+
     spot = Spot()
+    gather = Gather(spot, ((wq, wk, wv), (wo_s,), (wi_s,), (wout_s,)), bufs, gat_sems)
+    tokens = Tokens(spot, x, ct, xs, cts, pars4, tok_sems)
+    wqkv, wo, wi, wout = bufs
+    seq, width = xs.shape
+    own = seq // 2
+    half = qkv.shape[1] // 3
+    mine, theirs = spot.col * own, (1 - spot.col) * own
+
+    def rows_of(base, start, size):
+        return pl.ds(pl.multiple_of(base + start * size, size), size)
+
+    gather.load()
+    pars4[spot.row] = jnp.zeros(pars4.shape[1:], F32)
+    for i, p in enumerate(small):
+        pars4[spot.row, pl.ds(i, 1), :] = p[...].astype(F32).reshape(1, -1)
     greet(spot)
-    tokens = Tokens(spot, x, ct, par, xs, cts, pars, tok_sems)
-    gather = Gather(spot, shards, bufs, gat_sems)
+
+    saves = []
+
+    def keep(src, dst):
+        c = pltpu.make_async_copy(src, dst, save.at[len(saves)])
+        c.start()
+        saves.append(c)
+
+    def to_other(n, src, dst):
+        return remote(src, dst, core_s.at[n], core_r.at[n], spot.other_core)
+
+    def make_mask():
+        values = seg[...].astype(F32)
+        for i in range(seq // LANES):
+            down = jnp.broadcast_to(values[:, i * LANES : (i + 1) * LANES], (LANES, LANES)).T
+            for j in range(seq // LANES):
+                across = values[:, j * LANES : (j + 1) * LANES]
+                mask[pl.ds(i * LANES, LANES), pl.ds(j * LANES, LANES)] = jnp.where(down == across, 0.0, -1e30)
+        qkv_bias[:, pl.ds(0, half)] = jnp.broadcast_to(bq[...].astype(F32).reshape(1, half), (8, half))
+        qkv_bias[:, pl.ds(half, half)] = jnp.zeros((8, half), F32)
+        qkv_bias[:, pl.ds(2 * half, half)] = jnp.broadcast_to(bv[...].astype(F32).reshape(1, half), (8, half))
+
+    def spread_pars():
+        for r in range(LINE):
+            pars[:, pl.ds(r * (width // LINE), width // LINE)] = pars4[r]
+
+    def project():
+        def chunk(c):
+            cols = at(c, 256)
+            w = wqkv[:, :, cols].reshape(width, 256)
+            value = (dot(xs[...], w) + qkv_bias[0:1, cols]).astype(LOW).astype(F32)
+            qkv[:, cols] = (value * jnp.where(c < half // 256, 0.125, 1.0)).astype(LOW)
+
+        loop(3 * half // 256, chunk)
+
+    def transpose_x():
+        loop(width // LANES, lambda c: x_t.__setitem__((at(c, LANES), slice(None)), xs[:, at(c, LANES)].T))
+
+    def attend(pair):
+        lanes = pl.ds(pair * LANES, LANES)
+        keys = qkv[:, pl.ds(half + pair * LANES, LANES)]
+        values = qkv[:, pl.ds(2 * half + pair * LANES, LANES)]
+
+        def block(i):
+            rows = at(i, LANES)
+            queries = qkv[rows, lanes]
+            total = None
+            for h in range(2):
+                scores = dot_t(queries * head_lanes(h, LOW), keys) + mask[rows, :]
+                expo = jnp.exp(scores - jnp.max(scores, 1, keepdims=True))
+                p = (expo / jnp.sum(expo, 1, keepdims=True)).astype(LOW)
+                probs[2 * pair + h, rows, :] = p
+                head = dot(p, values) * head_lanes(h, F32)
+                total = head if total is None else total + head
+            mixed[rows, lanes] = total.astype(LOW)
+
+        loop(seq // LANES, block)
+        mixed_t[lanes, :] = mixed[:, lanes].T
+
+    def attn_out(r):
+        part[:, pl.ds(r * 256, 256)] = dot(mixed[...], wo[r])
+
+    def first_norm():
+        def block(i):
+            rows, there = at(i, BLOCK), rows_of(mine, i, BLOCK)
+            value = xs[there, :].astype(F32) + (part[there, :] + recv1[rows, :] + pars[0:1, :])
+            centred = value - jnp.mean(value, 1, keepdims=True)
+            scale = lax.rsqrt(jnp.mean(centred * centred, 1, keepdims=True) + norm_eps)
+            one = centred * scale
+            unit[rows, :] = one
+            inv[rows, :] = jnp.broadcast_to(scale, (BLOCK, LANES))
+            h = one * pars[1:2, :] + pars[2:3, :]
+            h1[rows, :] = h
+            h_low[there, :] = h.astype(LOW)
+
+        loop(own // BLOCK, block)
+
+    def transpose_h():
+        loop(width // LANES, lambda c: h_t.__setitem__((at(c, LANES), slice(None)), h_low[:, at(c, LANES)].T))
+
+    def grow(c):
+        cols = at(c, 256)
+        inner[...] = dot(h_low[...], wi[:, :, cols].reshape(width, 256))
+        bias = bi[cols].astype(F32).reshape(1, 256)
+
+        def block(i):
+            rows = at(i, 64)
+            v = inner[rows, :] + bias
+            cdf = 0.5 * (1.0 + lax.erf(v * inv_root_two))
+            slope[rows, cols] = cdf + v * (jnp.exp(-0.5 * v * v) * inv_root_two_pi)
+            act[rows, cols] = (v * cdf).astype(LOW)
+
+        loop(seq // 64, block)
+        act_t[cols, :] = act[:, cols].T
+
+    def shrink(r):
+        part[:, at(r, 256)] = dot(act[...], wout[r])
+
+    def second_norm():
+        sums[...] = jnp.zeros_like(sums)
+
+        def block(i):
+            rows, there = at(i, BLOCK), rows_of(mine, i, BLOCK)
+            value = h1[rows, :] + (part[there, :] + recv2[rows, :] + pars[3:4, :])
+            centred = value - jnp.mean(value, 1, keepdims=True)
+            scale = lax.rsqrt(jnp.mean(centred * centred, 1, keepdims=True) + norm_eps)
+            one = centred * scale
+            out[rows, :] = (one * pars[4:5, :] + pars[5:6, :]).astype(LOW)
+            dy = cts[rows, :].astype(F32)
+            s = dy * pars[4:5, :]
+            d = scale * (s - jnp.mean(s, 1, keepdims=True) - one * jnp.mean(s * one, 1, keepdims=True))
+            dpre[rows, :] = d
+            d_low = d.astype(LOW)
+            dout[there, :] = d_low
+            sums[0] += fold(d_low.astype(F32))
+            sums[1] += fold(dy * one)
+            sums[2] += fold(dy)
+
+        loop(own // BLOCK, block)
+
+    z = [(g, n) for g in range(GROUPS) for n in range(LINE - 1)]
+    done_z, done_xy = [0], [0]
+
+    def advance(n_z, n_xy):
+        while done_z[0] < n_z or done_xy[0] < n_xy:
+            if done_z[0] < n_z and done_z[0] - done_xy[0] < 3 or done_xy[0] >= n_xy:
+                g, n = z[done_z[0]]
+                if n == 0 and g + 1 < GROUPS:
+                    gather.start_own(g + 1)
+                gather.z_step(g, n)
+                done_z[0] += 1
+            else:
+                gather.xy_step(*z[done_xy[0]])
+                done_xy[0] += 1
+
+    def arrive(g):
+        for n in range(LINE - 1):
+            gather.arrive(g, n)
+
     gather.start_own(0)
     tokens.start_x()
     tokens.start_par()
-    todo = [(g, n) for g in range(GROUPS) for n in range(LINE - 1)]
-    for i, (g, n) in enumerate(todo):
-        if n == 0 and g + 1 < GROUPS:
-            gather.start_own(g + 1)
-        gather.z_step(g, n)
-        if i == 1:
-            tokens.wait_x()
-            tokens.start_ct()
-        if i >= 2:
-            gather.xy_step(*todo[i - 2])
-    for u in todo[-2:]:
-        gather.xy_step(*u)
-    for u in todo:
-        gather.arrive(*u)
-    for g in range(GROUPS):
-        gather.local(g).wait()
+    make_mask()
+    advance(2, 0)
+    tokens.wait_x()
+    advance(3, 1)
+    transpose_x()
+    keep(x_t, o_xt)
+    advance(5, 3)
+    arrive(0)
+    tokens.wait_par()
+    spread_pars()
+    project()
+    keep(wqkv, out_w[0])
+    keep(qkv, o_qkv)
+    keep(pars, o_pars)
+    tokens.start_ct()
+    for pair in range(half // LANES):
+        attend(pair)
+        advance(6 + pair // 2, 4 + pair // 2)
+    keep(probs, o_probs)
+    keep(mixed_t, o_mixed_t)
+    advance(8, 6)
+    arrive(1)
+    keep(wo, out_w[1])
+    for r in range(LINE):
+        attn_out(r)
+    first = to_other(0, part.at[pl.ds(pl.multiple_of(theirs, own), own)], recv1)
+    first.start()
+    advance(9, 7)
+    first.wait_recv()
+    first_norm()
+    pass_h = to_other(1, *[h_low.at[pl.ds(pl.multiple_of(mine, own), own)]] * 2)
+    pass_h.start()
+    keep(unit, o_unit)
+    keep(inv, o_inv)
+    advance(10, 8)
+    pass_h.wait_recv()
+    transpose_h()
+    keep(h_t, o_h_t)
+    advance(11, 9)
+    arrive(2)
+    keep(wi, out_w[2])
+    advance(12, 9)
+    first.wait_send()
+    loop(3, grow)
+    advance(12, 10)
+    loop(3, lambda c: grow(c + 3))
+    advance(12, 11)
+    loop(2, lambda c: grow(c + 6))
+    keep(slope, o_slope)
+    keep(act_t, o_act_t)
     tokens.wait_ct()
-    tokens.wait_par()
+    for n in range(LINE):
+        if n == 0:
+            r = spot.row
+        else:
+            r = spot.near[n - 1]
+            if n == LINE - 1:
+                advance(12, 12)
+            gather.arrive(3, n - 1)
+        shrink(r)
+    keep(wout, out_w[3])
+    second = to_other(2, part.at[pl.ds(pl.multiple_of(theirs, own), own)], recv2)
+    second.start()
+    second.wait_recv()
+    second_norm()
+    pass_d = to_other(3, *[dout.at[pl.ds(pl.multiple_of(mine, own), own)]] * 2)
+    pass_d.start()
+    keep(dpre, o_dpre)
+    keep(out, o_out)
+    keep(sums, o_sums)
+    pass_d.wait_recv()
+    keep(dout, o_dout)
+    second.wait_send()
+    pass_h.wait_send()
+    pass_d.wait_send()
     gather.drain()
     tokens.drain()
-
-
-def gather_all(x, ct, par, shards):
-    tokens, wide = x.shape
-    seq = tokens // 2
-    tok, gat = Tokens.SEMS, Gather.SEMS
-    outs = [
-        jax.ShapeDtypeStruct((seq, LINE * wide), x.dtype),
-        jax.ShapeDtypeStruct((seq // 2, LINE * wide), x.dtype),
-        jax.ShapeDtypeStruct((LINE,) + par.shape, par.dtype),
-    ] + [jax.ShapeDtypeStruct((LINE,) + s.shape, s.dtype) for s in shards]
-    anywhere = pl.BlockSpec(memory_space=pl.ANY)
-    return pl.pallas_call(
-        functools.partial(gather_kernel, len(tok), len(gat)),
-        name="gather",
-        out_shape=outs,
-        in_specs=[anywhere] * (3 + GROUPS),
-        out_specs=[anywhere] * len(outs),
-        scratch_shapes=tok + gat,
-        compiler_params=pltpu.CompilerParams(collective_id=0, has_side_effects=True),
-    )(x, ct, par, *shards)
-
-
-def scatter_kernel(n_sem, *refs):
-    grads, out, dx, rest = refs[:GROUPS], refs[GROUPS], refs[GROUPS + 1], refs[GROUPS + 2 :]
-    outs, placed_out, placed_dx, rest = rest[:GROUPS], rest[GROUPS], rest[GROUPS + 1], rest[GROUPS + 2 :]
-    parts, rel_a, rel_b, from_x, from_y, line, final = (rest[i * GROUPS : (i + 1) * GROUPS] for i in range(7))
-    sems = rest[7 * GROUPS : 7 * GROUPS + n_sem]
-    load = rest[7 * GROUPS + n_sem]
-    sems_out, sems_dx = rest[-4:-2], rest[-2:]
+    for c in saves:
+        c.wait()
+
+
+def forward(x, ct, wq, wk, wv, wo, wi, wout, seg, bq, bv, bi, small):
+    half, hidden = wq.shape[1], wi.shape[1]
+    seq, width = x.shape[0] // 2, MODEL_WIDTH
+    own, heads = seq // 2, half // HD
+    weights = [((LINE, wq.shape[0], 3 * half), LOW), ((LINE,) + wo.shape, LOW), ((LINE,) + wi.shape, LOW), ((LINE,) + wout.shape, LOW)]
+    named = dict(
+        xs=((seq, width), LOW), cts=((own, width), LOW), pars4=((LINE, 8, width // LINE), F32), pars=((8, width), F32),
+        qkv=((seq, 3 * half), LOW), qkv_bias=((8, 3 * half), F32), probs=((heads, seq, seq), LOW), mask=((seq, seq), F32),
+        mixed=((seq, half), LOW), part=((seq, width), F32), recv1=((own, width), F32), recv2=((own, width), F32),
+        unit=((own, width), F32), inv=((own, LANES), F32), h1=((own, width), F32), h_low=((seq, width), LOW),
+        inner=((seq, 256), F32), slope=((seq, hidden), F32), act=((seq, hidden), LOW), act_t=((hidden, seq), LOW),
+        h_t=((width, seq), LOW), x_t=((width, seq), LOW), mixed_t=((half, seq), LOW), dpre=((own, width), F32),
+        dout=((seq, width), LOW), out=((own, width), LOW), sums=((3, 8, width), F32),
+    )
+    saved = ("x_t", "qkv", "probs", "mixed_t", "unit", "inv", "h_t", "slope", "act_t", "dpre", "dout", "pars", "out", "sums")
+    outs = weights + [named[n] for n in saved]
+    res = pl.pallas_call(
+        forward_kernel,
+        name="forward",
+        out_shape=[jax.ShapeDtypeStruct(*o) for o in outs],
+        in_specs=[ANYWHERE] * 8 + [IN_VMEM] * (4 + len(small)),
+        out_specs=[ANYWHERE] * len(outs),
+        scratch_shapes=[pltpu.VMEM(*w) for w in weights]
+        + [pltpu.VMEM(*named[n]) for n in named]
+        + Tokens.SEMS
+        + Gather.SEMS
+        + [pltpu.SemaphoreType.DMA((4,)), pltpu.SemaphoreType.DMA((4,)), pltpu.SemaphoreType.DMA((len(outs),))],
+        compiler_params=pltpu.CompilerParams(collective_id=0, has_side_effects=True, vmem_limit_bytes=60 * 2**20),
+    )(x, ct, wq, wk, wv, wo, wi, wout, seg, bq, bv, bi, *small)
+    return res[:GROUPS], dict(zip(saved, res[GROUPS:]))
+
+
+class Sums:
+    SEMS = [pltpu.SemaphoreType.DMA((3,)), pltpu.SemaphoreType.DMA((3,)), pltpu.SemaphoreType.DMA((LINE,)), pltpu.SemaphoreType.DMA((LINE,))]
+
+    def __init__(self, spot, vec, from_core, with_x, from_x, with_y, from_y, from_line, sems):
+        self.spot, self.vec, self.from_core, self.with_x = spot, vec, from_core, with_x
+        self.from_x, self.with_y, self.from_y, self.from_line = from_x, with_y, from_y, from_line
+        self.s, self.r, self.z_s, self.z_r = sems
+
+    def hop(self, n):
+        s = self.spot
+        src, dst, to = (
+            (self.vec.at[pl.ds(0, 8)], self.from_core, s.other_core),
+            (self.with_x, self.from_x, s.beside_x),
+            (self.with_y, self.from_y, s.beside_y),
+        )[n]
+        return remote(src, dst, self.s.at[n], self.r.at[n], to)
+
+    def line(self, away):
+        s = self.spot
+        row = lax.rem(s.row + away, LINE)
+        return remote(self.from_line.at[s.row], self.from_line.at[s.row], self.z_s.at[away], self.z_r.at[s.row], s.at_row(row))
+
+    def step(self, n):
+        if n == 0:
+            self.hop(0).start()
+        elif n == 1:
+            self.hop(0).wait_recv()
+            self.with_x[pl.ds(0, 8), :] = self.vec[pl.ds(0, 8), :] + self.from_core[...]
+            self.with_x[pl.ds(8, 8), :] = self.vec[pl.ds(8, 8), :]
+            self.hop(1).start()
+        elif n == 2:
+            self.hop(1).wait_recv()
+            self.with_y[...] = self.with_x[...] + self.from_x[...]
+            self.hop(2).start()
+        elif n == 3:
+            self.hop(2).wait_recv()
+            self.from_line[self.spot.row] = self.with_y[...] + self.from_y[...]
+            for away in range(1, LINE):
+                self.line(away).start()
+
+    def total(self):
+        s = self.spot
+        for row in s.near:
+            block = self.from_line.at[row]
+            pltpu.make_async_copy(block, block, self.z_r.at[row]).wait()
+        return self.from_line[0] + self.from_line[1] + self.from_line[2] + self.from_line[3]
+
+    def drain(self):
+        for n in range(3):
+            self.hop(n).wait_send()
+        for away in range(1, LINE):
+            self.line(away).wait_send()
+
+
+SAVED = ("x_t", "qkv", "probs", "mixed_t", "unit", "inv", "h_t", "slope", "act_t", "dpre", "dout", "pars", "out")
+
+
+def backward_kernel(*refs):
+    it = iter(refs)
+
+    def take(n):
+        return [next(it) for _ in range(n)]
+
+    wqkv_h, wo_h, wi_h, wout_h = take(GROUPS)
+    saved = dict(zip(SAVED, take(len(SAVED))))
+    (sums2,) = take(1)
+    final = take(GROUPS)
+    placed_out, placed_dx, o_norms, o_bias = take(4)
+    wo, wi, wout, wst = take(4)
+    parts, rel_a, rel_b, from_x, from_y, line, stage = (take(GROUPS) for _ in range(7))
+    act_t, dout, h_t, dpre, unit, inv, pars, mixed_t, qkv = take(9)
+    slope, probs, ds, dinner, part, recv1, recv2, dattn, dmixed, dqkv, dx = take(11)
+    vecs = take(7)
+    scat_sems, sum_sems = take(len(Scatter.SEMS)), take(len(Sums.SEMS))
+    out_sems, dx_sems = take(2), take(2)
+    core_s, core_r, load, st_sem, sl_sem, pr_sem = take(6)
+
     spot = Spot()
-    for g in range(GROUPS):
-        pltpu.make_async_copy(grads[g], parts[g], load.at[g]).start()
+    scatter = Scatter(spot, parts, rel_a, rel_b, from_x, from_y, line, stage, final, scat_sems)
+    totals = Sums(spot, *vecs, sum_sems)
+    vec = vecs[0]
+    place_out, place_dx = Spread(spot, saved["out"], placed_out, out_sems), Spread(spot, dx, placed_dx, dx_sems)
+    seq, width = dout.shape
+    hidden = dinner.shape[1]
+    half = qkv.shape[1] // 3
+    own = seq // 2
+    cut = width // LINE
+    mine, theirs = spot.col * own, (1 - spot.col) * own
+
+    def rows_of(base, start, size):
+        return pl.ds(pl.multiple_of(base + start * size, size), size)
+
+    fetches = {}
+
+    def fetch(name, src, dst):
+        fetches[name] = pltpu.make_async_copy(src, dst, load.at[len(fetches)])
+        fetches[name].start()
+
+    def ready(*names):
+        for n in names:
+            fetches[n].wait()
+
+    def to_other(n, src, dst):
+        return remote(src, dst, core_s.at[n], core_r.at[n], spot.other_core)
+
+    units = [(g, t) for g in range(GROUPS) for t in range(LINE)]
+    second, third, fourth = [0], [0], [0]
+
+    def serve(n2, n3):
+        while second[0] < n2 or third[0] < n3:
+            if second[0] < n2 and (second[0] - third[0] < 2 or third[0] >= n3):
+                scatter.second(*units[second[0]])
+                second[0] += 1
+            else:
+                scatter.third(*units[third[0]])
+                third[0] += 1
+                while fourth[0] < GROUPS and third[0] >= LINE * (fourth[0] + 1) + 2:
+                    scatter.fourth(fourth[0])
+                    fourth[0] += 1
+
+    def send(g):
+        for t in range(LINE):
+            scatter.first(g, t)
+        for t in range(LINE):
+            scatter.direct(g, t)
+
+    def wout_grad(f):
+        rows = at(f, 512)
+        for r in range(LINE):
+            parts[0][r, rows, :] = dot(act_t[rows, :], dout[:, pl.ds(r * cut, cut)]).astype(LOW)
+
+    def slope_copy(f):
+        slot = lax.rem(f, 2)
+        return pltpu.make_async_copy(saved["slope"].at[:, at(f, 256)], slope.at[slot], sl_sem.at[slot])
+
+    def inner_grad(f):
+        rows = at(f, 256)
+
+        @pl.when(f + 1 < hidden // 256)
+        def _():
+            slope_copy(f + 1).start()
+
+        total = dot_t(dout[:, pl.ds(0, cut)], wout[0, rows, :])
+        for r in range(1, LINE):
+            total += dot_t(dout[:, pl.ds(r * cut, cut)], wout[r, rows, :])
+        slope_copy(f).wait()
+        part[:, pl.ds(0, 256)] = total
+        part[pl.ds(0, 8), pl.ds(256, 256)] = jnp.zeros((8, 256), F32)
+
+        def block(i):
+            here = at(i, 64)
+            d = (part[here, pl.ds(0, 256)] * slope[lax.rem(f, 2), here, :]).astype(LOW)
+            dinner[here, rows] = d
+            part[pl.ds(0, 8), pl.ds(256, 256)] += fold(d.astype(F32))
+
+        loop(seq // 64, block)
+        row, col = f // 4, lax.rem(f, 4)
+        vec[pl.ds(9 + row, 1), at(col, 256)] = jnp.sum(part[pl.ds(0, 8), pl.ds(256, 256)], 0, keepdims=True)
+
+    def hidden_grad(r):
+        part[:, at(r, cut)] = dot_t(dinner[...], wi[r])
+
+    def wi_grad(t):
+        row = scatter.order[t]
+
+        def chunk(n):
+            cols = at(n, 512)
+            parts[1][row, :, cols] = dot(h_t[at(row, cut), :], dinner[:, cols]).astype(LOW)
+
+        loop(hidden // 512, chunk)
+
+    def first_norm_back():
+        part_sums = jnp.zeros((8, width), F32)
+
+        def block(i, carry):
+            b_sum, g_sum, s_sum = carry
+            rows, there = at(i, BLOCK), rows_of(mine, i, BLOCK)
+            dh = dpre[rows, :] + (part[there, :] + recv1[rows, :])
+            one = unit[rows, :]
+            s = dh * pars[1:2, :]
+            scale = inv[rows, :][:, 0:1]
+            d = scale * (s - jnp.mean(s, 1, keepdims=True) - one * jnp.mean(s * one, 1, keepdims=True))
+            dpre[rows, :] = d
+            d_low = d.astype(LOW)
+            dattn[there, :] = d_low
+            return b_sum + fold(d_low.astype(F32)), g_sum + fold(dh * one), s_sum + fold(dh)
+
+        b_sum, g_sum, s_sum = lax.fori_loop(0, own // BLOCK, block, (part_sums, part_sums, part_sums))
+        for i, v in enumerate((b_sum, g_sum, s_sum)):
+            vec[pl.ds(i, 1), :] = jnp.sum(v, 0, keepdims=True)
+
+    def mixed_grad(n):
+        rows = at(n, 256)
+        total = dot_t(dattn[:, pl.ds(0, cut)], wo[0, rows, :])
+        for r in range(1, LINE):
+            total += dot_t(dattn[:, pl.ds(r * cut, cut)], wo[r, rows, :])
+        dmixed[:, rows] = total.astype(LOW)
+
+    def wo_grad(r):
+        parts[2][r] = dot(mixed_t[...], dattn[:, at(r, cut)]).astype(LOW)
+
+    def probs_copy(head):
+        return pltpu.make_async_copy(saved["probs"].at[head], probs.at[head % 4], pr_sem.at[head % 4])
+
+    def attend_back(pair):
+        lanes = pl.ds(pair * LANES, LANES)
+        keys_at, values_at = pl.ds(half + pair * LANES, LANES), pl.ds(2 * half + pair * LANES, LANES)
+        slots = [(2 * pair + h) % 4 for h in range(2)]
+
+        def block(i):
+            rows = at(i, LANES)
+            grad = dmixed[rows, lanes]
+            total = None
+            for h in range(2):
+                dp = dot_t(grad * head_lanes(h, LOW), qkv[:, values_at])
+                p = probs[slots[h], rows, :].astype(F32)
+                d = (p * (dp - jnp.sum(p * dp, 1, keepdims=True))).astype(LOW)
+                ds[h, rows, :] = d
+                head = dot(d, qkv[:, keys_at]) * head_lanes(h, F32)
+                total = head if total is None else total + head
+            dqkv[rows, lanes] = (total * 0.125).astype(LOW)
+
+        loop(seq // LANES, block)
+        queries_t, grad_t = qkv[:, lanes].T, dmixed[:, lanes].T
+        dk = jnp.concatenate([dot(queries_t[h * HD : (h + 1) * HD], ds[h]) for h in range(2)], 0)
+        dqkv[:, keys_at] = dk.astype(LOW).T
+        dv = jnp.concatenate([dot(grad_t[h * HD : (h + 1) * HD], probs[slots[h]]) for h in range(2)], 0)
+        dqkv[:, values_at] = dv.astype(LOW).T
+
+    def qkv_sums():
+        for i, base in enumerate((0, 2 * half)):
+            cols = pl.ds(base, half)
+
+            def block(n, carry):
+                return carry + fold(dqkv[at(n, 64), cols].astype(F32))
+
+            v = lax.fori_loop(0, seq // 64, block, jnp.zeros((8, half), F32))
+            vec[pl.ds(8, 1), pl.ds(i * half, half)] = jnp.sum(v, 0, keepdims=True)
+
+    def wqkv_grad(t):
+        row = scatter.order[t]
+
+        def chunk(n):
+            cols = at(n, 512)
+            parts[3][row, :, cols] = dot(h_t[at(row, cut), :], dqkv[:, cols]).astype(LOW)
+
+        loop(3 * half // 512, chunk)
+
+    def weight_copy(r):
+        return pltpu.make_async_copy(wqkv_h.at[r], wst.at[r % 2], st_sem.at[r % 2])
+
+    def input_grad(r):
+        weight_copy(r).wait()
+        part[:, pl.ds(r * cut, cut)] = dot_t(dqkv[...], wst[r % 2])
+        if r + 2 < LINE:
+            weight_copy(r + 2).start()
+
+    def finish_input():
+        def block(i):
+            rows, there = at(i, BLOCK), rows_of(mine, i, BLOCK)
+            dx[rows, :] = (dpre[rows, :] + (part[there, :] + recv2[rows, :])).astype(LOW)
+
+        loop(own // BLOCK, block)
+
+    their_half = part.at[pl.ds(pl.multiple_of(theirs, own), own)]
+    my_rows = pl.ds(pl.multiple_of(mine, own), own)
+
+    fetch("dout", saved["dout"], dout)
+    fetch("act_t", saved["act_t"], act_t)
     greet(spot)
-    places = Spread(spot, out, placed_out, sems_out), Spread(spot, dx, placed_dx, sems_dx)
-    scatter = Scatter(spot, parts, rel_a, rel_b, from_x, from_y, line, final, sems)
-    todo = [(g, t) for g in range(GROUPS) for t in range(LINE)]
-    count = len(todo)
-    for p in places:
-        p.start()
-    for i in range(count + 6):
-        if i < count:
-            g, t = todo[i]
-            if t == 0:
-                pltpu.make_async_copy(grads[g], parts[g], load.at[g]).wait()
-            scatter.first(g, t)
-        if 0 <= i - 1 < count:
-            scatter.second(*todo[i - 1])
-        if 0 <= i - 3 < count:
-            scatter.third(*todo[i - 3])
-        if 0 <= i - 5 < count and todo[i - 5][1] == LINE - 1:
-            scatter.fourth(todo[i - 5][0])
+    place_out.start()
+    ready("dout", "act_t")
+    fetch("wout", wout_h, wout)
+    slope_copy(0).start()
+    loop(hidden // 512, wout_grad)
+    send(0)
+    fetch("wi", wi_h, wi)
+    fetch("h_t", saved["h_t"], h_t)
+    for name, dst in (("dpre", dpre), ("unit", unit), ("inv", inv), ("pars", pars)):
+        fetch(name, saved[name], dst)
+    fetch("wo", wo_h, wo)
+    fetch("mixed_t", saved["mixed_t"], mixed_t)
+    fetch("qkv", saved["qkv"], qkv)
+    for head in range(4):
+        probs_copy(head).start()
+    weight_copy(0).start()
+    weight_copy(1).start()
+    vec[...] = jnp.zeros_like(vec)
+    for i in range(3):
+        vec[pl.ds(3 + i, 1), :] = jnp.sum(sums2[i], 0, keepdims=True)
+    ready("wout")
+    loop(hidden // 256, inner_grad)
+    ready("wi", "h_t")
+    loop(LINE, hidden_grad)
+    swap1 = to_other(0, their_half, recv1)
+    swap1.start()
+    serve(1, 0)
+    for t in range(LINE):
+        wi_grad(t)
+    send(1)
+    fetch("x_t", saved["x_t"], h_t)
+    serve(2, 0)
+    ready("dpre", "unit", "inv", "pars")
+    swap1.wait_recv()
+    first_norm_back()
+    pass_d = to_other(1, dattn.at[my_rows], dattn.at[my_rows])
+    pass_d.start()
+    serve(4, 1)
+    ready("wo", "mixed_t", "qkv")
+    pass_d.wait_recv()
+    loop(half // 256, mixed_grad)
+    loop(LINE, wo_grad)
+    send(2)
+    for pair in range(half // LANES):
+        for h in range(2):
+            probs_copy(2 * pair + h).wait()
+        attend_back(pair)
+        for h in range(2):
+            if 2 * pair + h + 4 < half // HD:
+                probs_copy(2 * pair + h + 4).start()
+        serve(4 + (pair + 1) // 2, 2 + pair // 2)
+    ready("x_t")
+    for t in range(LINE):
+        wqkv_grad(t)
+    send(3)
+    serve(6, 4)
+    swap1.wait_send()
+    for r in range(LINE):
+        input_grad(r)
+    swap2 = to_other(2, their_half, recv2)
+    swap2.start()
+    qkv_sums()
+    totals.step(0)
+    serve(7, 5)
+    swap2.wait_recv()
+    finish_input()
+    place_dx.start()
+    for n in range(1, 4):
+        totals.step(n)
+        serve(7 + n, 5 + n)
+    serve(len(units), len(units))
+    whole = totals.total()
+    totals.drain()
+    for i in range(8):
+        o_bias[pl.ds(i, 1), :] = whole[8 + i : 9 + i, :]
+    vecs[-1][0] = whole
+    o_norms[...] = vecs[-1][0, pl.ds(0, 8), at(spot.row, cut)]
+    while fourth[0] < GROUPS:
+        scatter.fourth(fourth[0])
+        fourth[0] += 1
     for g in range(GROUPS):
         scatter.fifth(g)
-        pltpu.make_async_copy(final[g], outs[g], load.at[g]).start()
-    for g in range(GROUPS):
-        pltpu.make_async_copy(final[g], outs[g], load.at[g]).wait()
     scatter.drain()
-    for p in places:
-        p.wait()
-
-
-def scatter_scratch(shapes):
+    for c in (swap2, pass_d):
+        c.wait_send()
+    place_out.wait()
+    place_dx.wait()
+
+
+def backward(weights, saved):
+    wqkv, wo, wi, wout = weights
+    shapes = [w.shape for w in (wout, wi, wo, wqkv)]
+    seq, width = saved["dout"].shape
+    half, hidden, own = wo.shape[1], wi.shape[2], seq // 2
+    cut = width // LINE
+
     def each(f):
-        return [pltpu.VMEM(f(*s), jnp.bfloat16) for s in shapes]
-
-    return (
-        each(lambda n, r, c: (n, r, c))
+        return [pltpu.VMEM(f(*s), LOW) for s in shapes]
+
+    def like(name):
+        return pltpu.VMEM(saved[name].shape, saved[name].dtype)
+
+    placed = jax.ShapeDtypeStruct((2 * seq, cut), LOW)
+    scratch = (
+        [pltpu.VMEM(w.shape, LOW) for w in (wo, wi, wout)]
+        + [pltpu.VMEM((2,) + wqkv.shape[1:], LOW)]
+        + each(lambda n, r, c: (n, r, c))
         + each(lambda n, r, c: (n, r // 8, c)) * 2
         + each(lambda n, r, c: (n, r // 4, c)) * 2
         + each(lambda n, r, c: (n + 1, r // 4, c))
-        + each(lambda n, r, c: (r, c))
-    )
-
-
-def scatter_all(grads, out, dx):
-    placed = jax.ShapeDtypeStruct((4 * out.shape[0], out.shape[1] // LINE), out.dtype)
-    anywhere = pl.BlockSpec(memory_space=pl.ANY)
-    return pl.pallas_call(
-        functools.partial(scatter_kernel, len(Scatter.SEMS)),
-        name="scatter",
-        out_shape=[jax.ShapeDtypeStruct(g.shape[1:], g.dtype) for g in grads] + [placed] * 2,
-        in_specs=[anywhere] * (GROUPS + 2),
-        out_specs=[anywhere] * (GROUPS + 2),
-        scratch_shapes=scatter_scratch([g.shape for g in grads]) + Scatter.SEMS + [pltpu.SemaphoreType.DMA((GROUPS,))] + Spread.SEMS * 2,
-        compiler_params=pltpu.CompilerParams(collective_id=1, has_side_effects=True, vmem_limit_bytes=60 * 2**20),
-    )(*grads, out, dx)
-
-
-def norm_whole(values, gain, offset):
-    mean = jnp.mean(values, 1, keepdims=True)
-    centred = values - mean
-    inverse = lax.rsqrt(jnp.mean(centred * centred, 1, keepdims=True) + norm_eps)
-    unit = centred * inverse
-    return unit * gain + offset, unit, inverse
-
-
-def norm_whole_back(grad, unit, inverse, gain):
-    scaled = grad * gain
-    return inverse * (scaled - jnp.mean(scaled, 1, keepdims=True) - unit * jnp.mean(scaled * unit, 1, keepdims=True))
+        + each(lambda n, r, c: (r // 4, c))
+        + [like(n) for n in ("act_t", "dout", "h_t", "dpre", "unit", "inv", "pars", "mixed_t", "qkv")]
+        + [
+            pltpu.VMEM((2, seq, 256), F32), pltpu.VMEM((4, seq, seq), LOW), pltpu.VMEM((2, seq, seq), LOW),
+            pltpu.VMEM((seq, hidden), LOW), pltpu.VMEM((seq, width), F32), pltpu.VMEM((own, width), F32),
+            pltpu.VMEM((own, width), F32), pltpu.VMEM((seq, width), LOW), pltpu.VMEM((seq, half), LOW),
+            pltpu.VMEM((seq, 3 * half), LOW), pltpu.VMEM((own, width), LOW),
+        ]
+        + [pltpu.VMEM(s, F32) for s in ((16, width), (8, width)) + ((16, width),) * 4 + ((LINE, 16, width),)]
+        + Scatter.SEMS
+        + Sums.SEMS
+        + Spread.SEMS * 2
+        + [pltpu.SemaphoreType.DMA((n,)) for n in (3, 3, 16, 2, 2, 4)]
+    )
+    res = pl.pallas_call(
+        backward_kernel,
+        name="backward",
+        out_shape=[jax.ShapeDtypeStruct(s[1:], LOW) for s in shapes]
+        + [placed] * 2
+        + [jax.ShapeDtypeStruct((8, cut), F32), jax.ShapeDtypeStruct((8, width), F32)],
+        in_specs=[ANYWHERE] * (GROUPS + len(SAVED)) + [IN_VMEM],
+        out_specs=[ANYWHERE] * (GROUPS + 2) + [IN_VMEM] * 2,
+        scratch_shapes=scratch,
+        compiler_params=pltpu.CompilerParams(collective_id=1, has_side_effects=True, vmem_limit_bytes=63 * 2**20),
+    )(*weights, *[saved[n] for n in SAVED], saved["sums"])
+    return res
 
 
 def per_chip(
@@ -995,88 +1596,23 @@
     attn_out_bias, norm1_gain, first_norm_offset, inner_weight, inner_bias, outer_weight, outer_bias, norm2_gain,
     second_norm_offset, cotangent,
 ):
-    f32, low = jnp.float32, jnp.bfloat16
     half = query_weight.shape[1]
-    heads = half // HD
-    row, col = lax.axis_index("row"), lax.axis_index("col")
-    blocks = (attn_out_bias, norm1_gain, first_norm_offset, outer_bias, norm2_gain, second_norm_offset)
-    par = jnp.zeros((16, MODEL_WIDTH // LINE), low).at[:6].set(jnp.stack(blocks))
-    shards = (
-        jnp.concatenate((query_weight, key_weight, value_weight), 1), attn_out_weight, inner_weight, outer_weight,
-    )
-    x, ct, pars, wqkv, wo, wi, wout = gather_all(hidden_in, cotangent, par, shards)
-    bo, g1, b1, bout, g2, b2 = jnp.transpose(pars, (1, 0, 2)).reshape(16, MODEL_WIDTH)[:6].astype(f32)
-    wqkv = wqkv.reshape(MODEL_WIDTH, 3 * half)
-    wi = wi.reshape(MODEL_WIDTH, -1)
-    qkv = product(x, wqkv)
-    q = (qkv[:, :half] + query_bias).astype(low)
-    k = qkv[:, half : 2 * half].astype(low)
-    v = (qkv[:, 2 * half :] + value_bias).astype(low)
-    qh, kh, vh = (t.reshape(SEQ, heads, HD) for t in (q, k, v))
-    mixed, lse = attend_forward((qh, kh, vh, segment_ids[0]))
-    mixed = mixed.reshape(SEQ, half)
-    wo_n = jnp.transpose(wo, (1, 0, 2)).reshape(half, MODEL_WIDTH)
-    wout_n = jnp.transpose(wout, (1, 0, 2)).reshape(-1, MODEL_WIDTH)
-    attn = col_reduce(product(mixed, wo_n)) + bo
-    x_own = lax.dynamic_slice_in_dim(x, col * (SEQ // 2), SEQ // 2, 0).astype(f32)
-    h1, unit1, inv1 = norm_whole(x_own + attn, g1, b1)
-    h1_low = col_gather(h1.astype(low))
-    inner = product(h1_low, wi) + inner_bias
-    cdf = 0.5 * (1.0 + lax.erf(inner * inv_root_two))
-    act = (inner * cdf).astype(low)
-    slope = cdf + inner * jnp.exp(-0.5 * inner * inner) * inv_root_two_pi
-    outer = col_reduce(product(act, wout_n)) + bout
-    out, unit2, inv2 = norm_whole(h1 + outer, g2, b2)
-    dy = ct.astype(f32)
-    g2_grad, b2_grad = jnp.sum(dy * unit2, 0), jnp.sum(dy, 0)
-    dpre2 = norm_whole_back(dy, unit2, inv2, g2)
-    dout2 = dpre2.astype(low)
-    bout_grad = jnp.sum(dout2, 0, dtype=f32)
-    dout2 = col_gather(dout2)
-    wout_grad = over_tokens(act, dout2)
-    dinner = (against(dout2, wout_n) * slope).astype(low)
-    bi_grad = jnp.sum(dinner, 0, dtype=f32)
-    wi_grad = over_tokens(h1_low, dinner)
-    dh1 = dpre2 + col_reduce(against(dinner, wi))
-    g1_grad, b1_grad = jnp.sum(dh1 * unit1, 0), jnp.sum(dh1, 0)
-    dpre1 = norm_whole_back(dh1, unit1, inv1, g1)
-    dattn = dpre1.astype(low)
-    bo_grad = jnp.sum(dattn, 0, dtype=f32)
-    dattn = col_gather(dattn)
-    wo_grad = over_tokens(mixed, dattn)
-    dmixed = against(dattn, wo_n).astype(low)
-    dq, dk, dv = attend_backward((qh, kh, vh, segment_ids[0], dmixed.reshape(SEQ, heads, HD), lse))
-    dq, dk, dv = (t.reshape(SEQ, half) for t in (dq, dk, dv))
-    bq_grad, bv_grad = jnp.sum(dq, 0, dtype=f32), jnp.sum(dv, 0, dtype=f32)
-    dqkv = jnp.concatenate((dq, dk, dv), 1)
-    wqkv_grad = over_tokens(x, dqkv)
-    dx = (dpre1 + col_reduce(against(dqkv, wqkv))).astype(low)
-
-    def blocks_of(w):
-        return jnp.transpose(w.reshape(-1, LINE, MODEL_WIDTH // LINE), (1, 0, 2)).astype(low)
-
-    grads = (
-        wqkv_grad.reshape(LINE, MODEL_WIDTH // LINE, -1).astype(low), blocks_of(wo_grad),
-        wi_grad.reshape(LINE, MODEL_WIDTH // LINE, -1).astype(low), blocks_of(wout_grad),
-    )
-    order = (3, 2, 1, 0)
-    *summed, layer_out, input_grad = scatter_all([grads[i] for i in order], out.astype(low), dx)
-    summed = [summed[order.index(i)].astype(f32) for i in range(GROUPS)]
-    rows_sum = lax.psum((bq_grad, bv_grad, bi_grad), ("dp", "row"))
-    wide = lax.psum((bo_grad, g1_grad, b1_grad, bout_grad, g2_grad, b2_grad), ("dp", "row", "col"))
-    cut = MODEL_WIDTH // LINE
-    bo_g, g1_g, b1_g, bout_g, g2_g, b2_g = (lax.dynamic_slice_in_dim(w, row * cut, cut) for w in wide)
-
-    wq_g, wk_g, wv_g = jnp.split(summed[0], 3, 1)
+    small = (attn_out_bias, norm1_gain, first_norm_offset, outer_bias, norm2_gain, second_norm_offset)
+    weights, saved = forward(
+        hidden_in, cotangent, query_weight, key_weight, value_weight, attn_out_weight, inner_weight, outer_weight,
+        segment_ids, query_bias, value_bias, inner_bias, small,
+    )
+    wout, wi, wo, wqkv, layer_out, input_grad, norms, biases = backward(weights, saved)
+    wq, wk, wv = jnp.split(wqkv.astype(F32), 3, 1)
     return (
-        layer_out, input_grad, wq_g, rows_sum[0], wk_g, wv_g, rows_sum[1], summed[1], bo_g, g1_g, b1_g,
-        summed[2], rows_sum[2], summed[3], bout_g, g2_g, b2_g,
+        layer_out, input_grad, wq, biases[0, :half], wk, wv, biases[0, half:], wo.astype(F32), norms[0], norms[1],
+        norms[2], wi.astype(F32), biases[1:3].reshape(-1), wout.astype(F32), norms[3], norms[4], norms[5],
     )
 
 
 def solution(mesh):
     def whole(*args):
-        x, segments, wq = args[0], args[1], args[2]
+        segments, wq = args[1], args[2]
         sizes = tuple(mesh.shape[a] for a in ("dp", "row", "col"))
         fits = sizes == (4, LINE, 2) and segments.shape == (16, SEQ) and wq.shape[0] == MODEL_WIDTH
         body = per_chip if fits else shards

time: 589 us -> 305 us (0.52); the launches traced: 581 us -> 305 us
  blocking collectives: 117 us -> 0 us
  matrix products: 66.7 us -> 0 us
  waiting for transfers between devices: 53.2 us -> 0 us
  local copies, waits for them, and re-layouts: 32.9 us -> 8.28 us
  other arithmetic: 29.3 us -> 4.81 us
  Pallas kernels: 267 us -> 291 us
  between operations: 15 us -> 0.7 us
    psum x2 -> x0, blocking collectives: 117 us -> none  [the longest x1 76.3 us: per_chip(): rows_sum = lax.psum((bq_grad, bv_grad, bi_grad), ('dp', 'row'))]
    dot_general x18 -> x0, matrix products: 66.7 us -> none  [the longest x4 18.9 us: over_tokens(): lax.dot_general(left, right, (((0,), (0,)), ((), ())), preferred_element_...]
    reduce_scatter x4 -> x0, waiting for transfers between devices: 28.7 us -> none  [col_reduce(): return lax.psum_scatter(values, 'col', scatter_dimension=0, tiled=True)]
    all_gather x3 -> x0, waiting for transfers between devices: 24.4 us -> none  [col_gather(): return lax.all_gather(values, 'col', axis=0, tiled=True)]
    pallas_call x2, Pallas kernels: 267 us -> 291 us  [the longest x1 163 us: backward(): pl.pallas_call(backward_kernel, name='backward', out_shape=[jax.ShapeDtyp...]
    reduce_sum x9 -> x0, other arithmetic: 13.7 us -> none  [the longest x2 3.07 us: norm_whole(): mean = jnp.mean(values, 1, keepdims=True)]
    transpose x2 -> x0, local copies, waits for them, and re-layouts: 7.8 us -> none  [the longest x1 6.3 us: per_chip(): wout_n = jnp.transpose(wout, (1, 0, 2)).reshape(-1, MODEL_WIDTH)]
    convert_element_type x11 -> x3, other arithmetic: 12.5 us -> 4.81 us  [the longest x1 1.78 us: per_chip(): wo.astype(F32)]
  transfers between devices with their start and end apart: 7 -> 0, of which waited for: 6 -> 0; matrix products, arithmetic and copies ran while one was open for 6% -> 0% of each run, Pallas kernels for 0% -> 0%
where the time goes in v2:
time: 305 us
  Pallas kernels  291 us (95%)
  local copies, waits for them, and re-layouts  8.28 us (3%)
  other arithmetic  4.81 us (2%)
    pallas_call x1, Pallas kernels, backward(): pl.pallas_call(backward_kernel, name='backward', out_shape=[jax.ShapeDtyp...  163 us
    pallas_call x1, Pallas kernels, forward(): pl.pallas_call(forward_kernel, name='forward', out_shape=[jax.ShapeDtypeS...  128 us

profile of v2, /device:TPU:0, one launch (start us, length us, event | category | flops | bytes accessed | tf_op | source)
XLA Modules:
  0.0 304.6 jit_solution(2528211463147778864)
XLA Ops:
  0.7 127.7 %forward.1 = (bf16[4,256,1536]{2,1,0:T(8,128)(2,1)}, bf16[4,512,256]{2,1,0:T(8,128)(2,1)}, bf16[4,256,2048]{2,1,0:T(8,128)(2,1)}, bf16[4,2048,256]{2,1,0:T(8,128...) custom-call(bf16[1024,256]{1,0:T(8,128)(2,1)} %refs_0_.1, ...), custom_call_target="tpu_custom_call" | custom-call | tf_op jit(solution)/shard_map/forward/pallas_call | solution.py:1170
  128.4 163.1 %backward.1 = (bf16[2048,256]{1,0:T(8,128)(2,1)}, bf16[256,2048]{1,0:T(8,128)(2,1)}, bf16[512,256]{1,0:T(8,128)(2,1)}, bf16[256,1536]{1,0:T(8,128)(2,1)}, bf16[1...) custom-call(bf16[4,256,1536]{2,1,0:T(8,128)(2,1)} %get-tuple-element.43.refs_0_, ...), custom_call_target="tpu_custom_call" | custom-call | tf_op jit(solution)/shard_map/backward/pallas_call | solution.py:1580
  291.5 0.0 copy-start.1
  291.5 1.4 fusion.1
  292.9 0.8 slice_bitcast_fusion
  293.6 0.6 copy.37
  294.2 1.5 fusion.2
  295.7 1.8 convert_element_type.13
  297.5 0.0 copy-start
  297.5 2.4 fusion
  299.9 0.0 copy-done.1
  299.9 0.0 copy-start.3
  299.9 0.0 copy-start.2
  299.9 1.6 convert_element_type.14
  301.5 0.0 copy-done
  301.5 1.5 convert_element_type.15
  303.0 0.0 copy-done.3
  303.0 0.8 copy.40
  303.8 0.0 copy-done.2
  303.8 0.8 copy.41
Async XLA Ops:
  291.5 8.5 %copy-start.1 = (bf16[256,2048]{1,0:T(8,128)(2,1)S(1)}, bf16[256,2048]{1,0:T(8,128)(2,1)}, u32[]{:S(2)}) copy-start(bf16[256,2048]{1,0:T(8,128)(2,1)} %get-tuple-element.67) | copy-start | bytes 3145732
  297.5 4.0 %copy-start = (bf16[2048,256]{1,0:T(8,128)(2,1)S(1)}, bf16[2048,256]{1,0:T(8,128)(2,1)}, u32[]{:S(2)}) copy-start(bf16[2048,256]{1,0:T(8,128)(2,1)} %get-tuple-element.68) | copy-start | bytes 3145732
  299.9 3.0 %copy-start.3 = (bf16[1024,256]{1,0:T(8,128)(2,1)S(1)}, bf16[1024,256]{1,0:T(8,128)(2,1)}, u32[]{:S(2)}) copy-start(bf16[1024,256]{1,0:T(8,128)(2,1)} %get-tuple-element.97) | copy-start | bytes 1572868
  299.9 3.8 %copy-start.2 = (bf16[1024,256]{1,0:T(8,128)(2,1)S(1)}, bf16[1024,256]{1,0:T(8,128)(2,1)}, u32[]{:S(2)}) copy-start(bf16[1024,256]{1,0:T(8,128)(2,1)} %get-tuple-element.98) | copy-start | bytes 1572868

commit v3 on v2

--- a/solution.py
+++ b/solution.py
@@ -297,6 +297,10 @@
 MESH = pl.DeviceIdType.MESH
 LINE = 4
 GROUPS = 4
+GATHERED = ((1, 0, 8), (0, 0, 8), (2, 0, 4), (2, 4, 4), (3, 0, 4), (3, 4, 4))
+SCATTERED = (
+    (0, 0, 4, True), (0, 4, 4, False), (1, 0, 8, False), (3, 0, 4, False), (3, 4, 4, False), (2, 0, 8, False),
+)
 
 
 class Spot:
@@ -343,22 +347,23 @@
 
 class Gather:
     SEMS = (
-        [pltpu.SemaphoreType.DMA((GROUPS, 2))]
+        [pltpu.SemaphoreType.DMA((len(GATHERED), 2))]
         + [pltpu.SemaphoreType.DMA((GROUPS, 3))]
-        + [pltpu.SemaphoreType.DMA((GROUPS, LINE))] * 10
+        + [pltpu.SemaphoreType.DMA((len(GATHERED), LINE))] * 10
     )
 
     def __init__(self, spot, shards, bufs, sems):
         self.spot, self.shards, self.bufs = spot, shards, bufs
         (self.own_s, self.own_l, self.zs, self.zr, self.xs, self.xr, self.ys, self.yr, self.fas, self.far, self.fbs, self.fbr) = sems
-        self.quarter = [b.shape[1] // 4 for b in bufs]
+        self.loaded = set()
 
     def piece(self, g, row, j, half=None):
-        q = self.quarter[g]
-        if half is None:
-            return self.bufs[g].at[row, pl.ds(pl.multiple_of(j * q, q), q)]
-        h = q // 2
-        return self.bufs[g].at[row, pl.ds(pl.multiple_of(j * q + half * h, h), h)]
+        which, first, count = GATHERED[g]
+        eighth = self.bufs[which].shape[1] // 8
+        q = eighth * count // 4
+        size = q if half is None else q // 2
+        start = first * eighth + j * q + (0 if half is None else half * size)
+        return self.bufs[which].at[row, pl.ds(pl.multiple_of(start, size), size)]
 
     def own_copy(self, g, up):
         s = self.spot
@@ -375,14 +380,17 @@
         ]
 
     def load(self):
-        for g in range(GROUPS):
+        for g in (1, 0, 2, 3):
             for c in self.local(g):
                 c.start()
 
     def start_own(self, g):
         s = self.spot
-        for c in self.local(g):
-            c.wait()
+        which = GATHERED[g][0]
+        if which not in self.loaded:
+            self.loaded.add(which)
+            for c in self.local(which):
+                c.wait()
 
         @pl.when(s.row < LINE - 1)
         def _():
@@ -428,15 +436,19 @@
         for c in self.across(g, n):
             c.start()
 
-    def xy_step(self, g, n):
-        a, b = self.relays(g, n)
+    def x_step(self, g, n):
         s = self.spot
         row = s.near[n]
-        px, py = self.piece(g, row, s.dp_x), self.piece(g, row, s.dp_y)
-        remote(px, px, self.xs.at[g, row], self.xr.at[g, row], s.beside_x).wait_recv()
-        b.start()
-        remote(py, py, self.ys.at[g, row], self.yr.at[g, row], s.beside_y).wait_recv()
-        a.start()
+        p = self.piece(g, row, s.dp_x)
+        remote(p, p, self.xs.at[g, row], self.xr.at[g, row], s.beside_x).wait_recv()
+        self.relays(g, n)[1].start()
+
+    def y_step(self, g, n):
+        s = self.spot
+        row = s.near[n]
+        p = self.piece(g, row, s.dp_y)
+        remote(p, p, self.ys.at[g, row], self.yr.at[g, row], s.beside_y).wait_recv()
+        self.relays(g, n)[0].start()
 
     def arrive(self, g, n):
         s = self.spot
@@ -447,7 +459,7 @@
 
     def drain(self):
         s = self.spot
-        for g in range(GROUPS):
+        for g in range(len(GATHERED)):
 
             @pl.when(s.row < LINE - 1)
             def _():
@@ -559,6 +571,9 @@
                 pltpu.make_async_copy(block, block, self.x_r.at[row]).wait()
                 self.relay(row).start()
 
+    def wait_relayed(self):
+        s = self.spot
+        first = s.row // 2 == s.col
         for row in self.rows():
 
             @pl.when(jnp.logical_not(first))
@@ -602,7 +617,11 @@
 
 
 class Scatter:
-    SEMS = [pltpu.SemaphoreType.DMA((GROUPS, LINE))] * 14 + [pltpu.SemaphoreType.DMA((GROUPS,))] * 10
+    SEMS = [pltpu.SemaphoreType.DMA((len(SCATTERED), LINE))] * 14 + [pltpu.SemaphoreType.DMA((len(SCATTERED),))] * 10
+
+    @staticmethod
+    def sizes(shapes):
+        return [(shapes[b][1] // 8 * n, shapes[b][2], 1 if line else LINE) for b, _, n, line in SCATTERED]
 
     def __init__(self, spot, parts, rel_a, rel_b, from_x, from_y, line, stage, final, sems):
         self.spot, self.parts, self.rel_a, self.rel_b = spot, parts, rel_a, rel_b
@@ -615,46 +634,57 @@
             self.above_r, self.fx_s, self.fx_r, self.fy_s, self.fy_r,
             self.ha_s, self.ha_r, self.hb_s, self.hb_r, self.own_s,
         ) = sems
-        self.quarter = [p.shape[1] // 4 for p in parts]
         self.order = (spot.near[2], spot.near[1], spot.near[0], spot.row)
 
-    def part(self, g, row, j, half=None):
-        q = self.quarter[g]
-        if half is None:
-            return self.parts[g].at[row, pl.ds(pl.multiple_of(j * q, q), q)]
-        h = q // 2
-        return self.parts[g].at[row, pl.ds(pl.multiple_of(j * q + half * h, h), h)]
-
-    def half(self, ref, g, row, half):
-        h = self.quarter[g] // 2
-        return ref[g].at[row, pl.ds(half * h, h)]
+    def rows(self, g, j, half):
+        which, first, count, _ = SCATTERED[g]
+        eighth = self.parts[which].shape[1] // 8
+        if j is None:
+            return pl.ds(first * eighth, count * eighth)
+        q = eighth * count // 4
+        size = q if half is None else q // 2
+        start = first * eighth + j * q + (0 if half is None else half * size)
+        return pl.ds(pl.multiple_of(start, size), size)
+
+    def part(self, g, row, j=None, half=None):
+        return self.parts[SCATTERED[g][0]].at[row, self.rows(g, j, half)]
+
+    def fin(self, g, j, half=None):
+        return self.final[SCATTERED[g][0]].at[self.rows(g, j, half)]
+
+    def slot(self, g, t):
+        return 0 if SCATTERED[g][3] else self.order[t]
+
+    def half(self, ref, g, t, half):
+        h = ref[g].shape[1] // 2
+        return ref[g].at[self.slot(g, t), pl.ds(half * h, h)]
 
     def send_a(self, g, t):
         s, row = self.spot, self.order[t]
-        return remote(self.part(g, row, s.dp_d, 0), self.rel_a[g].at[row], self.ra_s.at[g, row], self.ra_r.at[g, row], s.beside_y)
+        return remote(self.part(g, row, s.dp_d, 0), self.rel_a[g].at[self.slot(g, t)], self.ra_s.at[g, row], self.ra_r.at[g, row], s.beside_y)
 
     def send_b(self, g, t):
         s, row = self.spot, self.order[t]
-        return remote(self.part(g, row, s.dp_d, 1), self.rel_b[g].at[row], self.rb_s.at[g, row], self.rb_r.at[g, row], s.beside_x)
+        return remote(self.part(g, row, s.dp_d, 1), self.rel_b[g].at[self.slot(g, t)], self.rb_s.at[g, row], self.rb_r.at[g, row], s.beside_x)
 
     def send_xa(self, g, t):
         s, row = self.spot, self.order[t]
-        return remote(self.part(g, row, s.dp_x, 0), self.half(self.from_x, g, row, 0), self.xa_s.at[g, row], self.xa_r.at[g, row], s.beside_x)
+        return remote(self.part(g, row, s.dp_x, 0), self.half(self.from_x, g, t, 0), self.xa_s.at[g, row], self.xa_r.at[g, row], s.beside_x)
 
     def send_xb(self, g, t):
         s, row = self.spot, self.order[t]
-        return remote(self.part(g, row, s.dp_x, 1), self.half(self.from_x, g, row, 1), self.xb_s.at[g, row], self.xb_r.at[g, row], s.beside_x)
+        return remote(self.part(g, row, s.dp_x, 1), self.half(self.from_x, g, t, 1), self.xb_s.at[g, row], self.xb_r.at[g, row], s.beside_x)
 
     def send_ya(self, g, t):
         s, row = self.spot, self.order[t]
-        return remote(self.part(g, row, s.dp_y, 0), self.half(self.from_y, g, row, 0), self.ya_s.at[g, row], self.ya_r.at[g, row], s.beside_y)
+        return remote(self.part(g, row, s.dp_y, 0), self.half(self.from_y, g, t, 0), self.ya_s.at[g, row], self.ya_r.at[g, row], s.beside_y)
 
     def send_yb(self, g, t):
         s, row = self.spot, self.order[t]
-        return remote(self.part(g, row, s.dp_y, 1), self.half(self.from_y, g, row, 1), self.yb_s.at[g, row], self.yb_r.at[g, row], s.beside_y)
-
-    def add(self, g, rows, out, terms):
-        wide = out.shape[-1]
+        return remote(self.part(g, row, s.dp_y, 1), self.half(self.from_y, g, t, 1), self.yb_s.at[g, row], self.yb_r.at[g, row], s.beside_y)
+
+    def add(self, out, terms):
+        rows, wide = out.shape
         step = min(ROWS_AT_ONCE[wide], rows)
 
         def body(i, carry):
@@ -675,33 +705,28 @@
         self.send_xb(g, t).start()
         self.send_ya(g, t).start()
 
-    def second(self, g, t):
-        s, row = self.spot, self.order[t]
-        h = self.quarter[g] // 2
+    def second_a(self, g, t):
         self.send_a(g, t).wait_recv()
-        mine = self.part(g, row, s.dp_x, 0)
-        self.add(g, h, mine, (mine, self.rel_a[g].at[row]))
+        mine = self.part(g, self.order[t], self.spot.dp_x, 0)
+        self.add(mine, (mine, self.rel_a[g].at[self.slot(g, t)]))
         self.send_xa(g, t).start()
+
+    def second_b(self, g, t):
         self.send_b(g, t).wait_recv()
-        mine = self.part(g, row, s.dp_y, 1)
-        self.add(g, h, mine, (mine, self.rel_b[g].at[row]))
+        mine = self.part(g, self.order[t], self.spot.dp_y, 1)
+        self.add(mine, (mine, self.rel_b[g].at[self.slot(g, t)]))
         self.send_yb(g, t).start()
 
     def onward(self, g, t, above=False):
         s, row = self.spot, self.order[t]
         to = jnp.where(row > s.row, s.row + 1, s.row - 1)
         slot = jnp.where(row == s.row - 1, LINE, row)
-        piece = self.part(g, row, s.dp)
+        piece = self.part(g, row, None if SCATTERED[g][3] else s.dp)
         recv = self.above_r.at[g] if above else self.z_r.at[g, row]
         return remote(piece, self.line[g].at[slot], self.z_s.at[g, row], recv, s.at_row(to))
 
-    def third(self, g, t):
+    def along(self, g, t, mine, terms, out):
         s, row = self.spot, self.order[t]
-        q = self.quarter[g]
-        for c in (self.send_xa(g, t), self.send_xb(g, t), self.send_ya(g, t), self.send_yb(g, t)):
-            c.wait_recv()
-        mine = self.part(g, row, s.dp)
-        terms = (mine, self.from_x[g].at[row], self.from_y[g].at[row])
         if t < LINE - 1:
             passed = jnp.logical_or(jnp.logical_and(row > s.row, s.row > 0), jnp.logical_and(row < s.row, s.row < LINE - 1))
             last = row == s.row - 1
@@ -709,11 +734,13 @@
             @pl.when(passed)
             def _():
                 self.onward(g, t).wait_recv()
-                self.add(g, q, mine, terms + (self.line[g].at[row],))
-
-            @pl.when(jnp.logical_not(passed))
-            def _():
-                self.add(g, q, mine, terms)
+                self.add(mine, terms + (self.line[g].at[row],))
+
+            if len(terms) > 1:
+
+                @pl.when(jnp.logical_not(passed))
+                def _():
+                    self.add(mine, terms)
 
             @pl.when(last)
             def _():
@@ -722,9 +749,9 @@
             @pl.when(jnp.logical_not(last))
             def _():
                 self.onward(g, t).start()
+
         else:
             below, over = self.line[g].at[s.row], self.line[g].at[LINE]
-            whole = self.stage[g]
 
             def wait_below():
                 remote(below, below, self.z_s.at[g, s.row], self.z_r.at[g, s.row], s.beside_x).wait_recv()
@@ -736,28 +763,37 @@
             def _():
                 wait_below()
                 wait_over()
-                self.add(g, q, whole, terms + (below, over))
+                self.add(out, terms + (below, over))
 
             @pl.when(s.row == 0)
             def _():
                 wait_over()
-                self.add(g, q, whole, terms + (over,))
+                self.add(out, terms + (over,))
 
             @pl.when(s.row == LINE - 1)
             def _():
                 wait_below()
-                self.add(g, q, whole, terms + (below,))
-
+                self.add(out, terms + (below,))
+
+    def line_step(self, g, t):
+        mine = self.part(g, self.order[t])
+        self.along(g, t, mine, (mine,), mine)
+
+    def third(self, g, t):
+        s, row = self.spot, self.order[t]
+        for c in (self.send_xa(g, t), self.send_xb(g, t), self.send_ya(g, t), self.send_yb(g, t)):
+            c.wait_recv()
+        mine = self.part(g, row, s.dp)
+        slot = self.slot(g, t)
+        terms = (mine, self.from_x[g].at[slot], self.from_y[g].at[slot])
+        if SCATTERED[g][3]:
+            self.add(self.stage[g], terms)
+        else:
+            self.along(g, t, mine, terms, self.stage[g])
+        if t == LINE - 1:
             for c in self.spread(g):
                 c.start()
             self.settle(g).start()
-
-    def fin(self, g, j, half=None):
-        q = self.quarter[g]
-        if half is None:
-            return self.final[g].at[pl.ds(pl.multiple_of(j * q, q), q)]
-        h = q // 2
-        return self.final[g].at[pl.ds(pl.multiple_of(j * q + half * h, h), h)]
 
     def spread(self, g):
         s = self.spot
@@ -779,14 +815,17 @@
             remote(b, b, self.hb_s.at[g], self.hb_r.at[g], s.beside_y),
         )
 
-    def fourth(self, g):
-        s = self.spot
-        px, py = self.fin(g, s.dp_x), self.fin(g, s.dp_y)
-        a, b = self.relays(g)
-        remote(px, px, self.fx_s.at[g], self.fx_r.at[g], s.beside_x).wait_recv()
-        b.start()
-        remote(py, py, self.fy_s.at[g], self.fy_r.at[g], s.beside_y).wait_recv()
-        a.start()
+    def fourth_x(self, g):
+        s = self.spot
+        p = self.fin(g, s.dp_x)
+        remote(p, p, self.fx_s.at[g], self.fx_r.at[g], s.beside_x).wait_recv()
+        self.relays(g)[1].start()
+
+    def fourth_y(self, g):
+        s = self.spot
+        p = self.fin(g, s.dp_y)
+        remote(p, p, self.fy_s.at[g], self.fy_r.at[g], s.beside_y).wait_recv()
+        self.relays(g)[0].start()
 
     def fifth(self, g):
         s = self.spot
@@ -795,13 +834,14 @@
         remote(b, b, self.hb_s.at[g], self.hb_r.at[g], s.beside_y).wait_recv()
 
     def drain(self):
-        for g in range(GROUPS):
+        for g in range(len(SCATTERED)):
             for t in range(LINE):
-                for c in (
-                    self.send_a(g, t), self.send_b(g, t), self.send_xa(g, t),
-                    self.send_xb(g, t), self.send_ya(g, t), self.send_yb(g, t),
-                ):
-                    c.wait_send()
+                if t == LINE - 1 or not SCATTERED[g][3]:
+                    for c in (
+                        self.send_a(g, t), self.send_b(g, t), self.send_xa(g, t),
+                        self.send_xb(g, t), self.send_ya(g, t), self.send_yb(g, t),
+                    ):
+                        c.wait_send()
                 if t < LINE - 1:
                     self.onward(g, t).wait_send()
             for c in self.spread(g) + self.relays(g):
@@ -856,6 +896,51 @@
 
         for away in range(1, LINE):
             self.copy(away).wait_send()
+
+
+(OWN, TOKENS_IN, COTANGENT_IN, ALONG, FROM_X, FROM_Y, TO_CORE, TURN_X, PROJECT, ATTEND, ATTN_OUT, NORM_1, TURN_H, GROW, SHRINK, NORM_2, LAST) = range(17)
+(SEND, ADD_A, ADD_B, SUM_UP, LINE_STEP, BACK_X, BACK_Y, OUTER_W, INNER, HIDDEN, INNER_W, NORM_BACK, MIXED, ATTN_W, QKV_W, INPUT, SUMS, SUMS_X, SUMS_Y, SUMS_LINE, INPUT_LAST, PLACE_OUT, PLACE_INPUT) = range(17, 40)
+FORWARD_ORDER = (
+    (OWN, 0), (OWN, 1), (ALONG, 0, 0), (ALONG, 0, 1), (OWN, 2), (FROM_X, 0, 0), (FROM_Y, 0, 0), (ALONG, 1, 0),
+    (FROM_X, 0, 1), (FROM_Y, 0, 1), (ALONG, 1, 1), (ALONG, 0, 2), (FROM_Y, 1, 0), (ALONG, 2, 0), (TOKENS_IN,),
+    (ALONG, 2, 1), (ALONG, 1, 2), (FROM_X, 1, 1), (FROM_Y, 1, 1), (FROM_Y, 2, 0), (FROM_X, 1, 0), (OWN, 3),
+    (FROM_Y, 1, 2), (FROM_X, 0, 2), (FROM_X, 2, 1), (FROM_X, 1, 2), (TO_CORE,), (ALONG, 3, 0), (ALONG, 3, 1),
+    (OWN, 4), (PROJECT, 0), (ALONG, 3, 2), (PROJECT, 1), (PROJECT, 2), (PROJECT, 3), (PROJECT, 4), (ALONG, 2, 2),
+    (PROJECT, 5), (OWN, 5), (FROM_X, 3, 1), (ATTEND, 0, 0), (ATTEND, 0, 1), (FROM_X, 3, 0), (ALONG, 4, 0),
+    (FROM_Y, 3, 0), (TURN_X,), (ATTEND, 0, 2), (ATTEND, 0, 3), (ALONG, 4, 1), (ATTEND, 1, 0), (ATTEND, 1, 1),
+    (ATTEND, 1, 2), (ATTEND, 1, 3), (FROM_Y, 3, 1), (FROM_X, 4, 0), (ATTEND, 2, 0), (FROM_Y, 0, 2), (FROM_X, 2, 0),
+    (ATTEND, 2, 1), (FROM_Y, 3, 2), (ATTEND, 2, 2), (ATTEND, 2, 3), (ALONG, 4, 2), (ATTEND, 3, 0), (FROM_Y, 2, 1),
+    (ATTEND, 3, 1), (FROM_X, 2, 2), (FROM_Y, 4, 0), (FROM_X, 3, 2), (FROM_Y, 2, 2), (ATTEND, 3, 2), (ATTEND, 3, 3),
+    (ATTN_OUT, 0), (ATTN_OUT, 1), (ALONG, 5, 1), (ATTN_OUT, 2), (ATTN_OUT, 3), (ALONG, 5, 0), (NORM_1,),
+    (COTANGENT_IN,), (FROM_X, 4, 1), (ALONG, 5, 2), (FROM_Y, 4, 2), (FROM_X, 4, 2), (GROW, 0), (GROW, 1), (GROW, 2),
+    (FROM_Y, 4, 1), (GROW, 3), (FROM_X, 5, 1), (FROM_Y, 5, 1), (FROM_Y, 5, 0), (GROW, 4), (FROM_Y, 5, 2),
+    (FROM_X, 5, 0), (FROM_X, 5, 2), (GROW, 5), (GROW, 6), (GROW, 7), (SHRINK, 0), (TURN_H,), (SHRINK, 1), (SHRINK, 2),
+    (SHRINK, 3), (NORM_2,), (LAST,),
+)
+BACKWARD_ORDER = (
+    (OUTER_W, 0), (OUTER_W, 1), (OUTER_W, 2), (OUTER_W, 3), (SEND, 1, 3), (INNER, 0), (SEND, 1, 0), (INNER, 1),
+    (INNER, 2), (INNER, 3), (INNER, 4), (INNER, 5), (INNER, 6), (INNER, 7), (HIDDEN, 0), (HIDDEN, 1), (SEND, 1, 2),
+    (HIDDEN, 2), (HIDDEN, 3), (SEND, 1, 1), (INNER_W, 0), (SEND, 2, 0), (INNER_W, 1), (INNER_W, 2), (SEND, 2, 1),
+    (NORM_BACK,), (SEND, 2, 2), (LINE_STEP, 0, 0), (ADD_A, 1, 0), (ADD_B, 1, 0), (INNER_W, 3), (MIXED, 0),
+    (SEND, 2, 3), (ADD_B, 2, 0), (MIXED, 1), (ATTN_W, 0), (ATTEND, 0, 0), (ATTN_W, 1), (SEND, 5, 0), (ATTEND, 0, 1),
+    (SEND, 5, 1), (ATTEND, 0, 2), (ADD_A, 2, 0), (ATTEND, 0, 3), (ATTEND, 0, 4), (ATTEND, 1, 0), (ADD_A, 1, 2),
+    (ATTEND, 1, 1), (ATTEND, 1, 2), (ATTEND, 1, 3), (ATTEND, 1, 4), (ADD_A, 2, 1), (LINE_STEP, 0, 1),
+    (LINE_STEP, 0, 2), (ATTEND, 2, 0), (ADD_B, 2, 1), (ADD_A, 1, 1), (ATTEND, 2, 1), (ATTEND, 2, 2), (ATTEND, 2, 3),
+    (ATTEND, 2, 4), (ADD_B, 2, 2), (ATTEND, 3, 0), (ADD_A, 2, 2), (ADD_B, 5, 0), (ATTEND, 3, 1), (ATTEND, 3, 2),
+    (ATTN_W, 2), (ATTEND, 3, 3), (ADD_A, 5, 1), (ADD_B, 1, 1), (ATTEND, 3, 4), (QKV_W, 0), (SEND, 5, 2), (SEND, 4, 0),
+    (ATTN_W, 3), (QKV_W, 1), (SEND, 3, 1), (SEND, 3, 0), (QKV_W, 2), (PLACE_OUT,), (QKV_W, 3), (SEND, 4, 3),
+    (INPUT, 0), (SEND, 4, 2), (ADD_B, 5, 1), (ADD_B, 2, 3), (ADD_A, 5, 0), (ADD_A, 4, 0), (SUMS,), (SUM_UP, 2, 0),
+    (ADD_A, 3, 1), (ADD_B, 1, 2), (INPUT, 1), (INPUT, 2), (ADD_A, 5, 2), (ADD_B, 5, 2), (ADD_B, 4, 0), (SEND, 4, 1),
+    (ADD_A, 3, 0), (INPUT, 3), (SEND, 3, 2), (LINE_STEP, 0, 3), (ADD_B, 3, 0), (SEND, 0, 3), (SUM_UP, 2, 1),
+    (SEND, 3, 3), (ADD_A, 2, 3), (ADD_A, 4, 3), (SUM_UP, 1, 0), (ADD_B, 4, 1), (SEND, 5, 3), (ADD_B, 3, 1),
+    (SUM_UP, 5, 0), (SUM_UP, 2, 2), (ADD_A, 4, 1), (ADD_A, 0, 3), (ADD_B, 1, 3), (SUM_UP, 1, 1), (ADD_B, 0, 3),
+    (ADD_A, 1, 3), (ADD_B, 4, 2), (INPUT_LAST,), (SUM_UP, 3, 0), (ADD_B, 3, 3), (ADD_A, 4, 2), (SUM_UP, 5, 1),
+    (SUM_UP, 5, 2), (ADD_B, 5, 3), (ADD_B, 3, 2), (SUM_UP, 2, 3), (ADD_A, 5, 3), (SUM_UP, 4, 0), (SUMS_X,),
+    (SUM_UP, 1, 2), (ADD_A, 3, 2), (SUM_UP, 0, 3), (SUM_UP, 3, 1), (ADD_A, 3, 3), (SUM_UP, 4, 1), (PLACE_INPUT,),
+    (ADD_B, 4, 3), (SUM_UP, 5, 3), (BACK_Y, 2), (BACK_X, 2), (SUM_UP, 3, 2), (BACK_Y, 0), (SUM_UP, 4, 2), (BACK_X, 0),
+    (SUM_UP, 1, 3), (SUMS_Y,), (SUM_UP, 3, 3), (SUM_UP, 4, 3), (SUMS_LINE,), (BACK_X, 5), (BACK_Y, 3), (BACK_X, 3),
+    (BACK_X, 1), (BACK_Y, 1), (BACK_Y, 4), (BACK_Y, 5), (BACK_X, 4),
+)
 
 
 F32, LOW = jnp.float32, jnp.bfloat16
@@ -954,19 +1039,19 @@
         for r in range(LINE):
             pars[:, pl.ds(r * (width // LINE), width // LINE)] = pars4[r]
 
-    def project():
+    def project(n):
         def chunk(c):
             cols = at(c, 256)
             w = wqkv[:, :, cols].reshape(width, 256)
             value = (dot(xs[...], w) + qkv_bias[0:1, cols]).astype(LOW).astype(F32)
             qkv[:, cols] = (value * jnp.where(c < half // 256, 0.125, 1.0)).astype(LOW)
 
-        loop(3 * half // 256, chunk)
+        chunk(n)
 
     def transpose_x():
         loop(width // LANES, lambda c: x_t.__setitem__((at(c, LANES), slice(None)), xs[:, at(c, LANES)].T))
 
-    def attend(pair):
+    def attend(pair, i):
         lanes = pl.ds(pair * LANES, LANES)
         keys = qkv[:, pl.ds(half + pair * LANES, LANES)]
         values = qkv[:, pl.ds(2 * half + pair * LANES, LANES)]
@@ -974,18 +1059,20 @@
         def block(i):
             rows = at(i, LANES)
             queries = qkv[rows, lanes]
-            total = None
-            for h in range(2):
+
+            def head(h, total):
                 scores = dot_t(queries * head_lanes(h, LOW), keys) + mask[rows, :]
                 expo = jnp.exp(scores - jnp.max(scores, 1, keepdims=True))
                 p = (expo / jnp.sum(expo, 1, keepdims=True)).astype(LOW)
                 probs[2 * pair + h, rows, :] = p
-                head = dot(p, values) * head_lanes(h, F32)
-                total = head if total is None else total + head
+                return total + dot(p, values) * head_lanes(h, F32)
+
+            total = lax.fori_loop(0, 2, head, jnp.zeros((LANES, LANES), F32))
             mixed[rows, lanes] = total.astype(LOW)
 
-        loop(seq // LANES, block)
-        mixed_t[lanes, :] = mixed[:, lanes].T
+        block(i)
+        if i == seq // LANES - 1:
+            mixed_t[lanes, :] = mixed[:, lanes].T
 
     def attn_out(r):
         part[:, pl.ds(r * 256, 256)] = dot(mixed[...], wo[r])
@@ -1048,103 +1135,119 @@
 
         loop(own // BLOCK, block)
 
-    z = [(g, n) for g in range(GROUPS) for n in range(LINE - 1)]
-    done_z, done_xy = [0], [0]
-
-    def advance(n_z, n_xy):
-        while done_z[0] < n_z or done_xy[0] < n_xy:
-            if done_z[0] < n_z and done_z[0] - done_xy[0] < 3 or done_xy[0] >= n_xy:
-                g, n = z[done_z[0]]
-                if n == 0 and g + 1 < GROUPS:
-                    gather.start_own(g + 1)
-                gather.z_step(g, n)
-                done_z[0] += 1
-            else:
-                gather.xy_step(*z[done_xy[0]])
-                done_xy[0] += 1
-
-    def arrive(g):
-        for n in range(LINE - 1):
-            gather.arrive(g, n)
-
-    gather.start_own(0)
-    tokens.start_x()
-    tokens.start_par()
+    seen = set()
+
+    def once(*what):
+        new = what not in seen
+        seen.add(what)
+        return new
+
+    def arrived(which, turns=range(LINE - 1)):
+        for g in range(len(GATHERED)):
+            for n in turns:
+                if GATHERED[g][0] == which and once("arrived", g, n):
+                    gather.arrive(g, n)
+
+    def relayed():
+        if once("relayed"):
+            tokens.wait_relayed()
+
+    their_half = part.at[pl.ds(pl.multiple_of(theirs, own), own)]
+    my_rows = pl.ds(pl.multiple_of(mine, own), own)
+    first, second = to_other(0, their_half, recv1), to_other(2, their_half, recv2)
+    pass_h, pass_d = to_other(1, *[h_low.at[my_rows]] * 2), to_other(3, *[dout.at[my_rows]] * 2)
+
+    def hidden_there():
+        if once("hidden"):
+            pass_h.wait_recv()
+
+    def do(what, *n):
+        if what == OWN:
+            gather.start_own(*n)
+        elif what == TOKENS_IN:
+            tokens.start_x()
+            tokens.start_par()
+        elif what == COTANGENT_IN:
+            tokens.start_ct()
+        elif what == ALONG:
+            gather.z_step(*n)
+        elif what == FROM_X:
+            gather.x_step(*n)
+        elif what == FROM_Y:
+            gather.y_step(*n)
+        elif what == TO_CORE:
+            tokens.wait_x()
+        elif what == TURN_X:
+            relayed()
+            transpose_x()
+            keep(x_t, o_xt)
+        elif what == PROJECT:
+            relayed()
+            arrived(0)
+            project(*n)
+            if n[0] == 5:
+                keep(wqkv, out_w[0])
+                keep(qkv, o_qkv)
+        elif what == ATTEND:
+            attend(*n)
+            if n == (3, 3):
+                keep(probs, o_probs)
+                keep(mixed_t, o_mixed_t)
+        elif what == ATTN_OUT:
+            arrived(1)
+            attn_out(*n)
+            if n[0] == LINE - 1:
+                keep(wo, out_w[1])
+                first.start()
+        elif what == NORM_1:
+            tokens.wait_par()
+            spread_pars()
+            keep(pars, o_pars)
+            first.wait_recv()
+            first_norm()
+            pass_h.start()
+            keep(unit, o_unit)
+            keep(inv, o_inv)
+        elif what == TURN_H:
+            hidden_there()
+            transpose_h()
+            keep(h_t, o_h_t)
+        elif what == GROW:
+            hidden_there()
+            arrived(2)
+            grow(*n)
+            if n[0] == hidden // 256 - 1:
+                keep(wi, out_w[2])
+                keep(slope, o_slope)
+                keep(act_t, o_act_t)
+        elif what == SHRINK:
+            if n[0]:
+                arrived(3, (n[0] - 1,))
+            elif once("sent"):
+                first.wait_send()
+            row = spot.near[n[0] - 1] if n[0] else spot.row
+            shrink(row)
+            keep(wout.at[row], out_w[3].at[row])
+            if n[0] == LINE - 1:
+                second.start()
+        elif what == NORM_2:
+            tokens.wait_ct()
+            second.wait_recv()
+            second_norm()
+            pass_d.start()
+            keep(dpre, o_dpre)
+            keep(out, o_out)
+            keep(sums, o_sums)
+        elif what == LAST:
+            pass_d.wait_recv()
+            keep(dout, o_dout)
+
+    hidden = act.shape[1]
     make_mask()
-    advance(2, 0)
-    tokens.wait_x()
-    advance(3, 1)
-    transpose_x()
-    keep(x_t, o_xt)
-    advance(5, 3)
-    arrive(0)
-    tokens.wait_par()
-    spread_pars()
-    project()
-    keep(wqkv, out_w[0])
-    keep(qkv, o_qkv)
-    keep(pars, o_pars)
-    tokens.start_ct()
-    for pair in range(half // LANES):
-        attend(pair)
-        advance(6 + pair // 2, 4 + pair // 2)
-    keep(probs, o_probs)
-    keep(mixed_t, o_mixed_t)
-    advance(8, 6)
-    arrive(1)
-    keep(wo, out_w[1])
-    for r in range(LINE):
-        attn_out(r)
-    first = to_other(0, part.at[pl.ds(pl.multiple_of(theirs, own), own)], recv1)
-    first.start()
-    advance(9, 7)
-    first.wait_recv()
-    first_norm()
-    pass_h = to_other(1, *[h_low.at[pl.ds(pl.multiple_of(mine, own), own)]] * 2)
-    pass_h.start()
-    keep(unit, o_unit)
-    keep(inv, o_inv)
-    advance(10, 8)
-    pass_h.wait_recv()
-    transpose_h()
-    keep(h_t, o_h_t)
-    advance(11, 9)
-    arrive(2)
-    keep(wi, out_w[2])
-    advance(12, 9)
-    first.wait_send()
-    loop(3, grow)
-    advance(12, 10)
-    loop(3, lambda c: grow(c + 3))
-    advance(12, 11)
-    loop(2, lambda c: grow(c + 6))
-    keep(slope, o_slope)
-    keep(act_t, o_act_t)
-    tokens.wait_ct()
-    for n in range(LINE):
-        if n == 0:
-            r = spot.row
-        else:
-            r = spot.near[n - 1]
-            if n == LINE - 1:
-                advance(12, 12)
-            gather.arrive(3, n - 1)
-        shrink(r)
-    keep(wout, out_w[3])
-    second = to_other(2, part.at[pl.ds(pl.multiple_of(theirs, own), own)], recv2)
-    second.start()
-    second.wait_recv()
-    second_norm()
-    pass_d = to_other(3, *[dout.at[pl.ds(pl.multiple_of(mine, own), own)]] * 2)
-    pass_d.start()
-    keep(dpre, o_dpre)
-    keep(out, o_out)
-    keep(sums, o_sums)
-    pass_d.wait_recv()
-    keep(dout, o_dout)
-    second.wait_send()
-    pass_h.wait_send()
-    pass_d.wait_send()
+    for step in FORWARD_ORDER:
+        do(*step)
+    for c in (second, pass_h, pass_d):
+        c.wait_send()
     gather.drain()
     tokens.drain()
     for c in saves:
@@ -1177,7 +1280,7 @@
         + [pltpu.VMEM(*named[n]) for n in named]
         + Tokens.SEMS
         + Gather.SEMS
-        + [pltpu.SemaphoreType.DMA((4,)), pltpu.SemaphoreType.DMA((4,)), pltpu.SemaphoreType.DMA((len(outs),))],
+        + [pltpu.SemaphoreType.DMA((4,)), pltpu.SemaphoreType.DMA((4,)), pltpu.SemaphoreType.DMA((len(outs) + LINE,))],
         compiler_params=pltpu.CompilerParams(collective_id=0, has_side_effects=True, vmem_limit_bytes=60 * 2**20),
     )(x, ct, wq, wk, wv, wo, wi, wout, seg, bq, bv, bi, *small)
     return res[:GROUPS], dict(zip(saved, res[GROUPS:]))
@@ -1252,7 +1355,8 @@
     final = take(GROUPS)
     placed_out, placed_dx, o_norms, o_bias = take(4)
     wo, wi, wout, wst = take(4)
-    parts, rel_a, rel_b, from_x, from_y, line, stage = (take(GROUPS) for _ in range(7))
+    parts = take(GROUPS)
+    rel_a, rel_b, from_x, from_y, line, stage = (take(len(SCATTERED)) for _ in range(6))
     act_t, dout, h_t, dpre, unit, inv, pars, mixed_t, qkv = take(9)
     slope, probs, ds, dinner, part, recv1, recv2, dattn, dmixed, dqkv, dx = take(11)
     vecs = take(7)
@@ -1281,33 +1385,8 @@
         fetches[name] = pltpu.make_async_copy(src, dst, load.at[len(fetches)])
         fetches[name].start()
 
-    def ready(*names):
-        for n in names:
-            fetches[n].wait()
-
     def to_other(n, src, dst):
         return remote(src, dst, core_s.at[n], core_r.at[n], spot.other_core)
-
-    units = [(g, t) for g in range(GROUPS) for t in range(LINE)]
-    second, third, fourth = [0], [0], [0]
-
-    def serve(n2, n3):
-        while second[0] < n2 or third[0] < n3:
-            if second[0] < n2 and (second[0] - third[0] < 2 or third[0] >= n3):
-                scatter.second(*units[second[0]])
-                second[0] += 1
-            else:
-                scatter.third(*units[third[0]])
-                third[0] += 1
-                while fourth[0] < GROUPS and third[0] >= LINE * (fourth[0] + 1) + 2:
-                    scatter.fourth(fourth[0])
-                    fourth[0] += 1
-
-    def send(g):
-        for t in range(LINE):
-            scatter.first(g, t)
-        for t in range(LINE):
-            scatter.direct(g, t)
 
     def wout_grad(f):
         rows = at(f, 512)
@@ -1315,14 +1394,13 @@
             parts[0][r, rows, :] = dot(act_t[rows, :], dout[:, pl.ds(r * cut, cut)]).astype(LOW)
 
     def slope_copy(f):
-        slot = lax.rem(f, 2)
+        slot = f % 2
         return pltpu.make_async_copy(saved["slope"].at[:, at(f, 256)], slope.at[slot], sl_sem.at[slot])
 
     def inner_grad(f):
         rows = at(f, 256)
 
-        @pl.when(f + 1 < hidden // 256)
-        def _():
+        if f + 1 < hidden // 256:
             slope_copy(f + 1).start()
 
         total = dot_t(dout[:, pl.ds(0, cut)], wout[0, rows, :])
@@ -1334,12 +1412,12 @@
 
         def block(i):
             here = at(i, 64)
-            d = (part[here, pl.ds(0, 256)] * slope[lax.rem(f, 2), here, :]).astype(LOW)
+            d = (part[here, pl.ds(0, 256)] * slope[f % 2, here, :]).astype(LOW)
             dinner[here, rows] = d
             part[pl.ds(0, 8), pl.ds(256, 256)] += fold(d.astype(F32))
 
         loop(seq // 64, block)
-        row, col = f // 4, lax.rem(f, 4)
+        row, col = f // 4, f % 4
         vec[pl.ds(9 + row, 1), at(col, 256)] = jnp.sum(part[pl.ds(0, 8), pl.ds(256, 256)], 0, keepdims=True)
 
     def hidden_grad(r):
@@ -1387,7 +1465,7 @@
     def probs_copy(head):
         return pltpu.make_async_copy(saved["probs"].at[head], probs.at[head % 4], pr_sem.at[head % 4])
 
-    def attend_back(pair):
+    def attend_back(pair, i):
         lanes = pl.ds(pair * LANES, LANES)
         keys_at, values_at = pl.ds(half + pair * LANES, LANES), pl.ds(2 * half + pair * LANES, LANES)
         slots = [(2 * pair + h) % 4 for h in range(2)]
@@ -1395,17 +1473,20 @@
         def block(i):
             rows = at(i, LANES)
             grad = dmixed[rows, lanes]
-            total = None
-            for h in range(2):
+
+            def head(h, total):
                 dp = dot_t(grad * head_lanes(h, LOW), qkv[:, values_at])
-                p = probs[slots[h], rows, :].astype(F32)
+                p = probs[slots[0] + h, rows, :].astype(F32)
                 d = (p * (dp - jnp.sum(p * dp, 1, keepdims=True))).astype(LOW)
                 ds[h, rows, :] = d
-                head = dot(d, qkv[:, keys_at]) * head_lanes(h, F32)
-                total = head if total is None else total + head
+                return total + dot(d, qkv[:, keys_at]) * head_lanes(h, F32)
+
+            total = lax.fori_loop(0, 2, head, jnp.zeros((LANES, LANES), F32))
             dqkv[rows, lanes] = (total * 0.125).astype(LOW)
 
-        loop(seq // LANES, block)
+        if i < seq // LANES:
+            block(i)
+            return
         queries_t, grad_t = qkv[:, lanes].T, dmixed[:, lanes].T
         dk = jnp.concatenate([dot(queries_t[h * HD : (h + 1) * HD], ds[h]) for h in range(2)], 0)
         dqkv[:, keys_at] = dk.astype(LOW).T
@@ -1450,15 +1531,103 @@
     their_half = part.at[pl.ds(pl.multiple_of(theirs, own), own)]
     my_rows = pl.ds(pl.multiple_of(mine, own), own)
 
+    swap1, swap2 = to_other(0, their_half, recv1), to_other(2, their_half, recv2)
+    pass_d = to_other(1, dattn.at[my_rows], dattn.at[my_rows])
+    seen = set()
+
+    def once(*what):
+        new = what not in seen
+        seen.add(what)
+        return new
+
+    def need(*names):
+        for n in names:
+            if once("fetched", n):
+                fetches[n].wait()
+
+    def do(what, *n):
+        if what == SEND:
+            scatter.first(*n)
+            scatter.direct(*n)
+        elif what == ADD_A:
+            scatter.second_a(*n)
+        elif what == ADD_B:
+            scatter.second_b(*n)
+        elif what == SUM_UP:
+            scatter.third(*n)
+        elif what == LINE_STEP:
+            scatter.line_step(*n)
+        elif what == BACK_X:
+            scatter.fourth_x(*n)
+        elif what == BACK_Y:
+            scatter.fourth_y(*n)
+        elif what == OUTER_W:
+            wout_grad(*n)
+        elif what == INNER:
+            need("wout")
+            inner_grad(*n)
+        elif what == HIDDEN:
+            need("wi")
+            hidden_grad(*n)
+            if n[0] == LINE - 1:
+                swap1.start()
+        elif what == INNER_W:
+            need("h_t")
+            wi_grad(*n)
+            if n[0] == LINE - 1:
+                fetch("x_t", saved["x_t"], h_t)
+        elif what == NORM_BACK:
+            need("dpre", "unit", "inv", "pars")
+            swap1.wait_recv()
+            first_norm_back()
+            pass_d.start()
+        elif what == MIXED:
+            need("wo")
+            if once("passed"):
+                pass_d.wait_recv()
+            mixed_grad(*n)
+        elif what == ATTN_W:
+            need("mixed_t")
+            wo_grad(scatter.order[n[0]])
+        elif what == ATTEND:
+            need("qkv")
+            pair, i = n
+            if i == 0:
+                for h in range(2):
+                    probs_copy(2 * pair + h).wait()
+            attend_back(pair, i)
+            if i == seq // LANES:
+                for h in range(2):
+                    if 2 * pair + h + 4 < half // HD:
+                        probs_copy(2 * pair + h + 4).start()
+        elif what == QKV_W:
+            need("x_t")
+            wqkv_grad(*n)
+        elif what == INPUT:
+            if n[0] == 0:
+                swap1.wait_send()
+            input_grad(*n)
+            if n[0] == LINE - 1:
+                swap2.start()
+        elif what == SUMS:
+            qkv_sums()
+            totals.step(0)
+        elif what in (SUMS_X, SUMS_Y, SUMS_LINE):
+            totals.step(1 + what - SUMS_X)
+        elif what == INPUT_LAST:
+            swap2.wait_recv()
+            finish_input()
+        elif what == PLACE_OUT:
+            place_out.start()
+        elif what == PLACE_INPUT:
+            place_dx.start()
+
     fetch("dout", saved["dout"], dout)
     fetch("act_t", saved["act_t"], act_t)
     greet(spot)
-    place_out.start()
-    ready("dout", "act_t")
+    need("dout", "act_t")
     fetch("wout", wout_h, wout)
     slope_copy(0).start()
-    loop(hidden // 512, wout_grad)
-    send(0)
     fetch("wi", wi_h, wi)
     fetch("h_t", saved["h_t"], h_t)
     for name, dst in (("dpre", dpre), ("unit", unit), ("inv", inv), ("pars", pars)):
@@ -1473,67 +1642,15 @@
     vec[...] = jnp.zeros_like(vec)
     for i in range(3):
         vec[pl.ds(3 + i, 1), :] = jnp.sum(sums2[i], 0, keepdims=True)
-    ready("wout")
-    loop(hidden // 256, inner_grad)
-    ready("wi", "h_t")
-    loop(LINE, hidden_grad)
-    swap1 = to_other(0, their_half, recv1)
-    swap1.start()
-    serve(1, 0)
-    for t in range(LINE):
-        wi_grad(t)
-    send(1)
-    fetch("x_t", saved["x_t"], h_t)
-    serve(2, 0)
-    ready("dpre", "unit", "inv", "pars")
-    swap1.wait_recv()
-    first_norm_back()
-    pass_d = to_other(1, dattn.at[my_rows], dattn.at[my_rows])
-    pass_d.start()
-    serve(4, 1)
-    ready("wo", "mixed_t", "qkv")
-    pass_d.wait_recv()
-    loop(half // 256, mixed_grad)
-    loop(LINE, wo_grad)
-    send(2)
-    for pair in range(half // LANES):
-        for h in range(2):
-            probs_copy(2 * pair + h).wait()
-        attend_back(pair)
-        for h in range(2):
-            if 2 * pair + h + 4 < half // HD:
-                probs_copy(2 * pair + h + 4).start()
-        serve(4 + (pair + 1) // 2, 2 + pair // 2)
-    ready("x_t")
-    for t in range(LINE):
-        wqkv_grad(t)
-    send(3)
-    serve(6, 4)
-    swap1.wait_send()
-    for r in range(LINE):
-        input_grad(r)
-    swap2 = to_other(2, their_half, recv2)
-    swap2.start()
-    qkv_sums()
-    totals.step(0)
-    serve(7, 5)
-    swap2.wait_recv()
-    finish_input()
-    place_dx.start()
-    for n in range(1, 4):
-        totals.step(n)
-        serve(7 + n, 5 + n)
-    serve(len(units), len(units))
+    for step in BACKWARD_ORDER:
+        do(*step)
     whole = totals.total()
     totals.drain()
     for i in range(8):
         o_bias[pl.ds(i, 1), :] = whole[8 + i : 9 + i, :]
     vecs[-1][0] = whole
     o_norms[...] = vecs[-1][0, pl.ds(0, 8), at(spot.row, cut)]
-    while fourth[0] < GROUPS:
-        scatter.fourth(fourth[0])
-        fourth[0] += 1
-    for g in range(GROUPS):
+    for g in range(len(SCATTERED)):
         scatter.fifth(g)
     scatter.drain()
     for c in (swap2, pass_d):
@@ -1549,8 +1666,10 @@
     half, hidden, own = wo.shape[1], wi.shape[2], seq // 2
     cut = width // LINE
 
+    groups = Scatter.sizes(shapes)
+
     def each(f):
-        return [pltpu.VMEM(f(*s), LOW) for s in shapes]
+        return [pltpu.VMEM(f(*s), LOW) for s in groups]
 
     def like(name):
         return pltpu.VMEM(saved[name].shape, saved[name].dtype)
@@ -1559,11 +1678,11 @@
     scratch = (
         [pltpu.VMEM(w.shape, LOW) for w in (wo, wi, wout)]
         + [pltpu.VMEM((2,) + wqkv.shape[1:], LOW)]
-        + each(lambda n, r, c: (n, r, c))
-        + each(lambda n, r, c: (n, r // 8, c)) * 2
-        + each(lambda n, r, c: (n, r // 4, c)) * 2
-        + each(lambda n, r, c: (n + 1, r // 4, c))
-        + each(lambda n, r, c: (r // 4, c))
+        + [pltpu.VMEM(s, LOW) for s in shapes]
+        + each(lambda r, c, n: (n, r // 8, c)) * 2
+        + each(lambda r, c, n: (n, r // 4, c)) * 2
+        + each(lambda r, c, n: (LINE + 1, r if n == 1 else r // 4, c))
+        + each(lambda r, c, n: (r // 4, c))
         + [like(n) for n in ("act_t", "dout", "h_t", "dpre", "unit", "inv", "pars", "mixed_t", "qkv")]
         + [
             pltpu.VMEM((2, seq, 256), F32), pltpu.VMEM((4, seq, seq), LOW), pltpu.VMEM((2, seq, seq), LOW),
@@ -1591,6 +1710,51 @@
     return res
 
 
+def finish_kernel(wqkv, wo, wi, wout, out, dx, norms, biases, *outs):
+    wq_o, wk_o, wv_o, wo_o, wi_o, wout_o, out_o, dx_o, bq_o, bv_o, bi_o = outs[:11]
+    half = wq_o.shape[1]
+    for i, o in enumerate((wq_o, wk_o, wv_o)):
+        o[...] = wqkv[:, i * half : (i + 1) * half].astype(F32)
+    for src, dst in ((wo, wo_o), (wi, wi_o), (wout, wout_o)):
+        dst[...] = src[...].astype(F32)
+    out_o[...] = out[...]
+    dx_o[...] = dx[...]
+
+    @pl.when(pl.program_id(0) == 0)
+    def _():
+        bq_o[...] = biases[0, 0:half]
+        bv_o[...] = biases[0, half : 2 * half]
+        wide = biases.shape[1]
+        for i in range(bi_o.shape[0] // wide):
+            bi_o[i * wide : (i + 1) * wide] = biases[1 + i, :]
+        for i, o in enumerate(outs[11:]):
+            o[...] = norms[i, :]
+
+
+def finish(wqkv, wo, wi, wout, out, dx, norms, biases, steps=4):
+    half, cut = wqkv.shape[1] // 3, norms.shape[1]
+    big = [(wqkv.shape[0], half)] * 3 + [w.shape for w in (wo, wi, wout)]
+
+    def tiled(shape):
+        return pl.BlockSpec((shape[0] // steps, shape[1]), lambda i: (i, 0))
+
+    def whole(shape):
+        return pl.BlockSpec(shape, lambda i: (0,) * len(shape))
+
+    vectors = [(half,), (half,), (wi.shape[1],)] + [(cut,)] * 6
+    return pl.pallas_call(
+        finish_kernel,
+        name="finish",
+        grid=(steps,),
+        out_shape=[jax.ShapeDtypeStruct(s, F32) for s in big]
+        + [jax.ShapeDtypeStruct(v.shape, LOW) for v in (out, dx)]
+        + [jax.ShapeDtypeStruct(s, F32) for s in vectors],
+        in_specs=[tiled(v.shape) for v in (wqkv, wo, wi, wout, out, dx)] + [whole(norms.shape), whole(biases.shape)],
+        out_specs=[tiled(s) for s in big] + [tiled(out.shape)] * 2 + [whole(s) for s in vectors],
+        compiler_params=pltpu.CompilerParams(vmem_limit_bytes=63 * 2**20),
+    )(wqkv, wo, wi, wout, out, dx, norms, biases)
+
+
 def per_chip(
     hidden_in, segment_ids, query_weight, query_bias, key_weight, value_weight, value_bias, attn_out_weight,
     attn_out_bias, norm1_gain, first_norm_offset, inner_weight, inner_bias, outer_weight, outer_bias, norm2_gain,
@@ -1603,11 +1767,10 @@
         segment_ids, query_bias, value_bias, inner_bias, small,
     )
     wout, wi, wo, wqkv, layer_out, input_grad, norms, biases = backward(weights, saved)
-    wq, wk, wv = jnp.split(wqkv.astype(F32), 3, 1)
-    return (
-        layer_out, input_grad, wq, biases[0, :half], wk, wv, biases[0, half:], wo.astype(F32), norms[0], norms[1],
-        norms[2], wi.astype(F32), biases[1:3].reshape(-1), wout.astype(F32), norms[3], norms[4], norms[5],
-    )
+    wq, wk, wv, wo, wi, wout, layer_out, input_grad, bq, bv, bi, bo, g1, b1, bout, g2, b2 = finish(
+        wqkv, wo, wi, wout, layer_out, input_grad, norms, biases
+    )
+    return layer_out, input_grad, wq, bq, wk, wv, bv, wo, bo, g1, b1, wi, bi, wout, bout, g2, b2
 
 
 def solution(mesh):

time: 305 us -> 255 us (0.84)
  Pallas kernels: 291 us -> 252 us
  local copies, waits for them, and re-layouts: 8.28 us -> 0 us
  other arithmetic: 4.81 us -> 0 us
    pallas_call x1, Pallas kernels: 163 us -> 134 us  [backward(): pl.pallas_call(backward_kernel, name='backward', out_shape=[jax.ShapeDtyp...]
    pallas_call x1, Pallas kernels: 128 us -> 112 us  [forward(): pl.pallas_call(forward_kernel, name='forward', out_shape=[jax.ShapeDtypeS...]
    pallas_call x0 -> x1, Pallas kernels: none -> 5.71 us  [finish(): pl.pallas_call(finish_kernel, name='finish', grid=(steps,), out_shape=[ja...]
    convert_element_type x3 -> x0, other arithmetic: 4.81 us -> none  [the longest x1 1.78 us: per_chip(): wo.astype(F32)]
where the time goes in v3:
time: 255 us; the launch traced here: 253 us
  Pallas kernels  252 us (99%)
    pallas_call x1, Pallas kernels, backward(): pl.pallas_call(backward_kernel, name='backward', out_shape=[jax.ShapeDtyp...  134 us
    pallas_call x1, Pallas kernels, forward(): pl.pallas_call(forward_kernel, name='forward', out_shape=[jax.ShapeDtypeS...  112 us
    pallas_call x1, Pallas kernels, finish(): pl.pallas_call(finish_kernel, name='finish', grid=(steps,), out_shape=[ja...  5.71 us

profile of v3, /device:TPU:0, one launch (start us, length us, event | category | flops | bytes accessed | tf_op | source)
XLA Modules:
  0.0 253.0 jit_solution(16133177236751515021)
XLA Ops:
  0.7 112.4 %forward.1 = (bf16[4,256,1536]{2,1,0:T(8,128)(2,1)}, bf16[4,512,256]{2,1,0:T(8,128)(2,1)}, bf16[4,256,2048]{2,1,0:T(8,128)(2,1)}, bf16[4,2048,256]{2,1,0:T(8,128...) custom-call(bf16[1024,256]{1,0:T(8,128)(2,1)} %refs_0_.1, ...), custom_call_target="tpu_custom_call" | custom-call | tf_op jit(solution)/shard_map/forward/pallas_call | solution.py:1273
  113.1 134.0 %backward.1 = (bf16[2048,256]{1,0:T(8,128)(2,1)}, bf16[256,2048]{1,0:T(8,128)(2,1)}, bf16[512,256]{1,0:T(8,128)(2,1)}, bf16[256,1536]{1,0:T(8,128)(2,1)}, bf16[1...) custom-call(bf16[4,256,1536]{2,1,0:T(8,128)(2,1)} %get-tuple-element.60.refs_0_, ...), custom_call_target="tpu_custom_call" | custom-call | tf_op jit(solution)/shard_map/backward/pallas_call | solution.py:1699
  247.1 5.7 %finish.1 = (f32[256,512]{1,0:T(8,128)}, f32[256,512]{1,0:T(8,128)}, f32[256,512]{1,0:T(8,128)}, f32[512,256]{1,0:T(8,128)}, f32[256,2048]{1,0:T(8,128)}, /*inde...) custom-call(bf16[256,1536]{1,0:T(8,128)(2,1)} %get-tuple-element.78., ...), custom_call_target="tpu_custom_call" | custom-call | tf_op jit(solution)/shard_map/finish/pallas_call | solution.py:1745

commit v4 on v3

--- a/solution.py
+++ b/solution.py
@@ -297,9 +297,10 @@
 MESH = pl.DeviceIdType.MESH
 LINE = 4
 GROUPS = 4
-GATHERED = ((1, 0, 8), (0, 0, 8), (2, 0, 4), (2, 4, 4), (3, 0, 4), (3, 4, 4))
+GATHERED = ((1, 0, 8), (0, 0, 8), (2, 0, 8), (3, 0, 4), (3, 4, 4))
 SCATTERED = (
-    (0, 0, 4, True), (0, 4, 4, False), (1, 0, 8, False), (3, 0, 4, False), (3, 4, 4, False), (2, 0, 8, False),
+    (0, 0, 2, True), (0, 2, 2, True), (0, 4, 2, True), (0, 6, 2, False), (1, 0, 8, False), (3, 0, 8, False),
+    (2, 0, 8, False),
 )
 
 
@@ -331,18 +332,34 @@
     )
 
 
-def greet(spot):
+def greet(spot, far=False):
     barrier = pltpu.get_barrier_semaphore()
-    for away in range(LINE):
-        row = lax.rem(spot.row + away, LINE)
-        for core in range(2):
-            if away == 0 and core == 0:
-                continue
-            col = lax.rem(spot.col + core, 2)
-            pl.semaphore_signal(barrier, inc=1, device_id=(spot.dp, row, col), device_id_type=MESH)
-    pl.semaphore_signal(barrier, inc=1, device_id=spot.beside_x, device_id_type=MESH)
-    pl.semaphore_signal(barrier, inc=1, device_id=spot.beside_y, device_id_type=MESH)
-    pl.semaphore_wait(barrier, 2 * LINE + 1)
+
+    def tell(device):
+        pl.semaphore_signal(barrier, inc=1, device_id=device, device_id_type=MESH)
+
+    if far:
+        for away in range(LINE):
+            row = lax.rem(spot.row + away, LINE)
+            for core in (1, 2):
+                if away or core == 1:
+                    tell((spot.dp, row, lax.rem(spot.col + core, 2)))
+        tell(spot.beside_x)
+        tell(spot.beside_y)
+        pl.semaphore_wait(barrier, 2 * LINE + 1)
+        return
+    for device in (spot.beside_x, spot.beside_y, spot.other_core):
+        tell(device)
+
+    @pl.when(spot.row > 0)
+    def _():
+        tell(spot.at_row(spot.row - 1))
+
+    @pl.when(spot.row < LINE - 1)
+    def _():
+        tell(spot.at_row(spot.row + 1))
+
+    pl.semaphore_wait(barrier, 3 + jnp.where(spot.inside, 2, 1))
 
 
 class Gather:
@@ -901,45 +918,44 @@
 (OWN, TOKENS_IN, COTANGENT_IN, ALONG, FROM_X, FROM_Y, TO_CORE, TURN_X, PROJECT, ATTEND, ATTN_OUT, NORM_1, TURN_H, GROW, SHRINK, NORM_2, LAST) = range(17)
 (SEND, ADD_A, ADD_B, SUM_UP, LINE_STEP, BACK_X, BACK_Y, OUTER_W, INNER, HIDDEN, INNER_W, NORM_BACK, MIXED, ATTN_W, QKV_W, INPUT, SUMS, SUMS_X, SUMS_Y, SUMS_LINE, INPUT_LAST, PLACE_OUT, PLACE_INPUT) = range(17, 40)
 FORWARD_ORDER = (
-    (OWN, 0), (OWN, 1), (ALONG, 0, 0), (ALONG, 0, 1), (OWN, 2), (FROM_X, 0, 0), (FROM_Y, 0, 0), (ALONG, 1, 0),
-    (FROM_X, 0, 1), (FROM_Y, 0, 1), (ALONG, 1, 1), (ALONG, 0, 2), (FROM_Y, 1, 0), (ALONG, 2, 0), (TOKENS_IN,),
-    (ALONG, 2, 1), (ALONG, 1, 2), (FROM_X, 1, 1), (FROM_Y, 1, 1), (FROM_Y, 2, 0), (FROM_X, 1, 0), (OWN, 3),
-    (FROM_Y, 1, 2), (FROM_X, 0, 2), (FROM_X, 2, 1), (FROM_X, 1, 2), (TO_CORE,), (ALONG, 3, 0), (ALONG, 3, 1),
-    (OWN, 4), (PROJECT, 0), (ALONG, 3, 2), (PROJECT, 1), (PROJECT, 2), (PROJECT, 3), (PROJECT, 4), (ALONG, 2, 2),
-    (PROJECT, 5), (OWN, 5), (FROM_X, 3, 1), (ATTEND, 0, 0), (ATTEND, 0, 1), (FROM_X, 3, 0), (ALONG, 4, 0),
-    (FROM_Y, 3, 0), (TURN_X,), (ATTEND, 0, 2), (ATTEND, 0, 3), (ALONG, 4, 1), (ATTEND, 1, 0), (ATTEND, 1, 1),
-    (ATTEND, 1, 2), (ATTEND, 1, 3), (FROM_Y, 3, 1), (FROM_X, 4, 0), (ATTEND, 2, 0), (FROM_Y, 0, 2), (FROM_X, 2, 0),
-    (ATTEND, 2, 1), (FROM_Y, 3, 2), (ATTEND, 2, 2), (ATTEND, 2, 3), (ALONG, 4, 2), (ATTEND, 3, 0), (FROM_Y, 2, 1),
-    (ATTEND, 3, 1), (FROM_X, 2, 2), (FROM_Y, 4, 0), (FROM_X, 3, 2), (FROM_Y, 2, 2), (ATTEND, 3, 2), (ATTEND, 3, 3),
-    (ATTN_OUT, 0), (ATTN_OUT, 1), (ALONG, 5, 1), (ATTN_OUT, 2), (ATTN_OUT, 3), (ALONG, 5, 0), (NORM_1,),
-    (COTANGENT_IN,), (FROM_X, 4, 1), (ALONG, 5, 2), (FROM_Y, 4, 2), (FROM_X, 4, 2), (GROW, 0), (GROW, 1), (GROW, 2),
-    (FROM_Y, 4, 1), (GROW, 3), (FROM_X, 5, 1), (FROM_Y, 5, 1), (FROM_Y, 5, 0), (GROW, 4), (FROM_Y, 5, 2),
-    (FROM_X, 5, 0), (FROM_X, 5, 2), (GROW, 5), (GROW, 6), (GROW, 7), (SHRINK, 0), (TURN_H,), (SHRINK, 1), (SHRINK, 2),
-    (SHRINK, 3), (NORM_2,), (LAST,),
+    (OWN, 0), (OWN, 1), (ALONG, 0, 0), (ALONG, 0, 1), (FROM_Y, 0, 0), (FROM_X, 0, 0), (ALONG, 1, 0), (ALONG, 1, 1),
+    (ALONG, 0, 2), (TOKENS_IN,), (FROM_Y, 0, 1), (FROM_X, 0, 1), (ALONG, 1, 2), (OWN, 2), (FROM_X, 0, 2),
+    (FROM_Y, 1, 0), (FROM_X, 1, 0), (FROM_X, 1, 2), (FROM_Y, 0, 2), (FROM_Y, 1, 2), (FROM_X, 1, 1), (FROM_Y, 1, 1),
+    (ALONG, 2, 0), (ALONG, 2, 1), (TO_CORE,), (PROJECT, 0), (ALONG, 2, 2), (OWN, 3), (PROJECT, 1), (PROJECT, 2),
+    (OWN, 4), (PROJECT, 3), (PROJECT, 4), (PROJECT, 5), (ATTEND, 0, 0), (ATTEND, 0, 1), (FROM_X, 2, 1),
+    (ATTEND, 0, 2), (FROM_Y, 2, 1), (ATTEND, 0, 3), (ATTEND, 1, 0), (ATTEND, 1, 1), (ALONG, 3, 0), (ALONG, 3, 1),
+    (ATTEND, 1, 2), (ATTEND, 1, 3), (ATTEND, 2, 0), (FROM_Y, 2, 2), (ATTEND, 2, 1), (ALONG, 4, 0), (ATTEND, 2, 2),
+    (ATTEND, 2, 3), (ATTEND, 3, 0), (ALONG, 4, 1), (ATTEND, 3, 1), (FROM_Y, 3, 1), (ATTEND, 3, 2), (ATTEND, 3, 3),
+    (ATTN_OUT, 0), (ATTN_OUT, 1), (FROM_X, 2, 2), (FROM_X, 2, 0), (ATTN_OUT, 2), (FROM_Y, 2, 0), (FROM_Y, 3, 0),
+    (ATTN_OUT, 3), (ALONG, 3, 2), (FROM_X, 4, 0), (ALONG, 4, 2), (FROM_Y, 4, 1), (NORM_1,), (FROM_X, 3, 1),
+    (COTANGENT_IN,), (GROW, 0), (TURN_X,), (FROM_Y, 3, 2), (FROM_Y, 4, 0), (GROW, 1), (GROW, 2), (FROM_X, 3, 2),
+    (FROM_X, 3, 0), (GROW, 3), (FROM_X, 4, 1), (GROW, 4), (FROM_Y, 4, 2), (FROM_X, 4, 2), (GROW, 5), (GROW, 6),
+    (GROW, 7), (TURN_H,), (SHRINK, 0), (SHRINK, 1), (SHRINK, 2), (SHRINK, 3), (NORM_2,), (LAST,),
 )
 BACKWARD_ORDER = (
-    (OUTER_W, 0), (OUTER_W, 1), (OUTER_W, 2), (OUTER_W, 3), (SEND, 1, 3), (INNER, 0), (SEND, 1, 0), (INNER, 1),
-    (INNER, 2), (INNER, 3), (INNER, 4), (INNER, 5), (INNER, 6), (INNER, 7), (HIDDEN, 0), (HIDDEN, 1), (SEND, 1, 2),
-    (HIDDEN, 2), (HIDDEN, 3), (SEND, 1, 1), (INNER_W, 0), (SEND, 2, 0), (INNER_W, 1), (INNER_W, 2), (SEND, 2, 1),
-    (NORM_BACK,), (SEND, 2, 2), (LINE_STEP, 0, 0), (ADD_A, 1, 0), (ADD_B, 1, 0), (INNER_W, 3), (MIXED, 0),
-    (SEND, 2, 3), (ADD_B, 2, 0), (MIXED, 1), (ATTN_W, 0), (ATTEND, 0, 0), (ATTN_W, 1), (SEND, 5, 0), (ATTEND, 0, 1),
-    (SEND, 5, 1), (ATTEND, 0, 2), (ADD_A, 2, 0), (ATTEND, 0, 3), (ATTEND, 0, 4), (ATTEND, 1, 0), (ADD_A, 1, 2),
-    (ATTEND, 1, 1), (ATTEND, 1, 2), (ATTEND, 1, 3), (ATTEND, 1, 4), (ADD_A, 2, 1), (LINE_STEP, 0, 1),
-    (LINE_STEP, 0, 2), (ATTEND, 2, 0), (ADD_B, 2, 1), (ADD_A, 1, 1), (ATTEND, 2, 1), (ATTEND, 2, 2), (ATTEND, 2, 3),
-    (ATTEND, 2, 4), (ADD_B, 2, 2), (ATTEND, 3, 0), (ADD_A, 2, 2), (ADD_B, 5, 0), (ATTEND, 3, 1), (ATTEND, 3, 2),
-    (ATTN_W, 2), (ATTEND, 3, 3), (ADD_A, 5, 1), (ADD_B, 1, 1), (ATTEND, 3, 4), (QKV_W, 0), (SEND, 5, 2), (SEND, 4, 0),
-    (ATTN_W, 3), (QKV_W, 1), (SEND, 3, 1), (SEND, 3, 0), (QKV_W, 2), (PLACE_OUT,), (QKV_W, 3), (SEND, 4, 3),
-    (INPUT, 0), (SEND, 4, 2), (ADD_B, 5, 1), (ADD_B, 2, 3), (ADD_A, 5, 0), (ADD_A, 4, 0), (SUMS,), (SUM_UP, 2, 0),
-    (ADD_A, 3, 1), (ADD_B, 1, 2), (INPUT, 1), (INPUT, 2), (ADD_A, 5, 2), (ADD_B, 5, 2), (ADD_B, 4, 0), (SEND, 4, 1),
-    (ADD_A, 3, 0), (INPUT, 3), (SEND, 3, 2), (LINE_STEP, 0, 3), (ADD_B, 3, 0), (SEND, 0, 3), (SUM_UP, 2, 1),
-    (SEND, 3, 3), (ADD_A, 2, 3), (ADD_A, 4, 3), (SUM_UP, 1, 0), (ADD_B, 4, 1), (SEND, 5, 3), (ADD_B, 3, 1),
-    (SUM_UP, 5, 0), (SUM_UP, 2, 2), (ADD_A, 4, 1), (ADD_A, 0, 3), (ADD_B, 1, 3), (SUM_UP, 1, 1), (ADD_B, 0, 3),
-    (ADD_A, 1, 3), (ADD_B, 4, 2), (INPUT_LAST,), (SUM_UP, 3, 0), (ADD_B, 3, 3), (ADD_A, 4, 2), (SUM_UP, 5, 1),
-    (SUM_UP, 5, 2), (ADD_B, 5, 3), (ADD_B, 3, 2), (SUM_UP, 2, 3), (ADD_A, 5, 3), (SUM_UP, 4, 0), (SUMS_X,),
-    (SUM_UP, 1, 2), (ADD_A, 3, 2), (SUM_UP, 0, 3), (SUM_UP, 3, 1), (ADD_A, 3, 3), (SUM_UP, 4, 1), (PLACE_INPUT,),
-    (ADD_B, 4, 3), (SUM_UP, 5, 3), (BACK_Y, 2), (BACK_X, 2), (SUM_UP, 3, 2), (BACK_Y, 0), (SUM_UP, 4, 2), (BACK_X, 0),
-    (SUM_UP, 1, 3), (SUMS_Y,), (SUM_UP, 3, 3), (SUM_UP, 4, 3), (SUMS_LINE,), (BACK_X, 5), (BACK_Y, 3), (BACK_X, 3),
-    (BACK_X, 1), (BACK_Y, 1), (BACK_Y, 4), (BACK_Y, 5), (BACK_X, 4),
+    (PLACE_OUT,), (OUTER_W, 0), (OUTER_W, 1), (OUTER_W, 2), (OUTER_W, 3), (SEND, 3, 1), (INNER, 0), (INNER, 1),
+    (SEND, 3, 0), (INNER, 2), (INNER, 3), (INNER, 4), (SEND, 3, 2), (SEND, 3, 3), (INNER, 5), (INNER, 6), (INNER, 7),
+    (INNER_W, 0), (HIDDEN, 0), (INNER_W, 1), (SEND, 4, 1), (LINE_STEP, 0, 0), (SEND, 4, 0), (HIDDEN, 1), (INNER_W, 2),
+    (HIDDEN, 2), (HIDDEN, 3), (SEND, 4, 2), (ADD_B, 3, 3), (ADD_A, 3, 1), (ADD_B, 4, 1), (LINE_STEP, 0, 1),
+    (INNER_W, 3), (ADD_B, 3, 0), (NORM_BACK,), (LINE_STEP, 0, 2), (ADD_A, 4, 1), (SEND, 4, 3), (MIXED, 0),
+    (ATTN_W, 0), (ADD_B, 4, 0), (ADD_A, 3, 0), (ADD_A, 3, 2), (MIXED, 1), (SEND, 6, 0), (ATTEND, 0, 0),
+    (ATTEND, 0, 1), (ATTEND, 0, 2), (LINE_STEP, 1, 0), (ATTEND, 0, 3), (ATTEND, 0, 4), (ATTN_W, 1), (ATTEND, 1, 0),
+    (ADD_A, 4, 0), (ATTEND, 1, 1), (ATTEND, 1, 2), (ATTEND, 1, 3), (ATTEND, 1, 4), (ATTEND, 2, 0), (ADD_A, 4, 2),
+    (LINE_STEP, 1, 1), (ATTN_W, 2), (ATTEND, 2, 1), (ATTEND, 2, 2), (SEND, 6, 2), (LINE_STEP, 1, 2), (SEND, 6, 1),
+    (ATTEND, 2, 3), (ADD_A, 3, 3), (ADD_B, 4, 3), (ATTEND, 2, 4), (ATTEND, 3, 0), (ATTEND, 3, 1), (ATTEND, 3, 2),
+    (ATTEND, 3, 3), (ATTEND, 3, 4), (ADD_B, 3, 1), (QKV_W, 0), (SEND, 5, 0), (LINE_STEP, 0, 3), (ATTN_W, 3),
+    (ADD_B, 4, 2), (SUM_UP, 3, 0), (INPUT, 0), (ADD_B, 6, 0), (ADD_A, 6, 2), (INPUT, 1), (ADD_A, 4, 3),
+    (LINE_STEP, 2, 0), (QKV_W, 1), (LINE_STEP, 1, 3), (ADD_B, 6, 1), (INPUT, 2), (SEND, 6, 3), (SUM_UP, 4, 0),
+    (SEND, 0, 3), (ADD_A, 6, 1), (SUM_UP, 3, 1), (INPUT, 3), (SEND, 5, 1), (ADD_A, 5, 0), (QKV_W, 2), (SEND, 5, 2),
+    (ADD_B, 6, 3), (LINE_STEP, 2, 1), (ADD_B, 5, 0), (LINE_STEP, 2, 2), (SEND, 1, 3), (QKV_W, 3), (SEND, 5, 3),
+    (ADD_B, 3, 2), (SUM_UP, 4, 1), (LINE_STEP, 2, 3), (SEND, 2, 3), (SUM_UP, 4, 2), (ADD_B, 1, 3), (ADD_A, 6, 0),
+    (SUMS,), (ADD_A, 5, 3), (SUMS_X,), (ADD_A, 5, 1), (ADD_B, 5, 3), (ADD_B, 5, 1), (ADD_A, 0, 3), (ADD_B, 5, 2),
+    (ADD_B, 0, 3), (ADD_B, 6, 2), (ADD_A, 2, 3), (INPUT_LAST,), (ADD_A, 6, 3), (ADD_A, 5, 2), (SUM_UP, 5, 0),
+    (SUM_UP, 6, 0), (ADD_B, 2, 3), (SUMS_Y,), (SUM_UP, 4, 3), (SUM_UP, 5, 1), (SUM_UP, 3, 2), (ADD_A, 1, 3),
+    (SUM_UP, 6, 1), (SUM_UP, 5, 2), (SUM_UP, 3, 3), (SUM_UP, 2, 3), (SUM_UP, 6, 2), (SUM_UP, 0, 3), (PLACE_INPUT,),
+    (SUM_UP, 1, 3), (SUM_UP, 5, 3), (BACK_Y, 0), (SUM_UP, 6, 3), (BACK_Y, 2), (BACK_X, 4), (SUMS_LINE,), (BACK_Y, 4),
+    (BACK_X, 3), (BACK_X, 2), (BACK_Y, 6), (BACK_X, 5), (BACK_X, 0), (BACK_X, 1), (BACK_Y, 3), (BACK_X, 6),
+    (BACK_Y, 1), (BACK_Y, 5),
 )
 
 
@@ -1154,7 +1170,14 @@
 
     their_half = part.at[pl.ds(pl.multiple_of(theirs, own), own)]
     my_rows = pl.ds(pl.multiple_of(mine, own), own)
-    first, second = to_other(0, their_half, recv1), to_other(2, their_half, recv2)
+    first = to_other(0, their_half, recv1)
+
+    def second(row):
+        cols = at(row, 256)
+        return to_other(
+            4 + row, part.at[pl.ds(pl.multiple_of(theirs, own), own), cols], recv2.at[:, cols]
+        )
+
     pass_h, pass_d = to_other(1, *[h_low.at[my_rows]] * 2), to_other(3, *[dout.at[my_rows]] * 2)
 
     def hidden_there():
@@ -1228,11 +1251,11 @@
             row = spot.near[n[0] - 1] if n[0] else spot.row
             shrink(row)
             keep(wout.at[row], out_w[3].at[row])
-            if n[0] == LINE - 1:
-                second.start()
+            second(row).start()
         elif what == NORM_2:
             tokens.wait_ct()
-            second.wait_recv()
+            for row in range(LINE):
+                second(row).wait_recv()
             second_norm()
             pass_d.start()
             keep(dpre, o_dpre)
@@ -1246,7 +1269,7 @@
     make_mask()
     for step in FORWARD_ORDER:
         do(*step)
-    for c in (second, pass_h, pass_d):
+    for c in (pass_h, pass_d, *(second(row) for row in range(LINE))):
         c.wait_send()
     gather.drain()
     tokens.drain()
@@ -1280,7 +1303,7 @@
         + [pltpu.VMEM(*named[n]) for n in named]
         + Tokens.SEMS
         + Gather.SEMS
-        + [pltpu.SemaphoreType.DMA((4,)), pltpu.SemaphoreType.DMA((4,)), pltpu.SemaphoreType.DMA((len(outs) + LINE,))],
+        + [pltpu.SemaphoreType.DMA((4 + LINE,)), pltpu.SemaphoreType.DMA((4 + LINE,)), pltpu.SemaphoreType.DMA((len(outs) + LINE,))],
         compiler_params=pltpu.CompilerParams(collective_id=0, has_side_effects=True, vmem_limit_bytes=60 * 2**20),
     )(x, ct, wq, wk, wv, wo, wi, wout, seg, bq, bv, bi, *small)
     return res[:GROUPS], dict(zip(saved, res[GROUPS:]))
@@ -1624,7 +1647,7 @@
 
     fetch("dout", saved["dout"], dout)
     fetch("act_t", saved["act_t"], act_t)
-    greet(spot)
+    greet(spot, far=True)
     need("dout", "act_t")
     fetch("wout", wout_h, wout)
     slope_copy(0).start()
@@ -1731,7 +1754,7 @@
             o[...] = norms[i, :]
 
 
-def finish(wqkv, wo, wi, wout, out, dx, norms, biases, steps=4):
+def finish(wqkv, wo, wi, wout, out, dx, norms, biases, steps=2):
     half, cut = wqkv.shape[1] // 3, norms.shape[1]
     big = [(wqkv.shape[0], half)] * 3 + [w.shape for w in (wo, wi, wout)]
 

time: 255 us -> 247 us (0.969)
  Pallas kernels: 252 us -> 246 us
    pallas_call x1, Pallas kernels: 112 us -> 107 us  [forward(): pl.pallas_call(forward_kernel, name='forward', out_shape=[jax.ShapeDtypeS...]
where the time goes in v4:
time: 247 us
  Pallas kernels  246 us (100%)
    pallas_call x1, Pallas kernels, backward(): pl.pallas_call(backward_kernel, name='backward', out_shape=[jax.ShapeDtyp...  134 us
    pallas_call x1, Pallas kernels, forward(): pl.pallas_call(forward_kernel, name='forward', out_shape=[jax.ShapeDtypeS...  107 us
    pallas_call x1, Pallas kernels, finish(): pl.pallas_call(finish_kernel, name='finish', grid=(steps,), out_shape=[ja...  4.94 us

profile of v4, /device:TPU:0, one launch (start us, length us, event | category | flops | bytes accessed | tf_op | source)
XLA Modules:
  0.0 246.6 jit_solution(13890695212772163017)
XLA Ops:
  0.7 107.1 %forward.1 = (bf16[4,256,1536]{2,1,0:T(8,128)(2,1)}, bf16[4,512,256]{2,1,0:T(8,128)(2,1)}, bf16[4,256,2048]{2,1,0:T(8,128)(2,1)}, bf16[4,2048,256]{2,1,0:T(8,128...) custom-call(bf16[1024,256]{1,0:T(8,128)(2,1)} %refs_0_.1, ...), custom_call_target="tpu_custom_call" | custom-call | tf_op jit(solution)/shard_map/forward/pallas_call | solution.py:1296
  107.8 133.7 %backward.1 = (bf16[2048,256]{1,0:T(8,128)(2,1)}, bf16[256,2048]{1,0:T(8,128)(2,1)}, bf16[512,256]{1,0:T(8,128)(2,1)}, bf16[256,1536]{1,0:T(8,128)(2,1)}, bf16[1...) custom-call(bf16[4,256,1536]{2,1,0:T(8,128)(2,1)} %get-tuple-element.60.refs_0_, ...), custom_call_target="tpu_custom_call" | custom-call | tf_op jit(solution)/shard_map/backward/pallas_call | solution.py:1722
  241.4 4.9 %finish.1 = (f32[256,512]{1,0:T(8,128)}, f32[256,512]{1,0:T(8,128)}, f32[256,512]{1,0:T(8,128)}, f32[512,256]{1,0:T(8,128)}, f32[256,2048]{1,0:T(8,128)}, /*inde...) custom-call(bf16[256,1536]{1,0:T(8,128)(2,1)} %get-tuple-element.78., ...), custom_call_target="tpu_custom_call" | custom-call | tf_op jit(solution)/shard_map/finish/pallas_call | solution.py:1768

commit v5 on v4

--- a/solution.py
+++ b/solution.py
@@ -918,44 +918,44 @@
 (OWN, TOKENS_IN, COTANGENT_IN, ALONG, FROM_X, FROM_Y, TO_CORE, TURN_X, PROJECT, ATTEND, ATTN_OUT, NORM_1, TURN_H, GROW, SHRINK, NORM_2, LAST) = range(17)
 (SEND, ADD_A, ADD_B, SUM_UP, LINE_STEP, BACK_X, BACK_Y, OUTER_W, INNER, HIDDEN, INNER_W, NORM_BACK, MIXED, ATTN_W, QKV_W, INPUT, SUMS, SUMS_X, SUMS_Y, SUMS_LINE, INPUT_LAST, PLACE_OUT, PLACE_INPUT) = range(17, 40)
 FORWARD_ORDER = (
-    (OWN, 0), (OWN, 1), (ALONG, 0, 0), (ALONG, 0, 1), (FROM_Y, 0, 0), (FROM_X, 0, 0), (ALONG, 1, 0), (ALONG, 1, 1),
-    (ALONG, 0, 2), (TOKENS_IN,), (FROM_Y, 0, 1), (FROM_X, 0, 1), (ALONG, 1, 2), (OWN, 2), (FROM_X, 0, 2),
-    (FROM_Y, 1, 0), (FROM_X, 1, 0), (FROM_X, 1, 2), (FROM_Y, 0, 2), (FROM_Y, 1, 2), (FROM_X, 1, 1), (FROM_Y, 1, 1),
-    (ALONG, 2, 0), (ALONG, 2, 1), (TO_CORE,), (PROJECT, 0), (ALONG, 2, 2), (OWN, 3), (PROJECT, 1), (PROJECT, 2),
-    (OWN, 4), (PROJECT, 3), (PROJECT, 4), (PROJECT, 5), (ATTEND, 0, 0), (ATTEND, 0, 1), (FROM_X, 2, 1),
-    (ATTEND, 0, 2), (FROM_Y, 2, 1), (ATTEND, 0, 3), (ATTEND, 1, 0), (ATTEND, 1, 1), (ALONG, 3, 0), (ALONG, 3, 1),
-    (ATTEND, 1, 2), (ATTEND, 1, 3), (ATTEND, 2, 0), (FROM_Y, 2, 2), (ATTEND, 2, 1), (ALONG, 4, 0), (ATTEND, 2, 2),
-    (ATTEND, 2, 3), (ATTEND, 3, 0), (ALONG, 4, 1), (ATTEND, 3, 1), (FROM_Y, 3, 1), (ATTEND, 3, 2), (ATTEND, 3, 3),
-    (ATTN_OUT, 0), (ATTN_OUT, 1), (FROM_X, 2, 2), (FROM_X, 2, 0), (ATTN_OUT, 2), (FROM_Y, 2, 0), (FROM_Y, 3, 0),
-    (ATTN_OUT, 3), (ALONG, 3, 2), (FROM_X, 4, 0), (ALONG, 4, 2), (FROM_Y, 4, 1), (NORM_1,), (FROM_X, 3, 1),
-    (COTANGENT_IN,), (GROW, 0), (TURN_X,), (FROM_Y, 3, 2), (FROM_Y, 4, 0), (GROW, 1), (GROW, 2), (FROM_X, 3, 2),
-    (FROM_X, 3, 0), (GROW, 3), (FROM_X, 4, 1), (GROW, 4), (FROM_Y, 4, 2), (FROM_X, 4, 2), (GROW, 5), (GROW, 6),
-    (GROW, 7), (TURN_H,), (SHRINK, 0), (SHRINK, 1), (SHRINK, 2), (SHRINK, 3), (NORM_2,), (LAST,),
+    (OWN, 0), (OWN, 1), (ALONG, 0, 0), (ALONG, 0, 1), (ALONG, 1, 0), (ALONG, 1, 1), (ALONG, 0, 2), (TOKENS_IN,),
+    (FROM_Y, 0, 0), (FROM_X, 0, 0), (FROM_X, 1, 0), (FROM_X, 0, 1), (FROM_Y, 1, 0), (ALONG, 1, 2), (OWN, 2),
+    (FROM_Y, 1, 1), (FROM_X, 1, 1), (FROM_Y, 1, 2), (FROM_X, 0, 2), (FROM_Y, 0, 2), (FROM_X, 1, 2), (FROM_Y, 0, 1),
+    (TO_CORE,), (ALONG, 2, 0), (ALONG, 2, 1), (OWN, 3), (PROJECT, 0), (PROJECT, 1), (PROJECT, 2), (PROJECT, 3),
+    (PROJECT, 4), (PROJECT, 5), (FROM_Y, 2, 0), (ATTEND, 0, 0), (FROM_X, 2, 0), (ALONG, 2, 2), (ATTEND, 0, 1),
+    (OWN, 4), (ATTEND, 0, 2), (ATTEND, 0, 3), (ATTEND, 1, 0), (FROM_X, 2, 1), (ALONG, 3, 0), (ATTEND, 1, 1),
+    (ALONG, 3, 1), (ATTEND, 1, 2), (ATTEND, 1, 3), (ATTEND, 2, 0), (ATTEND, 2, 1), (ATTEND, 2, 2), (ALONG, 4, 0),
+    (ALONG, 4, 1), (ATTEND, 2, 3), (ATTEND, 3, 0), (ATTEND, 3, 1), (ATTEND, 3, 2), (FROM_Y, 2, 2), (ATTEND, 3, 3),
+    (ATTN_OUT, 0), (ATTN_OUT, 1), (ATTN_OUT, 2), (ATTN_OUT, 3), (ALONG, 3, 2), (FROM_X, 2, 2), (FROM_Y, 2, 1),
+    (TURN_X,), (FROM_Y, 4, 0), (FROM_X, 3, 1), (ALONG, 4, 2), (NORM_1,), (COTANGENT_IN,), (FROM_X, 4, 1),
+    (FROM_Y, 3, 0), (FROM_X, 3, 0), (FROM_Y, 4, 1), (FROM_Y, 3, 1), (FROM_Y, 3, 2), (FROM_X, 4, 0), (FROM_X, 3, 2),
+    (GROW, 0), (GROW, 1), (GROW, 2), (GROW, 3), (GROW, 4), (GROW, 5), (GROW, 6), (FROM_X, 4, 2), (GROW, 7),
+    (FROM_Y, 4, 2), (SHRINK, 0), (SHRINK, 1), (SHRINK, 2), (SHRINK, 3), (TURN_H,), (NORM_2,), (LAST,),
 )
 BACKWARD_ORDER = (
-    (PLACE_OUT,), (OUTER_W, 0), (OUTER_W, 1), (OUTER_W, 2), (OUTER_W, 3), (SEND, 3, 1), (INNER, 0), (INNER, 1),
-    (SEND, 3, 0), (INNER, 2), (INNER, 3), (INNER, 4), (SEND, 3, 2), (SEND, 3, 3), (INNER, 5), (INNER, 6), (INNER, 7),
-    (INNER_W, 0), (HIDDEN, 0), (INNER_W, 1), (SEND, 4, 1), (LINE_STEP, 0, 0), (SEND, 4, 0), (HIDDEN, 1), (INNER_W, 2),
-    (HIDDEN, 2), (HIDDEN, 3), (SEND, 4, 2), (ADD_B, 3, 3), (ADD_A, 3, 1), (ADD_B, 4, 1), (LINE_STEP, 0, 1),
-    (INNER_W, 3), (ADD_B, 3, 0), (NORM_BACK,), (LINE_STEP, 0, 2), (ADD_A, 4, 1), (SEND, 4, 3), (MIXED, 0),
-    (ATTN_W, 0), (ADD_B, 4, 0), (ADD_A, 3, 0), (ADD_A, 3, 2), (MIXED, 1), (SEND, 6, 0), (ATTEND, 0, 0),
-    (ATTEND, 0, 1), (ATTEND, 0, 2), (LINE_STEP, 1, 0), (ATTEND, 0, 3), (ATTEND, 0, 4), (ATTN_W, 1), (ATTEND, 1, 0),
-    (ADD_A, 4, 0), (ATTEND, 1, 1), (ATTEND, 1, 2), (ATTEND, 1, 3), (ATTEND, 1, 4), (ATTEND, 2, 0), (ADD_A, 4, 2),
-    (LINE_STEP, 1, 1), (ATTN_W, 2), (ATTEND, 2, 1), (ATTEND, 2, 2), (SEND, 6, 2), (LINE_STEP, 1, 2), (SEND, 6, 1),
-    (ATTEND, 2, 3), (ADD_A, 3, 3), (ADD_B, 4, 3), (ATTEND, 2, 4), (ATTEND, 3, 0), (ATTEND, 3, 1), (ATTEND, 3, 2),
-    (ATTEND, 3, 3), (ATTEND, 3, 4), (ADD_B, 3, 1), (QKV_W, 0), (SEND, 5, 0), (LINE_STEP, 0, 3), (ATTN_W, 3),
-    (ADD_B, 4, 2), (SUM_UP, 3, 0), (INPUT, 0), (ADD_B, 6, 0), (ADD_A, 6, 2), (INPUT, 1), (ADD_A, 4, 3),
-    (LINE_STEP, 2, 0), (QKV_W, 1), (LINE_STEP, 1, 3), (ADD_B, 6, 1), (INPUT, 2), (SEND, 6, 3), (SUM_UP, 4, 0),
-    (SEND, 0, 3), (ADD_A, 6, 1), (SUM_UP, 3, 1), (INPUT, 3), (SEND, 5, 1), (ADD_A, 5, 0), (QKV_W, 2), (SEND, 5, 2),
-    (ADD_B, 6, 3), (LINE_STEP, 2, 1), (ADD_B, 5, 0), (LINE_STEP, 2, 2), (SEND, 1, 3), (QKV_W, 3), (SEND, 5, 3),
-    (ADD_B, 3, 2), (SUM_UP, 4, 1), (LINE_STEP, 2, 3), (SEND, 2, 3), (SUM_UP, 4, 2), (ADD_B, 1, 3), (ADD_A, 6, 0),
-    (SUMS,), (ADD_A, 5, 3), (SUMS_X,), (ADD_A, 5, 1), (ADD_B, 5, 3), (ADD_B, 5, 1), (ADD_A, 0, 3), (ADD_B, 5, 2),
-    (ADD_B, 0, 3), (ADD_B, 6, 2), (ADD_A, 2, 3), (INPUT_LAST,), (ADD_A, 6, 3), (ADD_A, 5, 2), (SUM_UP, 5, 0),
-    (SUM_UP, 6, 0), (ADD_B, 2, 3), (SUMS_Y,), (SUM_UP, 4, 3), (SUM_UP, 5, 1), (SUM_UP, 3, 2), (ADD_A, 1, 3),
-    (SUM_UP, 6, 1), (SUM_UP, 5, 2), (SUM_UP, 3, 3), (SUM_UP, 2, 3), (SUM_UP, 6, 2), (SUM_UP, 0, 3), (PLACE_INPUT,),
-    (SUM_UP, 1, 3), (SUM_UP, 5, 3), (BACK_Y, 0), (SUM_UP, 6, 3), (BACK_Y, 2), (BACK_X, 4), (SUMS_LINE,), (BACK_Y, 4),
-    (BACK_X, 3), (BACK_X, 2), (BACK_Y, 6), (BACK_X, 5), (BACK_X, 0), (BACK_X, 1), (BACK_Y, 3), (BACK_X, 6),
-    (BACK_Y, 1), (BACK_Y, 5),
+    (PLACE_OUT,), (OUTER_W, 0), (OUTER_W, 1), (OUTER_W, 2), (OUTER_W, 3), (SEND, 3, 2), (INNER, 0), (INNER, 1),
+    (SEND, 3, 1), (SEND, 3, 3), (SEND, 3, 0), (INNER, 2), (INNER, 3), (INNER, 4), (INNER, 5), (INNER, 6), (INNER, 7),
+    (INNER_W, 0), (SEND, 4, 0), (LINE_STEP, 0, 0), (INNER_W, 1), (SEND, 4, 1), (HIDDEN, 0), (HIDDEN, 1),
+    (ADD_B, 4, 0), (HIDDEN, 2), (HIDDEN, 3), (ADD_A, 3, 1), (ADD_A, 3, 2), (ADD_A, 3, 0), (LINE_STEP, 0, 1),
+    (INNER_W, 2), (SEND, 4, 2), (ADD_A, 3, 3), (ADD_B, 3, 3), (NORM_BACK,), (LINE_STEP, 1, 0), (INNER_W, 3),
+    (LINE_STEP, 0, 2), (ADD_A, 4, 1), (MIXED, 0), (SEND, 4, 3), (ATTN_W, 0), (MIXED, 1), (ATTEND, 0, 0),
+    (ADD_B, 4, 2), (ADD_B, 4, 1), (ATTEND, 0, 1), (ATTEND, 0, 2), (ATTN_W, 1), (ATTEND, 0, 3), (ATTEND, 0, 4),
+    (ADD_A, 4, 2), (ATTEND, 1, 0), (ATTEND, 1, 1), (ATTEND, 1, 2), (LINE_STEP, 1, 1), (ADD_A, 4, 0), (ATTN_W, 2),
+    (ATTEND, 1, 3), (ATTN_W, 3), (LINE_STEP, 1, 2), (SEND, 6, 2), (ADD_B, 3, 1), (ADD_A, 4, 3), (ATTEND, 1, 4),
+    (ADD_B, 4, 3), (SEND, 6, 0), (ATTEND, 2, 0), (ATTEND, 2, 1), (SEND, 6, 1), (SEND, 6, 3), (ATTEND, 2, 2),
+    (ATTEND, 2, 3), (ATTEND, 2, 4), (ADD_B, 3, 0), (LINE_STEP, 0, 3), (ATTEND, 3, 0), (ATTEND, 3, 1), (SEND, 0, 3),
+    (LINE_STEP, 2, 0), (ATTEND, 3, 2), (ATTEND, 3, 3), (ATTEND, 3, 4), (QKV_W, 0), (SEND, 5, 0), (QKV_W, 1),
+    (SUM_UP, 4, 0), (QKV_W, 2), (ADD_B, 0, 3), (ADD_A, 0, 3), (ADD_A, 6, 0), (SEND, 5, 1), (LINE_STEP, 2, 1),
+    (ADD_B, 6, 1), (ADD_B, 6, 3), (SUMS,), (SEND, 5, 2), (LINE_STEP, 2, 2), (INPUT, 0), (SUM_UP, 0, 3), (ADD_A, 6, 2),
+    (INPUT, 1), (LINE_STEP, 1, 3), (SUMS_X,), (ADD_B, 5, 1), (SEND, 1, 3), (ADD_A, 6, 1), (ADD_B, 6, 0), (QKV_W, 3),
+    (SUM_UP, 3, 0), (ADD_A, 6, 3), (ADD_B, 6, 2), (ADD_A, 5, 0), (SUM_UP, 4, 1), (SUM_UP, 4, 2), (ADD_B, 5, 0),
+    (SEND, 5, 3), (ADD_A, 1, 3), (INPUT, 2), (ADD_B, 3, 2), (ADD_B, 1, 3), (BACK_X, 0), (LINE_STEP, 2, 3),
+    (ADD_A, 5, 1), (SUM_UP, 6, 0), (SEND, 2, 3), (ADD_A, 5, 2), (ADD_B, 5, 2), (BACK_Y, 0), (INPUT, 3),
+    (SUM_UP, 5, 0), (SUMS_Y,), (SUM_UP, 6, 1), (ADD_A, 2, 3), (SUM_UP, 4, 3), (SUM_UP, 3, 1), (ADD_A, 5, 3),
+    (ADD_B, 5, 3), (SUM_UP, 5, 1), (SUM_UP, 3, 2), (SUM_UP, 5, 2), (ADD_B, 2, 3), (INPUT_LAST,), (SUM_UP, 6, 2),
+    (PLACE_INPUT,), (SUM_UP, 1, 3), (SUM_UP, 3, 3), (SUM_UP, 2, 3), (SUM_UP, 5, 3), (BACK_Y, 3), (SUMS_LINE,),
+    (SUM_UP, 6, 3), (BACK_X, 4), (BACK_Y, 2), (BACK_X, 3), (BACK_X, 1), (BACK_Y, 5), (BACK_X, 2), (BACK_Y, 1),
+    (BACK_Y, 4), (BACK_X, 5), (BACK_Y, 6), (BACK_X, 6),
 )
 
 

time: 247 us -> 243 us (0.984)
  Pallas kernels: 246 us -> 242 us
    pallas_call x1, Pallas kernels: 134 us -> 130 us  [backward(): pl.pallas_call(backward_kernel, name='backward', out_shape=[jax.ShapeDtyp...]
where the time goes in v5:
time: 243 us
  Pallas kernels  242 us (100%)
    pallas_call x1, Pallas kernels, backward(): pl.pallas_call(backward_kernel, name='backward', out_shape=[jax.ShapeDtyp...  130 us
    pallas_call x1, Pallas kernels, forward(): pl.pallas_call(forward_kernel, name='forward', out_shape=[jax.ShapeDtypeS...  108 us
    pallas_call x1, Pallas kernels, finish(): pl.pallas_call(finish_kernel, name='finish', grid=(steps,), out_shape=[ja...  4.94 us

profile of v5, /device:TPU:0, one launch (start us, length us, event | category | flops | bytes accessed | tf_op | source)
XLA Modules:
  0.0 243.0 jit_solution(3552975015220375123)
XLA Ops:
  0.7 107.7 %forward.1 = (bf16[4,256,1536]{2,1,0:T(8,128)(2,1)}, bf16[4,512,256]{2,1,0:T(8,128)(2,1)}, bf16[4,256,2048]{2,1,0:T(8,128)(2,1)}, bf16[4,2048,256]{2,1,0:T(8,128...) custom-call(bf16[1024,256]{1,0:T(8,128)(2,1)} %refs_0_.1, ...), custom_call_target="tpu_custom_call" | custom-call | tf_op jit(solution)/shard_map/forward/pallas_call | solution.py:1296
  108.4 129.5 %backward.1 = (bf16[2048,256]{1,0:T(8,128)(2,1)}, bf16[256,2048]{1,0:T(8,128)(2,1)}, bf16[512,256]{1,0:T(8,128)(2,1)}, bf16[256,1536]{1,0:T(8,128)(2,1)}, bf16[1...) custom-call(bf16[4,256,1536]{2,1,0:T(8,128)(2,1)} %get-tuple-element.60.refs_0_, ...), custom_call_target="tpu_custom_call" | custom-call | tf_op jit(solution)/shard_map/backward/pallas_call | solution.py:1722
  237.9 4.9 %finish.1 = (f32[256,512]{1,0:T(8,128)}, f32[256,512]{1,0:T(8,128)}, f32[256,512]{1,0:T(8,128)}, f32[512,256]{1,0:T(8,128)}, f32[256,2048]{1,0:T(8,128)}, /*inde...) custom-call(bf16[256,1536]{1,0:T(8,128)(2,1)} %get-tuple-element.78., ...), custom_call_target="tpu_custom_call" | custom-call | tf_op jit(solution)/shard_map/finish/pallas_call | solution.py:1768
